TPU v7x, 32 devices: a whole 2x2x4 slice. The times are simulated.
32 devices in a mesh: dp: 8 (over y, x, core), tensor: 4 (over z).
Axes of the slice: x: 2, y: 2, z: 4, core: 2. Of those that a mesh axis runs over, the one named last changes fastest.
Arguments:
- tokens: bfloat16 [16384, 2048], P(('dp', 'tensor')), may hold values from -6 to 6
- segment_ids: int32 [8, 2048], P('dp'), may hold values from 0 to 15, never falling along the last dimension, each value on 1 to 1024 neighbouring positions
- attngain: float32 [2048], replicated, may hold values from 0.5 to 1.5
- attnshift: float32 [2048], replicated, may hold values from -1.75 to 1.75
- queryweight: bfloat16 [2048, 2048], P('dp', 'tensor'), may hold values from -0.125 to 0.125
- querybias: float32 [2048], P('tensor'), may hold values from -3 to 3
- keyvalue: bfloat16 [2048, 256], P('dp'), may hold values from -0.125 to 0.125
- valuebias: float32 [128], replicated, may hold values from -0.3125 to 0.3125
- outweight: bfloat16 [2048, 2048], P('tensor', 'dp'), may hold values from -0.75 to 0.75
- outbias: float32 [2048], replicated, may hold values from -3 to 3
- mlpgain: float32 [2048], replicated, may hold values from 0.5 to 1.5
- mlpshift: float32 [2048], replicated, may hold values from -1.75 to 1.75
- upweight: bfloat16 [2048, 8192], P('dp', 'tensor'), may hold values from -0.125 to 0.125
- upbias: float32 [8192], P('tensor'), may hold values from -3 to 3
- downweight: bfloat16 [8192, 2048], P('tensor', 'dp'), may hold values from -0.0625 to 0.0625
- downbias: float32 [2048], replicated, may hold values from -3 to 3
- cotangent: bfloat16 [16384, 2048], P(('dp', 'tensor')), may hold values from -6 to 6
Outputs:
- layer_output: bfloat16 [16384, 2048], P(('dp', 'tensor'))
- tokens_grad: bfloat16 [16384, 2048], P(('dp', 'tensor'))
- attngain_grad: float32 [2048], replicated
- attnshift_grad: float32 [2048], replicated
- queryweight_grad: float32 [2048, 2048], P('dp', 'tensor')
- querybias_grad: float32 [2048], P('tensor')
- keyvalue_grad: float32 [2048, 256], P('dp')
- valuebias_grad: float32 [128], replicated
- outweight_grad: float32 [2048, 2048], P('tensor', 'dp')
- outbias_grad: float32 [2048], replicated
- mlpgain_grad: float32 [2048], replicated
- mlpshift_grad: float32 [2048], replicated
- upweight_grad: float32 [2048, 8192], P('dp', 'tensor')
- upbias_grad: float32 [8192], P('tensor')
- downweight_grad: float32 [8192, 2048], P('tensor', 'dp')
- downbias_grad: float32 [2048], replicated
Inputs may be any that keep to these rules, and one draw needn't show every extreme that they name: `segment_ids`: along each sequence the document numbers never fall.
All inputs are finite; a program needn't handle non-finite values.
Results may differ from a plain program's by a relative error of at most 0.015.
Values may be sent and summed in bfloat16 or wider, within the bound.
No kernel may reach another device: no remote copies, remote signals or barrier semaphores. Data moves between devices by JAX's collectives and lax.ppermute only.
A program may use at most 256 MiB of HBM per device.

v0:
```python
import functools

import jax
import jax.numpy as jnp
from jax import lax
from jax.experimental import pallas as pl
from jax.experimental.pallas import tpu as pltpu
from jax.sharding import PartitionSpec as P

eps_norm = 1e-05
masked_score = -1e30
log2_e = 1.4426950408889634
bf16 = jnp.bfloat16
f32 = jnp.float32


def dot_nn(left_side, right_side):
    return jnp.dot(left_side, right_side, preferred_element_type=f32)


def dot_tn(left_side, right_side):
    return lax.dot_general(
        left_side, right_side, (((0,), (0,)), ((), ())), preferred_element_type=f32
    )


def dot_nt(left_side, right_side):
    return lax.dot_general(
        left_side, right_side, (((1,), (1,)), ((), ())), preferred_element_type=f32
    )


def norm_stats(values):
    row_mean = jnp.mean(values, axis=-1, keepdims=True)
    centered = values - row_mean
    row_var = jnp.mean(centered * centered, axis=-1, keepdims=True)
    scale = lax.rsqrt(row_var + eps_norm)
    return row_mean, scale


def norm_backward(values, row_mean, scale, gain, grad):
    xhat = (values - row_mean) * scale
    u = grad * gain
    u_mean = jnp.mean(u, axis=-1, keepdims=True)
    ux_mean = jnp.mean(u * xhat, axis=-1, keepdims=True)
    grad_in = (u - u_mean - xhat * ux_mean) * scale
    return grad_in, jnp.sum(grad * xhat, axis=0), jnp.sum(grad, axis=0)


def norm_backward_kernel(
    one_ref, two_ref, three_ref, values_ref, out_ref, gain_ref, resid_ref, branch_ref, sums_ref
):
    grad = one_ref[...].astype(f32) + two_ref[...].astype(f32) + three_ref[...].astype(f32)
    values = values_ref[...]
    grad_out = out_ref[...].astype(f32)
    mean, scale = norm_stats(values)
    xhat = (values - mean) * scale
    u = grad * gain_ref[...]
    u_mean = jnp.mean(u, axis=-1, keepdims=True)
    ux_mean = jnp.mean(u * xhat, axis=-1, keepdims=True)
    resid = grad_out + (u - u_mean - xhat * ux_mean) * scale
    branch = resid.astype(bf16)
    resid_ref[...] = resid
    branch_ref[...] = branch

    @pl.when(pl.program_id(0) == 0)
    def _():
        sums_ref[...] = jnp.zeros_like(sums_ref)

    for k, rows in enumerate((grad * xhat, grad, branch.astype(f32), grad_out)):
        sums_ref[k : k + 1] += jnp.sum(rows, axis=0, keepdims=True)


def norm_backward_shares(shares, values, grad_out, gain):
    count, model = values.shape
    rows = min(128, count)
    tile = pl.BlockSpec((rows, model), lambda i: (i, 0))
    return pl.pallas_call(
        norm_backward_kernel,
        grid=(count // rows,),
        in_specs=[tile] * 5 + [pl.BlockSpec((1, model), lambda i: (0, 0))],
        out_specs=[tile, tile, pl.BlockSpec((8, model), lambda i: (0, 0))],
        out_shape=[
            jax.ShapeDtypeStruct((count, model), f32),
            jax.ShapeDtypeStruct((count, model), bf16),
            jax.ShapeDtypeStruct((8, model), f32),
        ],
        name="norm_backward",
    )(*shares, values, grad_out, gain.reshape(1, model))


gelu_c = 0.7978845608028654


def gelu_both(v):
    square = v * v
    inner = gelu_c * v * (1.0 + 0.044715 * square)
    t = jnp.tanh(inner)
    half = 0.5 * (1.0 + t)
    value = v * half
    slope = half + 0.5 * v * (1.0 - t * t) * (gelu_c * (1.0 + 3.0 * 0.044715 * square))
    return value, slope


def stack_heads(block, heads, width):
    return jnp.concatenate(
        [block[:, h * width : (h + 1) * width] for h in range(heads)], axis=0
    )


def block_bias(first_key, keys, start_row, query_row):
    key_at = first_key + lax.broadcasted_iota(jnp.int32, (keys, start_row.shape[1]), 0)
    allowed = (key_at >= start_row) & (key_at <= query_row)
    return jnp.where(allowed, 0.0, masked_score)


def attend_forward_kernel(
    heads, width, keys, info_ref, q_ref, kv_ref, start_ref, o_ref, total_ref
):
    at = pl.program_id(1)
    rows = q_ref.shape[0]
    q = stack_heads(q_ref[...], heads, width)
    start_row = start_ref[...]
    query_row = info_ref[2, at] + lax.broadcasted_iota(jnp.int32, (1, rows), 1)
    scale = width**-0.5 * log2_e

    def step(block, carried):
        top, total, mixed = carried
        first_key = pl.multiple_of(block * keys, keys)
        k = kv_ref[pl.ds(first_key, keys), :width]
        v = kv_ref[pl.ds(first_key, keys), width:]
        bias = block_bias(first_key, keys, start_row, query_row)
        scores = dot_nt(k, q) * scale + jnp.concatenate([bias] * heads, axis=1)
        new_top = jnp.maximum(top, jnp.max(scores, axis=0, keepdims=True))
        shrink = jnp.exp2(top - new_top)
        part = jnp.exp2(scores - new_top)
        total = total * shrink + jnp.sum(part, axis=0, keepdims=True)
        mixed = mixed * shrink + dot_tn(v, part.astype(bf16))
        return new_top, total, mixed

    count = heads * rows
    top, total, mixed = lax.fori_loop(
        info_ref[0, at],
        info_ref[1, at],
        step,
        (
            jnp.full((1, count), masked_score, f32),
            jnp.zeros((1, count), f32),
            jnp.zeros((width, count), f32),
        ),
    )
    out = (mixed / total).T.astype(bf16)
    for h in range(heads):
        o_ref[:, h * width : (h + 1) * width] = out[h * rows : (h + 1) * rows]
    total_ref[...] = (top + jnp.log2(total)).reshape(total_ref.shape)


def attend_backward_kernel(
    heads,
    width,
    keys,
    info_ref,
    q_ref,
    grad_ref,
    o_ref,
    kv_ref,
    start_ref,
    total_ref,
    dq_ref,
    dkv_ref,
):
    at = pl.program_id(1)
    rows = q_ref.shape[0]

    @pl.when((pl.program_id(0) == 0) & (at == 0))
    def _():
        dkv_ref[...] = jnp.zeros_like(dkv_ref)

    q = stack_heads(q_ref[...], heads, width)
    grad = stack_heads(grad_ref[...], heads, width)
    out = stack_heads(o_ref[...], heads, width)
    delta = jnp.sum((grad.astype(f32) * out.astype(f32)).T, axis=0, keepdims=True)
    count = heads * rows
    total = total_ref[...].reshape(1, count)
    start_row = start_ref[...]
    query_row = info_ref[2, at] + lax.broadcasted_iota(jnp.int32, (1, rows), 1)
    scale = width**-0.5

    def step(block, dq):
        first_key = pl.multiple_of(block * keys, keys)
        k = kv_ref[pl.ds(first_key, keys), :width]
        v = kv_ref[pl.ds(first_key, keys), width:]
        bias = block_bias(first_key, keys, start_row, query_row)
        scores = dot_nt(k, q) * (scale * log2_e) + jnp.concatenate([bias] * heads, axis=1)
        probs = jnp.exp2(scores - total)
        dprobs = dot_nt(v, grad)
        dscores = (probs * (dprobs - delta)).astype(bf16)
        dkv_ref[pl.ds(first_key, keys), :width] += dot_nn(dscores, q) * scale
        dkv_ref[pl.ds(first_key, keys), width:] += dot_nn(probs.astype(bf16), grad)
        return dq + dot_tn(k, dscores)

    dq = lax.fori_loop(
        info_ref[0, at], info_ref[1, at], step, jnp.zeros((width, count), f32)
    )
    dq = (dq * scale).T.astype(bf16)
    for h in range(heads):
        dq_ref[:, h * width : (h + 1) * width] = dq[h * rows : (h + 1) * rows]


def attend_shapes(queries, width):
    tokens = queries.shape[0]
    heads_all = queries.shape[1] // width
    heads = 16 if heads_all % 16 == 0 else heads_all
    rows = min(128, tokens)
    return tokens, heads_all, heads, heads_all // heads, rows, tokens // rows


def attend_forward(queries, kv_all, info, starts, width, keys):
    tokens, heads_all, heads, groups, rows, blocks = attend_shapes(queries, width)
    return pl.pallas_call(
        functools.partial(attend_forward_kernel, heads, width, keys),
        grid_spec=pltpu.PrefetchScalarGridSpec(
            num_scalar_prefetch=1,
            grid=(groups, blocks),
            in_specs=[
                pl.BlockSpec((rows, heads * width), lambda g, i, info: (i, g)),
                pl.BlockSpec(kv_all.shape, lambda g, i, info: (0, 0)),
                pl.BlockSpec((1, rows), lambda g, i, info: (0, i)),
            ],
            out_specs=[
                pl.BlockSpec((rows, heads * width), lambda g, i, info: (i, g)),
                pl.BlockSpec((1, 1, 1, heads * rows), lambda g, i, info: (g, i, 0, 0)),
            ],
        ),
        out_shape=[
            jax.ShapeDtypeStruct((tokens, heads_all * width), bf16),
            jax.ShapeDtypeStruct((groups, blocks, 1, heads * rows), f32),
        ],
        name="attend_forward",
    )(info, queries, kv_all, starts)


def attend_backward(queries, grad, mixed, kv_all, info, starts, totals, width, keys):
    tokens, heads_all, heads, groups, rows, blocks = attend_shapes(queries, width)
    tile = pl.BlockSpec((rows, heads * width), lambda g, i, info: (i, g))
    return pl.pallas_call(
        functools.partial(attend_backward_kernel, heads, width, keys),
        grid_spec=pltpu.PrefetchScalarGridSpec(
            num_scalar_prefetch=1,
            grid=(groups, blocks),
            in_specs=[
                tile,
                tile,
                tile,
                pl.BlockSpec(kv_all.shape, lambda g, i, info: (0, 0)),
                pl.BlockSpec((1, rows), lambda g, i, info: (0, i)),
                pl.BlockSpec((1, 1, 1, heads * rows), lambda g, i, info: (g, i, 0, 0)),
            ],
            out_specs=[
                tile,
                pl.BlockSpec(kv_all.shape, lambda g, i, info: (0, 0)),
            ],
        ),
        out_shape=[
            jax.ShapeDtypeStruct((tokens, heads_all * width), bf16),
            jax.ShapeDtypeStruct(kv_all.shape, f32),
        ],
        name="attend_backward",
    )(info, queries, grad, mixed, kv_all, starts, totals)


def after(value, *earlier):
    return lax.optimization_barrier((value, earlier))[0]


def axis_gather(block, axis):
    copies = jnp.broadcast_to(block[None], (lax.axis_size(axis),) + block.shape)
    return lax.all_to_all(copies, axis, 0, 0)


def tensor_exchange(parts, rows):
    parts = parts.reshape(lax.axis_size("tensor"), rows, parts.shape[1])
    return lax.all_to_all(parts, "tensor", 0, 0)


def tensor_swaps(parts):
    size = lax.axis_size("tensor")
    index = lax.axis_index("tensor")
    found = jnp.zeros(parts.shape, parts.dtype)
    zeros = (0,) * (parts.ndim - 1)
    for s in range(size):
        part = lax.dynamic_index_in_dim(parts, (index + s) % size, 0)
        if s:
            part = lax.ppermute(part, "tensor", [(i, (i + s) % size) for i in range(size)])
        found = lax.dynamic_update_slice(found, part, ((index - s) % size,) + zeros)
    return found


class Ring:
    def __init__(self, size):
        self.size = size
        self.chips = size // 2
        half = self.chips // 2
        if half:
            self.order = list(range(half)) + list(range(self.chips - 1, half - 1, -1))
        else:
            self.order = [0]
        n = self.chips
        self.pairs = []
        for i in range(n):
            here, there = self.order[i], self.order[(i + 1) % n]
            self.pairs += [(2 * here, 2 * there), (2 * there + 1, 2 * here + 1)]
        self.swap_pairs = [(i, i ^ 1) for i in range(size)]
        self.keys = [(s, c) for s in range(n) for c in (0, 1)]

    def owner(self, index, s, c):
        place = [0] * self.chips
        for i, chip in enumerate(self.order):
            place[chip] = i
        at = jnp.array(place, jnp.int32)[index // 2]
        core = index % 2 if c == 0 else 1 - index % 2
        at = (at + jnp.where(core == 0, -s, s)) % self.chips
        return 2 * jnp.array(self.order, jnp.int32)[at] + core

    def step(self, value):
        return lax.ppermute(value, "dp", self.pairs)

    def swap(self, value):
        return lax.ppermute(value, "dp", self.swap_pairs)

    def gather(self, own, gates=()):
        blocks = {(0, 0): own, (0, 1): self.swap(own)}
        for s in range(1, self.chips):
            if s < len(gates) and gates[s] is not None:
                own = after(own, gates[s])
            own = self.step(own)
            blocks[(s, 0)] = own
            blocks[(s, 1)] = self.swap(own)
        return blocks

    def sums(self, parts):
        held = None
        gate = yield
        for s in list(range(1, self.chips)) + [0]:
            there = self.swap(parts[(s, 1)].astype(bf16))
            if gate is not None:
                there = after(there, gate)
            shares = [parts[(s, 0)], there] + ([] if held is None else [held])
            if s:
                value = total(shares).astype(bf16)
                held = self.step(value)
                gate = yield value
            else:
                gate = yield shares


def total(shares):
    return sum(share.astype(f32) for share in shares)


def started(sums):
    next(sums)
    return sums


def units_kernel(count, piece, tiles, *refs):
    seconds, grads = refs[:count], refs[count : 2 * count]
    rows_ref, cols_ref, shift_ref = refs[2 * count : 2 * count + 3]
    outs = refs[2 * count + 3 :]
    actives, pres, shares, lasts = (outs[k * count : (k + 1) * count] for k in range(4))
    active_kept, pre_kept = (outs[k * count : (k + 1) * count] for k in (4, 5))
    at = pl.program_id(0)

    def pieces(block, first):
        width = block.shape[1]
        return jnp.concatenate(
            [block[:, k : k + piece] for k in range(first * piece, width, 2 * piece)], axis=1
        )

    @pl.when(at < tiles)
    def _():
        up, down = pieces(rows_ref, 0), pieces(rows_ref, 1)
        for k in range(count):
            preact = dot_nt(seconds[k][...], up) + shift_ref[...]
            grad_active = dot_nt(grads[k][...], down)
            value, slope = gelu_both(preact)
            value = value.astype(bf16)
            pre = (grad_active * slope).astype(bf16)
            actives[k][...] = value
            pres[k][...] = pre
            active_kept[k][at] = value
            pre_kept[k][at] = pre

    @pl.when(at >= tiles)
    def _():
        up, down = pieces(cols_ref, 0), pieces(cols_ref, 1)
        for k in range(count):
            pre = jnp.concatenate([pre_kept[k][j] for j in range(tiles)], axis=1)
            shares[k][...] = dot_nn(pre, up).astype(bf16)
            value = jnp.concatenate([active_kept[k][j] for j in range(tiles)], axis=1)
            lasts[k][...] = dot_nn(value, down).astype(bf16)


def units(seconds, grads, weights, piece, shift):
    count = len(seconds)
    rows, model = seconds[0].shape
    hidden = weights.shape[0]
    width = min(256, hidden)
    tiles = hidden // width
    turns = model // (2 * piece)
    tile = pl.BlockSpec((rows, width), lambda j: (0, jnp.minimum(j, tiles - 1)))
    whole = pl.BlockSpec((rows, model), lambda j: (0, 0))
    part = pl.BlockSpec((rows, 2 * piece), lambda j: (0, jnp.maximum(j - tiles, 0)))
    out = pl.pallas_call(
        functools.partial(units_kernel, count, piece, tiles),
        grid=(tiles + turns,),
        in_specs=[whole] * (2 * count)
        + [
            pl.BlockSpec((width, 2 * model), lambda j: (jnp.minimum(j, tiles - 1), 0)),
            pl.BlockSpec((hidden, 4 * piece), lambda j: (0, jnp.maximum(j - tiles, 0))),
            pl.BlockSpec((1, width), lambda j: (0, jnp.minimum(j, tiles - 1))),
        ],
        out_specs=[tile] * (2 * count) + [part] * (2 * count),
        out_shape=[jax.ShapeDtypeStruct((rows, hidden), bf16)] * (2 * count)
        + [jax.ShapeDtypeStruct((rows, model), bf16)] * (2 * count),
        scratch_shapes=[pltpu.VMEM((tiles, rows, width), bf16)] * (2 * count),
        cost_estimate=pl.CostEstimate(
            flops=8 * count * rows * model * hidden,
            transcendentals=count * rows * hidden,
            bytes_accessed=8 * hidden * model + 4 * count * rows * (2 * model + hidden),
        ),
        name="units",
    )(*seconds, *grads, weights, weights, shift.reshape(1, hidden))
    return [out[k * count : (k + 1) * count] for k in range(4)]


def rows_product_kernel(depth, owner_ref, left_ref, shift_ref, *refs):
    blocks, out_ref = refs[:-1], refs[-1]
    total = jnp.broadcast_to(shift_ref[...], out_ref.shape)
    for k, block in enumerate(blocks):
        at = pl.multiple_of(owner_ref[k] * depth, depth)
        total = total + dot_nn(left_ref[:, pl.ds(at, depth)], block[...])
    out_ref[...] = total.astype(out_ref.dtype)


def rows_product(left, blocks, owners, shift):
    depth, width = blocks[0].shape
    tile = 128 * max(t for t in range(1, 9) if width % (128 * t) == 0)
    return pl.pallas_call(
        functools.partial(rows_product_kernel, depth),
        grid_spec=pltpu.PrefetchScalarGridSpec(
            num_scalar_prefetch=1,
            grid=(width // tile,),
            in_specs=[
                pl.BlockSpec(left.shape, lambda j, owner: (0, 0)),
                pl.BlockSpec((1, tile), lambda j, owner: (0, j)),
            ]
            + [pl.BlockSpec((depth, tile), lambda j, owner: (0, j)) for _ in blocks],
            out_specs=pl.BlockSpec((left.shape[0], tile), lambda j, owner: (0, j)),
        ),
        out_shape=jax.ShapeDtypeStruct((left.shape[0], width), bf16),
        cost_estimate=pl.CostEstimate(
            flops=2 * left.shape[0] * left.shape[1] * width,
            transcendentals=0,
            bytes_accessed=2 * left.shape[1] * width,
        ),
        name="rows_product",
    )(owners, left, shift.reshape(1, width), *blocks)


def grads_product_kernel(count, *refs):
    out_ref, sum_ref = refs[2 * count :]
    total = dot_tn(refs[0][...], refs[count][...])
    for k in range(1, count):
        total = total + dot_tn(refs[k][...], refs[count + k][...])
    out_ref[...] = total.astype(out_ref.dtype)

    @pl.when(pl.program_id(0) == 0)
    def _():
        sums = jnp.zeros(sum_ref.shape, f32)
        for k in range(count):
            sums = sums + jnp.sum(refs[k][...].astype(f32), axis=0, keepdims=True)
        sum_ref[...] = sums


def grads_product(lefts, rights):
    rows, units = lefts[0].shape
    width = rights[0].shape[1]
    tile = min(512, width)
    count = len(lefts)
    return pl.pallas_call(
        functools.partial(grads_product_kernel, count),
        grid=(width // tile,),
        in_specs=[pl.BlockSpec((rows, units), lambda j: (0, 0)) for _ in lefts]
        + [pl.BlockSpec((rows, tile), lambda j: (0, j)) for _ in rights],
        out_specs=[
            pl.BlockSpec((units, tile), lambda j: (0, j)),
            pl.BlockSpec((1, units), lambda j: (0, 0)),
        ],
        out_shape=[
            jax.ShapeDtypeStruct((units, width), bf16),
            jax.ShapeDtypeStruct((1, units), f32),
        ],
        cost_estimate=pl.CostEstimate(
            flops=2 * count * rows * units * width,
            transcendentals=0,
            bytes_accessed=2 * count * rows * (units + width) + 2 * units * width,
        ),
        name="grads_product",
    )(*lefts, *rights)


def cols_product_kernel(depth, owner_ref, left_ref, *refs):
    blocks, out_ref = refs[:-1], refs[-1]
    left = left_ref[...]
    for k, block in enumerate(blocks):
        at = pl.multiple_of(owner_ref[k] * depth, depth)
        out_ref[:, pl.ds(at, depth)] = dot_nt(left, block[...])


def cols_product(left, blocks, owners):
    depth, width = blocks[0].shape
    rows = left.shape[0]
    out_width = depth * len(blocks)
    return pl.pallas_call(
        functools.partial(cols_product_kernel, depth),
        grid_spec=pltpu.PrefetchScalarGridSpec(
            num_scalar_prefetch=1,
            grid=(left.shape[0] // rows,),
            in_specs=[pl.BlockSpec((rows, width), lambda i, owner: (i, 0))]
            + [pl.BlockSpec((depth, width), lambda i, owner: (0, 0)) for _ in blocks],
            out_specs=pl.BlockSpec((rows, out_width), lambda i, owner: (i, 0)),
        ),
        out_shape=jax.ShapeDtypeStruct((left.shape[0], out_width), f32),
        cost_estimate=pl.CostEstimate(
            flops=2 * left.shape[0] * out_width * width,
            transcendentals=0,
            bytes_accessed=2 * out_width * width,
        ),
        name="cols_product",
    )(owners, left, *blocks)


def on_device(
    tokens,
    segment_ids,
    attngain,
    attnshift,
    queryweight,
    querybias,
    keyvalue,
    valuebias,
    outweight,
    outbias,
    mlpgain,
    mlpshift,
    upweight,
    upbias,
    downweight,
    downbias,
    cotangent,
):
    head_dim = valuebias.shape[0]
    count, model = tokens.shape
    n_dp = lax.axis_size("dp")
    n_tensor = lax.axis_size("tensor")
    dp_index = lax.axis_index("dp")
    tensor_index = lax.axis_index("tensor")
    ring = Ring(n_dp)
    order = ring.keys
    owners = jnp.stack([ring.owner(dp_index, *key) for key in order]).astype(jnp.int32)
    segment = segment_ids[0]
    length = segment.shape[0]
    rows = tokens.astype(f32)
    depth = queryweight.shape[0]
    width = queryweight.shape[1]

    both = lax.all_gather(jnp.stack([queryweight, outweight.T]), "tensor", axis=0)
    both = both.transpose(1, 2, 0, 3).reshape(2, depth, n_tensor * width)

    hidden_own = upweight.shape[1] // n_dp
    bias_part = lax.dynamic_slice_in_dim(upbias, dp_index * hidden_own, hidden_own)
    biases = axis_gather(jnp.concatenate([querybias, bias_part]), "tensor")
    query_shift = biases[:, :width].reshape(-1)
    up_shift = biases[:, width:].reshape(-1)
    pair_full = axis_gather(after(keyvalue, biases), "dp").reshape(model, 2 * head_dim)

    first_mean, first_scale = norm_stats(rows)
    normed_first = ((rows - first_mean) * first_scale * attngain + attnshift).astype(bf16)
    pair_shift = jnp.concatenate([jnp.zeros((head_dim,), f32), valuebias])
    pairs = (dot_nn(normed_first, pair_full) + pair_shift).astype(bf16)

    weights = after(jnp.concatenate([upweight.T, downweight], axis=1), pair_full)
    weights = lax.all_to_all(weights, "dp", 0, 1, tiled=True)
    kv_all = axis_gather(after(pairs, weights), "tensor").reshape(length, 2 * head_dim)

    first_blocks = ring.gather(both[0], (None, None, weights, kv_all))
    first_list = [first_blocks[key] for key in order]
    weights = lax.all_gather(after(weights, kv_all), "tensor", axis=0, tiled=True)

    grads = {(0, 0): cotangent, (1, 0): ring.step(cotangent)}
    normed_late = after(normed_first, grads[(1, 0)])
    queries = rows_product(normed_late, first_list, owners, query_shift)
    if ring.chips > 2:
        grads[(2, 0)] = ring.step(after(grads[(1, 0)], queries))
    keys = 256 if length % 256 == 0 else 128
    query_block = min(128, count)
    first_row = tensor_index * count
    own_segment = lax.dynamic_slice_in_dim(segment, first_row, count)
    starts = jnp.sum(
        (segment[None, :] < own_segment[:, None]).astype(jnp.int32), axis=1
    )
    block_first = first_row + jnp.arange(count // query_block, dtype=jnp.int32) * query_block
    info = jnp.stack(
        [
            starts[::query_block] // keys,
            (block_first + query_block - 1) // keys + 1,
            block_first,
        ]
    ).astype(jnp.int32)
    starts = starts.reshape(1, count)
    mixed, totals = attend_forward(queries, kv_all, info, starts, head_dim, keys)
    for at in range(3, ring.chips):
        grads[(at, 0)] = ring.step(after(grads[(at - 1, 0)], mixed))
    for at in range(ring.chips):
        grads[(at, 1)] = ring.swap(after(grads[(at, 0)], mixed))
    out_blocks = ring.gather(both[1], (None, first_list, queries, mixed))
    out_list = [out_blocks[key] for key in order]
    residual = rows + cols_product(after(mixed, grads[(min(2, ring.chips - 1), 0)]), out_list, owners) + outbias
    second_mean, second_scale = norm_stats(residual)
    normed_second = ((residual - second_mean) * second_scale * mlpgain + mlpshift).astype(bf16)

    active, grad_pre, second_parts, last_parts, seconds = {}, {}, {}, {}, {}
    done = []

    def work(s):
        keys_here = [(s, 0), (s, 1)]
        seconds[keys_here[0]] = passed[s]
        seconds[keys_here[1]] = ring.swap(after(passed[s], done))
        found = units(
            [after(seconds[key], done[-1:]) for key in keys_here],
            [grads[key] for key in keys_here],
            weights,
            depth,
            up_shift,
        )
        done.append(found[2])
        for kept, values in zip((active, grad_pre, second_parts, last_parts), found):
            kept.update(zip(keys_here, values))

    passed = [normed_second]
    for s in range(1, ring.chips):
        if s >= 3:
            work(s - 2)
        passed.append(ring.step(after(passed[-1], done)))
    for s in range(max(1, ring.chips - 2), ring.chips):
        work(s)
    work(0)
    sums = started(ring.sums(second_parts))
    for at in range(ring.chips):
        grad_second = sums.send(done[min(at + 1, len(done) - 1)])
    parts_done = done[-1]
    up_local, upbias_part = grads_product(
        [after(grad_pre[key], parts_done) for key in order], [seconds[key] for key in order]
    )
    up_part = lax.psum_scatter(up_local, "tensor", scatter_dimension=0, tiled=True)
    grad_second = [after(share, up_local) for share in grad_second]
    grad_second += [jnp.zeros_like(cotangent)] * (3 - len(grad_second))

    grad_resid, grad_branch, second_sums = norm_backward_shares(
        grad_second, residual, cotangent, mlpgain
    )
    grad_mixed = rows_product(grad_branch, out_list, owners, jnp.zeros((model,), f32))
    grad_queries, grad_kv = attend_backward(
        queries, grad_mixed, mixed, kv_all, info, starts, totals, head_dim, keys
    )

    def depth_sums(local):
        return started(
            ring.sums(
                {
                    key: lax.dynamic_slice_in_dim(local, owners[k] * depth, depth, 0)
                    for k, key in enumerate(order)
                }
            )
        )

    def width_owner(block):
        parts = block.astype(bf16).reshape(depth, n_tensor, width).transpose(1, 0, 2)
        return lax.psum_scatter(parts, "tensor", scatter_dimension=0, tiled=False).astype(f32)

    chips = ring.chips
    last_sums = started(ring.sums(last_parts))
    last_sent = [last_sums.send(gate) for gate in (grad_mixed, grad_queries)[:chips]]
    pair_raw = tensor_exchange(grad_kv.astype(bf16), count)
    down_local, _ = grads_product(
        [after(active[key], grad_queries, last_sent) for key in order],
        [grads[key] for key in order],
    )
    down_part = lax.psum_scatter(down_local, "tensor", scatter_dimension=0, tiled=True)
    out_local = dot_tn(after(grad_branch, down_local), mixed).astype(bf16)
    out_sums = depth_sums(out_local)
    out_sent = [out_sums.send(None)]
    if chips > 2:
        last_sent.append(last_sums.send(down_local))
    pair_shares = after(pair_raw, down_local)
    grad_pairs = jnp.sum(pair_shares.astype(f32), axis=0).astype(bf16)
    grad_qkv = jnp.concatenate([grad_queries, grad_pairs], axis=1)
    first_local = dot_tn(normed_first, grad_qkv).astype(bf16)
    first_sums = depth_sums(first_local)
    first_sent = [first_sums.send(None) for _ in range(chips)]
    first_part = total(first_sent[-1])
    for at in range(1, chips):
        out_sent.append(out_sums.send(first_part))
    out_part = total(out_sent[-1])
    for at in range(len(last_sent), chips):
        last_sent.append(last_sums.send(first_part))
    layer_out = residual + total(last_sent[-1]) + downbias
    up_grad = lax.all_to_all(after(up_part, first_part), "dp", 1, 0, tiled=True).astype(f32).T
    grad_first = cols_product(after(grad_queries, first_sent[min(1, chips - 1)]), first_list, owners)
    grad_first = grad_first + dot_nt(grad_pairs, pair_full)
    grad_one, attngain_part, attnshift_part = norm_backward(
        rows, first_mean, first_scale, attngain, grad_first
    )
    tokens_grad = (grad_resid + grad_one).astype(bf16)

    shift_part = jnp.sum(grad_qkv.astype(f32), axis=0)
    vectors = [
        attngain_part,
        attnshift_part,
        second_sums[0],
        second_sums[1],
        second_sums[2],
        second_sums[3],
        shift_part[:model],
        shift_part[model + head_dim :],
    ]
    sizes = [v.shape[0] for v in vectors]
    plain = sum(sizes)
    flat = jnp.concatenate(vectors + [upbias_part[0]])
    flat = axis_gather(flat, "dp")
    units_flat = flat[:, plain:].reshape(n_dp, n_tensor, hidden_own)
    units_flat = units_flat.transpose(1, 0, 2).reshape(n_tensor, n_dp * hidden_own)
    flat = jnp.broadcast_to(jnp.sum(flat[:, :plain], axis=0), (n_tensor, plain))
    flat = lax.all_to_all(jnp.concatenate([flat, units_flat], axis=1), "tensor", 0, 0, tiled=True)
    flat = jnp.sum(flat, axis=0)

    first_sent = first_part.astype(bf16)
    first_sent = jnp.concatenate(
        [
            first_sent[:, :model].reshape(depth, n_tensor, width).transpose(1, 0, 2),
            jnp.broadcast_to(first_sent[None, :, model:], (n_tensor, depth, 2 * head_dim)),
        ],
        axis=2,
    )
    first_sent = tensor_swaps(first_sent)
    down_grad = lax.all_to_all(after(down_part, up_grad), "dp", 1, 0, tiled=True).astype(f32)
    out_grad = width_owner(after(out_part, first_sent)).T
    first_grad = jnp.sum(first_sent.astype(f32), axis=0)
    query_grad = first_grad[:, :width]
    keyvalue_grad = first_grad[:, width:]

    upbias_grad = flat[plain : plain + n_dp * hidden_own]
    found = []
    at = 0
    for size in sizes:
        found.append(flat[at : at + size])
        at += size
    attngain_grad, attnshift_grad, mlpgain_grad, mlpshift_grad = found[:4]
    outbias_grad, downbias_grad, query_shift_grad, valuebias_grad = found[4:]
    querybias_grad = lax.dynamic_slice_in_dim(query_shift_grad, tensor_index * width, width)
    return (
        layer_out.astype(bf16),
        tokens_grad,
        attngain_grad,
        attnshift_grad,
        query_grad,
        querybias_grad,
        keyvalue_grad,
        valuebias_grad,
        out_grad,
        outbias_grad,
        mlpgain_grad,
        mlpshift_grad,
        up_grad,
        upbias_grad,
        down_grad,
        downbias_grad,
    )


def solution(mesh):
    return jax.shard_map(
        on_device,
        mesh=mesh,
        in_specs=(
            P(("dp", "tensor"), None),
            P("dp", None),
            P(),
            P(),
            P("dp", "tensor"),
            P("tensor"),
            P("dp", None),
            P(),
            P("tensor", "dp"),
            P(),
            P(),
            P(),
            P("dp", "tensor"),
            P("tensor"),
            P("tensor", "dp"),
            P(),
            P(("dp", "tensor"), None),
        ),
        out_specs=(
            P(("dp", "tensor"), None),
            P(("dp", "tensor"), None),
            P(),
            P(),
            P("dp", "tensor"),
            P("tensor"),
            P("dp", None),
            P(),
            P("tensor", "dp"),
            P(),
            P(),
            P(),
            P("dp", "tensor"),
            P("tensor"),
            P("tensor", "dp"),
            P(),
        ),
        check_vma=False,
    )
```

profile of v0, /device:TPU:0, one launch (start us, length us, event | category | flops | bytes accessed | tf_op | source)
XLA Modules:
  0.0 758.4 jit_solution(17818944491803588209)
XLA Ops:
  11.0 11.7 %all_to_all.87 = f32[4,1,768]{2,1,0:T(1,128)S(1)} all-to-all(f32[4,1,768]{2,1,0:T(1,128)S(1)} %broadcast_in_dim.16), channel_id=1, replica_groups=mesh['dp'=8,'tensor'=4] {'tensor'}, dimensions={0} | all-to-all | bytes 24576 | tf_op jit(solution)/shard_map/all_to_all | solution.py:278
  32.9 10.1 %all-to-all-done.1 = bf16[8,256,256]{2,1,0:T(8,128)(2,1)S(1)} async-done(((bf16[8,256,256]{2,1,0:T(8,128)(2,1)}), bf16[8,256,256]{2,1,0:T(8,128)(2,1)S(1)}, u32[]{:S(2)}, u32[]{:S(2)}) %all-to-all-start.1) | async-done | bytes 1048608 | tf_op jit(solution)/shard_map/all_to_all | solution.py:278
  48.1 10.9 %all-gather.6.cloned.1.call-done = bf16[8,256,512]{2,1,0:T(8,128)(2,1)} async-done(((bf16[2,256,512]{2,1,0:T(8,128)(2,1)}), bf16[8,256,512]{2,1,0:T(8,128)(2,1)}) %all-gather.6.cloned.1.call-update) | async-done | bytes 2097168 | tf_op jit(solution)/shard_map/all_gather | solution.py:578
  85.3 19.6 %all-to-all-done.3 = bf16[4,512,256]{2,1,0:T(8,128)(2,1)S(1)} async-done(((bf16[4,512,256]{2,1,0:T(8,128)(2,1)}), bf16[4,512,256]{2,1,0:T(8,128)(2,1)S(1)}, u32[]{:S(2)}, u32[]{:S(2)}) %all-to-all-start.3) | async-done | bytes 1048608 | tf_op jit(solution)/shard_map/all_to_all | solution.py:278
  109.6 11.7 %collective-permute-done.6.refs_6_ = bf16[256,2048]{1,0:T(8,128)(2,1)} collective-permute-done((bf16[256,2048]{1,0:T(8,128)(2,1)}, bf16[256,2048]{1,0:T(8,128)(2,1)}, u32[]{:S(2)}, u32[]{:S(2)}) %collective-permute-start.6) | collective-permute-done | bytes 1048608 | tf_op jit(solution)/shard_map/ppermute | solution.py:326
  143.7 10.1 %rows_product.2.q_ref = bf16[512,2048]{1,0:T(8,128)(2,1)} custom-call(s32[8]{0:T(128)} %stack.52.owner_ref, bf16[512,2048]{1,0:T(8,128)(2,1)} %copy-done.13, f32[1,2048]{1,0:T(1,128)} %bitcast.141, bf16[256,2048]{1,0:T(8,128)(2,1)} %bitcast.70.refs_0_, bf16[256,2048]{1,0:T(8,128)(2,1)} %copy-done.43, bf16[256,2048]{1,0:T(8,128)(2,1)} %collective-permute-done.2.refs_2_, ...), custom_call_target="tpu_custom_call" | custom-call | flops 4294967296 | bytes 8388608 | tf_op jit(solution)/shard_map/rows_product/pallas_call | solution.py:449
  159.4 12.0 %attend_forward.1 = (bf16[512,2048]{1,0:T(8,128)(2,1)}, f32[1,4,1,2048]{3,2,1,0:T(1,128)}) custom-call(s32[3,4]{1,0:T(4,128)} %pad_add_fusion.info_ref, bf16[512,2048]{1,0:T(8,128)(2,1)} %rows_product.2.q_ref, bf16[2048,256]{1,0:T(8,128)(2,1)} %bitcast.105, s32[1,512]{1,0:T(1,128)} %bitcast.138), custom_call_target="tpu_custom_call" | custom-call | tf_op jit(solution)/shard_map/attend_forward/pallas_call | solution.py:220
  173.0 30.7 %collective-permute-done.14.refs_6_ = bf16[256,2048]{1,0:T(8,128)(2,1)S(1)} collective-permute-done((bf16[256,2048]{1,0:T(8,128)(2,1)S(1)}, bf16[256,2048]{1,0:T(8,128)(2,1)S(1)}, u32[]{:S(2)}, u32[]{:S(2)}) %collective-permute-start.14) | collective-permute-done | bytes 1048608 | tf_op jit(solution)/shard_map/ppermute | solution.py:326
  206.5 11.4 %cols_product.2 = f32[512,2048]{1,0:T(8,128)} custom-call(s32[8]{0:T(128)} %stack.52.owner_ref, bf16[512,2048]{1,0:T(8,128)(2,1)} %get-tuple-element.126.left_ref.o_ref, bf16[256,2048]{1,0:T(8,128)(2,1)} %bitcast.73.refs_0_, bf16[256,2048]{1,0:T(8,128)(2,1)} %copy-done.49, bf16[256,2048]{1,0:T(8,128)(2,1)} %collective-permute-done.10.refs_2_, ...), custom_call_target="tpu_custom_call" | custom-call | flops 4294967296 | bytes 8388608 | tf_op jit(solution)/shard_map/cols_product/pallas_call | solution.py:525
  227.4 23.6 %collective-permute-done.16.refs_0_.refs_10_ = bf16[512,2048]{1,0:T(8,128)(2,1)} collective-permute-done((bf16[512,2048]{1,0:T(8,128)(2,1)S(1)}, bf16[512,2048]{1,0:T(8,128)(2,1)}, u32[]{:S(2)}, u32[]{:S(2)}) %collective-permute-start.16) | collective-permute-done | bytes 2097184 | tf_op jit(solution)/shard_map/ppermute | solution.py:326
  259.8 28.0 %units.4 = (bf16[512,1024]{1,0:T(8,128)(2,1)}, bf16[512,1024]{1,0:T(8,128)(2,1)}, bf16[512,1024]{1,0:T(8,128)(2,1)}, bf16[512,1024]{1,0:T(8,128)(2,1)}, bf16[512...) custom-call(bf16[512,2048]{1,0:T(8,128)(2,1)} %collective-permute-done.16., ...), custom_call_target="tpu_custom_call" | custom-call | flops 17179869184 | bytes 37748736 | tf_op jit(solution)/shard_map/units/pallas_call | solution.py:414
  288.4 13.2 %collective-permute-start.20 = (bf16[512,2048]{1,0:T(8,128)(2,1)}, bf16[512,2048]{1,0:T(8,128)(2,1)}, u32[]{:S(2)}, u32[]{:S(2)}) collective-permute-start(bf16[512,2048]{1,0:T(8,128)(2,1)} %collective-permute-done.17.refs_0_.refs_12_), channel_id=1, source_target_pairs={{0,8},{12,4},{8,24},{28,12},{24,16},{20,28},{16,0},{4,20},{1,9},{1... | collective-permute-start | bytes 6291464 | tf_op jit(solution)/shard_map/ppermute | solution.py:326
  301.6 27.9 %units.5 = (bf16[512,1024]{1,0:T(8,128)(2,1)}, bf16[512,1024]{1,0:T(8,128)(2,1)}, bf16[512,1024]{1,0:T(8,128)(2,1)}, bf16[512,1024]{1,0:T(8,128)(2,1)}, bf16[512...) custom-call(bf16[512,2048]{1,0:T(8,128)(2,1)} %collective-permute-done.17., ...), custom_call_target="tpu_custom_call" | custom-call | flops 17179869184 | bytes 37748736 | tf_op jit(solution)/shard_map/units/pallas_call | solution.py:414
  337.2 27.9 %units.6 = (bf16[512,1024]{1,0:T(8,128)(2,1)}, bf16[512,1024]{1,0:T(8,128)(2,1)}, bf16[512,1024]{1,0:T(8,128)(2,1)}, bf16[512,1024]{1,0:T(8,128)(2,1)}, bf16[512...) custom-call(bf16[512,2048]{1,0:T(8,128)(2,1)} %collective-permute-done.20., ...), custom_call_target="tpu_custom_call" | custom-call | flops 17179869184 | bytes 37748736 | tf_op jit(solution)/shard_map/units/pallas_call | solution.py:414
  375.5 28.0 %units.7 = (bf16[512,1024]{1,0:T(8,128)(2,1)}, bf16[512,1024]{1,0:T(8,128)(2,1)}, bf16[512,1024]{1,0:T(8,128)(2,1)}, bf16[512,1024]{1,0:T(8,128)(2,1)}, bf16[512...) custom-call(bf16[512,2048]{1,0:T(8,128)(2,1)} %copy-done.20, ...), custom_call_target="tpu_custom_call" | custom-call | flops 17179869184 | bytes 37748736 | tf_op jit(solution)/shard_map/units/pallas_call | solution.py:414
  403.5 5.7 add_convert_fusion.4
  411.4 26.0 %grads_product.2 = (bf16[1024,2048]{1,0:T(8,128)(2,1)}, f32[1,1024]{1,0:T(1,128)}) custom-call(bf16[512,1024]{1,0:T(8,128)(2,1)} %get-tuple-element.154.refs_0_, bf16[512,1024]{1,0:T(8,128)(2,1)} %get-tuple-element.156.refs_1_, bf16[512,1024]{1,0:T(8,128)(2,1)} %get-tuple-element.158.refs_2_, bf16[512,1024]{1,0:T(8,128)(2,1)} %get-tuple-element.160.refs_3_, ...), custom_call_target="tpu_custom_call" | custom-call | flops 17179869184 | bytes 29360128 | tf_op jit(solution)/shard_map/grads_product/pallas_call | solution.py:491
  439.0 9.7 %norm_backward.1 = (f32[512,2048]{1,0:T(8,128)}, bf16[512,2048]{1,0:T(8,128)(2,1)}, f32[8,2048]{1,0:T(8,128)}) custom-call(bf16[512,2048]{1,0:T(8,128)(2,1)} %get-tuple-element.170.one_ref, bf16[512,2048]{1,0:T(8,128)(2,1)} %collective-permute-done.29.two_ref, bf16[512,2048]{1,0:T(8,128)(2,1)} %copy-done.21, f32[512,2048]{1,0:T(8,128)} %copy-done, ...), custom_call_target="tpu_custom_call" | custom-call | tf_op jit(solution)/shard_map/norm_backward/pallas_call | solution.py:78
  449.3 10.1 %rows_product.3.grad_ref = bf16[512,2048]{1,0:T(8,128)(2,1)} custom-call(s32[8]{0:T(128)} %stack.52.owner_ref, bf16[512,2048]{1,0:T(8,128)(2,1)} %get-tuple-element.213.left_ref, f32[1,2048]{1,0:T(1,128)} %reshape.220.shift_ref, bf16[256,2048]{1,0:T(8,128)(2,1)} %bitcast.73.refs_0_, bf16[256,2048]{1,0:T(8,128)(2,1)} %copy-done.49, ...), custom_call_target="tpu_custom_call" | custom-call | flops 4294967296 | bytes 8388608 | tf_op jit(solution)/shard_map/rows_product/pallas_call | solution.py:449
  464.2 16.4 %attend_backward.1 = (bf16[512,2048]{1,0:T(8,128)(2,1)}, f32[2048,256]{1,0:T(8,128)}) custom-call(s32[3,4]{1,0:T(4,128)} %pad_add_fusion.info_ref, bf16[512,2048]{1,0:T(8,128)(2,1)} %rows_product.2.q_ref, bf16[512,2048]{1,0:T(8,128)(2,1)} %rows_product.3.grad_ref, bf16[512,2048]{1,0:T(8,128)(2,1)} %get-tuple-element.126.left_ref.o_ref, ...), custom_call_target="tpu_custom_call" | custom-call | tf_op jit(solution)/shard_map/attend_backward/pallas_call | solution.py:246
  483.5 19.6 %all-to-all-start.4 = ((bf16[4,512,256]{2,1,0:T(8,128)(2,1)}), bf16[4,512,256]{2,1,0:T(8,128)(2,1)S(1)}, u32[]{:S(2)}, u32[]{:S(2)}) async-start(bf16[4,512,256]{2,1,0:T(8,128)(2,1)} %bitcast.31), calls=%async_computation.4 | async-start | bytes 2097152 | tf_op jit(solution)/shard_map/all_to_all | solution.py:283
  508.1 26.2 %grads_product.3 = (bf16[1024,2048]{1,0:T(8,128)(2,1)}, f32[1,1024]{1,0:T(1,128)}) custom-call(bf16[512,1024]{1,0:T(8,128)(2,1)} %get-tuple-element.188.refs_0_, bf16[512,1024]{1,0:T(8,128)(2,1)} %get-tuple-element.190.refs_1_, bf16[512,1024]{1,0:T(8,128)(2,1)} %get-tuple-element.192.refs_2_, bf16[512,1024]{1,0:T(8,128)(2,1)} %get-tuple-element.194.refs_3_, ...), custom_call_target="tpu_custom_call" | custom-call | flops 17179869184 | bytes 29360128 | tf_op jit(solution)/shard_map/grads_product/pallas_call | solution.py:491
  534.6 7.0 convolution_convert_fusion
  552.7 6.4 convolution_convert_fusion.1
  566.1 19.2 %collective-permute-done.43 = bf16[256,2304]{1,0:T(8,128)(2,1)S(1)} collective-permute-done((bf16[256,2304]{1,0:T(8,128)(2,1)S(1)}, bf16[256,2304]{1,0:T(8,128)(2,1)S(1)}, u32[]{:S(2)}, u32[]{:S(2)}) %collective-permute-start.43) | collective-permute-done | bytes 1179680 | tf_op jit(solution)/shard_map/ppermute | solution.py:326
  590.7 11.5 %cols_product.3 = f32[512,2048]{1,0:T(8,128)} custom-call(s32[8]{0:T(128)} %stack.52.owner_ref, bf16[512,2048]{1,0:T(8,128)(2,1)} %get-tuple-element.210.left_ref, bf16[256,2048]{1,0:T(8,128)(2,1)} %bitcast.70.refs_0_, bf16[256,2048]{1,0:T(8,128)(2,1)} %copy-done.43, bf16[256,2048]{1,0:T(8,128)(2,1)} %collective-permute-done.2.refs_2_, ...), custom_call_target="tpu_custom_call" | custom-call | flops 4294967296 | bytes 8388608 | tf_op jit(solution)/shard_map/cols_product/pallas_call | solution.py:525
  602.2 5.9 fusion.13
  619.8 18.8 %collective-permute-done.45 = bf16[256,2304]{1,0:T(8,128)(2,1)} collective-permute-done((bf16[256,2304]{1,0:T(8,128)(2,1)}, bf16[256,2304]{1,0:T(8,128)(2,1)}, u32[]{:S(2)}, u32[]{:S(2)}) %collective-permute-start.45) | collective-permute-done | bytes 1179680 | tf_op jit(solution)/shard_map/ppermute | solution.py:326
  671.1 9.1 %collective-permute-done.49 = bf16[1,256,768]{2,1,0:T(8,128)(2,1)} collective-permute-done((bf16[1,256,768]{2,1,0:T(8,128)(2,1)}, bf16[1,256,768]{2,1,0:T(8,128)(2,1)}, u32[]{:S(2)}, u32[]{:S(2)}) %collective-permute-start.49) | collective-permute-done | bytes 393248 | tf_op jit(solution)/shard_map/ppermute | solution.py:294
  682.0 16.0 %collective-permute-done.50 = bf16[1,256,768]{2,1,0:T(8,128)(2,1)} collective-permute-done((bf16[1,256,768]{2,1,0:T(8,128)(2,1)}, bf16[1,256,768]{2,1,0:T(8,128)(2,1)}, u32[]{:S(2)}, u32[]{:S(2)}) %collective-permute-start.50) | collective-permute-done | bytes 393248 | tf_op jit(solution)/shard_map/ppermute | solution.py:294
  718.6 7.9 %all-to-all-done.7 = bf16[256,8,256]{2,0,1:T(8,128)(2,1)S(1)} async-done(((bf16[256,8,256]{2,0,1:T(8,128)(2,1)}), bf16[256,8,256]{2,0,1:T(8,128)(2,1)S(1)}, u32[]{:S(2)}, u32[]{:S(2)}) %all-to-all-start.7) | async-done | bytes 1048608 | tf_op jit(solution)/shard_map/all_to_all | solution.py:719
  734.6 6.3 add_convert_fusion
  (345 shorter events, 234.1 us)
Async XLA Ops:
  7.2 51.8 %all-gather.6.cloned.1.call-start = ((), (), s32[]{:S(2)}) async-start(), calls=%async_computation.16 | async-start | bytes 2621440 | tf_op jit(solution)/shard_map/all_gather | solution.py:578
  82.0 176.5 %all-gather.4.cloned.1.call-start = ((), (), s32[]{:S(2)}) async-start(), calls=%async_computation.12 | async-start | bytes 10485760 | tf_op jit(solution)/shard_map/all_gather | solution.py:599
  108.7 596.7 %reduce-scatter.6.cloned.1.call-start = ((), (), s32[]{:S(2)}) async-start(), calls=%async_computation.14 | async-start | bytes 5242880 | tf_op jit(solution)/shard_map/reduce_scatter | solution.py:666
  108.7 35.0 %collective-permute-start = (bf16[512,2048]{1,0:T(8,128)(2,1)}, bf16[512,2048]{1,0:T(8,128)(2,1)}, u32[]{:S(2)}, u32[]{:S(2)}) collective-permute-start(bf16[512,2048]{1,0:T(8,128)(2,1)} %refs_8_.1), channel_id=1, source_target_pairs={{0,8},{12,4},{8,24},{28,12},{24,16},{20,28},{16,0},{4,20},{1,9},{1... | collective-permute-start | bytes 6291464 | tf_op jit(solution)/shard_map/ppermute | solution.py:326
  158.8 44.9 %collective-permute-start.8 = (bf16[512,2048]{1,0:T(8,128)(2,1)}, bf16[512,2048]{1,0:T(8,128)(2,1)}, u32[]{:S(2)}, u32[]{:S(2)}) collective-permute-start(bf16[512,2048]{1,0:T(8,128)(2,1)} %collective-permute-done.refs_2_.refs_10_), channel_id=1, source_target_pairs={{0,8},{12,4},{8,24},{28,12},{24,16},{20,28},{16,0},{4,20},{1,9},{1... | collective-permute-start | bytes 6291464 | tf_op jit(solution)/shard_map/ppermute | solution.py:326
  171.4 32.3 %collective-permute-start.14 = (bf16[256,2048]{1,0:T(8,128)(2,1)S(1)}, bf16[256,2048]{1,0:T(8,128)(2,1)S(1)}, u32[]{:S(2)}, u32[]{:S(2)}) collective-permute-start(bf16[256,2048]{1,0:T(8,128)(2,1)S(1)} %collective-permute-done.12.refs_4_), channel_id=1, source_target_pairs={{0,8},{12,4},{8,24},{28,12},{24,16},{20,28},{16,0},{4,20},{1,9},{1... | collective-permute-start | bytes 3145736 | tf_op jit(solution)/shard_map/ppermute | solution.py:326
  251.6 36.2 %collective-permute-start.17 = (bf16[512,2048]{1,0:T(8,128)(2,1)}, bf16[512,2048]{1,0:T(8,128)(2,1)}, u32[]{:S(2)}, u32[]{:S(2)}) collective-permute-start(bf16[512,2048]{1,0:T(8,128)(2,1)} %collective-permute-done.16.refs_0_.refs_10_), channel_id=1, source_target_pairs={{0,8},{12,4},{8,24},{28,12},{24,16},{20,28},{16,0},{4,20},{1,9},{1... | collective-permute-start | bytes 6291464 | tf_op jit(solution)/shard_map/ppermute | solution.py:326
  254.7 46.9 %collective-permute-start.24 = (bf16[512,2048]{1,0:T(8,128)(2,1)}, bf16[512,2048]{1,0:T(8,128)(2,1)}, u32[]{:S(2)}, u32[]{:S(2)}) collective-permute-start(bf16[512,2048]{1,0:T(8,128)(2,1)} %collective-permute-done.8.refs_2_.refs_12_), channel_id=1, source_target_pairs={{0,8},{12,4},{8,24},{28,12},{24,16},{20,28},{16,0},{4,20},{1,9},{1... | collective-permute-start | bytes 6291464 | tf_op jit(solution)/shard_map/ppermute | solution.py:326
  288.4 41.2 %collective-permute-start.20 = (bf16[512,2048]{1,0:T(8,128)(2,1)}, bf16[512,2048]{1,0:T(8,128)(2,1)}, u32[]{:S(2)}, u32[]{:S(2)}) collective-permute-start(bf16[512,2048]{1,0:T(8,128)(2,1)} %collective-permute-done.17.refs_0_.refs_12_), channel_id=1, source_target_pairs={{0,8},{12,4},{8,24},{28,12},{24,16},{20,28},{16,0},{4,20},{1,9},{1... | collective-permute-start | bytes 6291464 | tf_op jit(solution)/shard_map/ppermute | solution.py:326
  330.2 35.9 %collective-permute-start.31 = (bf16[512,2048]{1,0:T(8,128)(2,1)}, bf16[512,2048]{1,0:T(8,128)(2,1)}, u32[]{:S(2)}, u32[]{:S(2)}) collective-permute-start(bf16[512,2048]{1,0:T(8,128)(2,1)} %get-tuple-element.138), channel_id=1, source_target_pairs={{0,4},{4,0},{8,12},{12,8},{16,20},{20,16},{24,28},{28,24},{1,5},{5... | collective-permute-start | bytes 6291464 | tf_op jit(solution)/shard_map/ppermute | solution.py:329
  334.3 31.8 %collective-permute-start.33 = (bf16[512,2048]{1,0:T(8,128)(2,1)}, bf16[512,2048]{1,0:T(8,128)(2,1)}, u32[]{:S(2)}, u32[]{:S(2)}) collective-permute-start(bf16[512,2048]{1,0:T(8,128)(2,1)} %add_convert_fusion.6), channel_id=1, source_target_pairs={{0,8},{12,4},{8,24},{28,12},{24,16},{20,28},{16,0},{4,20},{1,9},{1... | collective-permute-start | bytes 6291464 | tf_op jit(solution)/shard_map/ppermute | solution.py:326
  365.7 37.8 %collective-permute-start.30 = (bf16[512,2048]{1,0:T(8,128)(2,1)}, bf16[512,2048]{1,0:T(8,128)(2,1)}, u32[]{:S(2)}, u32[]{:S(2)}) collective-permute-start(bf16[512,2048]{1,0:T(8,128)(2,1)} %get-tuple-element.144), channel_id=1, source_target_pairs={{0,4},{4,0},{8,12},{12,8},{16,20},{20,16},{24,28},{28,24},{1,5},{5... | collective-permute-start | bytes 6291464 | tf_op jit(solution)/shard_map/ppermute | solution.py:329
  410.9 48.5 %collective-permute-start.36 = (bf16[512,2048]{1,0:T(8,128)(2,1)}, bf16[512,2048]{1,0:T(8,128)(2,1)}, u32[]{:S(2)}, u32[]{:S(2)}) collective-permute-start(bf16[512,2048]{1,0:T(8,128)(2,1)} %get-tuple-element.183), channel_id=1, source_target_pairs={{0,4},{4,0},{8,12},{12,8},{16,20},{20,16},{24,28},{28,24},{1,5},{5... | collective-permute-start | bytes 6291464 | tf_op jit(solution)/shard_map/ppermute | solution.py:329
  437.5 46.1 %collective-permute-start.37 = (bf16[512,2048]{1,0:T(8,128)(2,1)}, bf16[512,2048]{1,0:T(8,128)(2,1)}, u32[]{:S(2)}, u32[]{:S(2)}) collective-permute-start(bf16[512,2048]{1,0:T(8,128)(2,1)} %get-tuple-element.186), channel_id=1, source_target_pairs={{0,4},{4,0},{8,12},{12,8},{16,20},{20,16},{24,28},{28,24},{1,5},{5... | collective-permute-start | bytes 6291464 | tf_op jit(solution)/shard_map/ppermute | solution.py:329
  463.2 40.1 %collective-permute-start.38 = (bf16[512,2048]{1,0:T(8,128)(2,1)}, bf16[512,2048]{1,0:T(8,128)(2,1)}, u32[]{:S(2)}, u32[]{:S(2)}) collective-permute-start(bf16[512,2048]{1,0:T(8,128)(2,1)} %add_convert_fusion.3), channel_id=1, source_target_pairs={{0,8},{12,4},{8,24},{28,12},{24,16},{20,28},{16,0},{4,20},{1,9},{1... | collective-permute-start | bytes 6291464 | tf_op jit(solution)/shard_map/ppermute | solution.py:326
  464.0 83.4 %collective-permute-start.46 = (bf16[512,2048]{1,0:T(8,128)(2,1)}, bf16[512,2048]{1,0:T(8,128)(2,1)}, u32[]{:S(2)}, u32[]{:S(2)}) collective-permute-start(bf16[512,2048]{1,0:T(8,128)(2,1)} %get-tuple-element.207), channel_id=1, source_target_pairs={{0,4},{4,0},{8,12},{12,8},{16,20},{20,16},{24,28},{28,24},{1,5},{5... | collective-permute-start | bytes 6291464 | tf_op jit(solution)/shard_map/ppermute | solution.py:329
  483.5 50.8 %all-to-all-start.4 = ((bf16[4,512,256]{2,1,0:T(8,128)(2,1)}), bf16[4,512,256]{2,1,0:T(8,128)(2,1)S(1)}, u32[]{:S(2)}, u32[]{:S(2)}) async-start(bf16[4,512,256]{2,1,0:T(8,128)(2,1)} %bitcast.31), calls=%async_computation.4 | async-start | bytes 2097152 | tf_op jit(solution)/shard_map/all_to_all | solution.py:283
  503.1 225.4 %reduce-scatter.8.cloned.1.call-start = ((), (), s32[]{:S(2)}) async-start(), calls=%async_computation.15 | async-start | bytes 5242880 | tf_op jit(solution)/shard_map/reduce_scatter | solution.py:700
  546.4 101.3 %collective-permute-start.47 = (bf16[512,2048]{1,0:T(8,128)(2,1)}, bf16[512,2048]{1,0:T(8,128)(2,1)}, u32[]{:S(2)}, u32[]{:S(2)}) collective-permute-start(bf16[512,2048]{1,0:T(8,128)(2,1)} %add_convert_fusion.2), channel_id=1, source_target_pairs={{0,8},{12,4},{8,24},{28,12},{24,16},{20,28},{16,0},{4,20},{1,9},{1... | collective-permute-start | bytes 6291464 | tf_op jit(solution)/shard_map/ppermute | solution.py:326
  551.4 33.9 %collective-permute-start.43 = (bf16[256,2304]{1,0:T(8,128)(2,1)S(1)}, bf16[256,2304]{1,0:T(8,128)(2,1)S(1)}, u32[]{:S(2)}, u32[]{:S(2)}) collective-permute-start(bf16[256,2304]{1,0:T(8,128)(2,1)S(1)} %add_convert_fusion.10), channel_id=1, source_target_pairs={{0,8},{12,4},{8,24},{28,12},{24,16},{20,28},{16,0},{4,20},{1,9},{1... | collective-permute-start | bytes 3538952 | tf_op jit(solution)/shard_map/ppermute | solution.py:326
  560.9 80.2 %collective-permute-start.54 = (bf16[256,2048]{1,0:T(8,128)(2,1)}, bf16[256,2048]{1,0:T(8,128)(2,1)}, u32[]{:S(2)}, u32[]{:S(2)}) collective-permute-start(bf16[256,2048]{1,0:T(8,128)(2,1)} %get-tuple-element.233), channel_id=1, source_target_pairs={{0,4},{4,0},{8,12},{12,8},{16,20},{20,16},{24,28},{28,24},{1,5},{5... | collective-permute-start | bytes 3145736 | tf_op jit(solution)/shard_map/ppermute | solution.py:329
  566.0 53.4 %collective-permute-start.39 = (bf16[256,2304]{1,0:T(8,128)(2,1)S(1)}, bf16[256,2304]{1,0:T(8,128)(2,1)}, u32[]{:S(2)}, u32[]{:S(2)}) collective-permute-start(bf16[256,2304]{1,0:T(8,128)(2,1)S(1)} %get-tuple-element.227), channel_id=1, source_target_pairs={{0,4},{4,0},{8,12},{12,8},{16,20},{20,16},{24,28},{28,24},{1,5},{5... | collective-permute-start | bytes 3538952 | tf_op jit(solution)/shard_map/ppermute | solution.py:329
  608.1 33.0 %collective-permute-start.56 = (bf16[256,2048]{1,0:T(8,128)(2,1)}, bf16[256,2048]{1,0:T(8,128)(2,1)}, u32[]{:S(2)}, u32[]{:S(2)}) collective-permute-start(bf16[256,2048]{1,0:T(8,128)(2,1)} %add_convert_fusion.13), channel_id=1, source_target_pairs={{0,8},{12,4},{8,24},{28,12},{24,16},{20,28},{16,0},{4,20},{1,9},{1... | collective-permute-start | bytes 3145736 | tf_op jit(solution)/shard_map/ppermute | solution.py:326
  615.3 37.2 %all-to-all-start.5 = ((f32[8,1,15488]{2,1,0:T(1,128)}), f32[8,1,15488]{2,1,0:T(1,128)}, u32[]{:S(2)}, u32[]{:S(2)}) async-start(f32[8,1,15488]{2,1,0:T(1,128)} %broadcast_in_dim.20), calls=%async_computation.5 | async-start | bytes 991232 | tf_op jit(solution)/shard_map/all_to_all | solution.py:278
  619.5 51.5 %collective-permute-start.52 = (bf16[256,2048]{1,0:T(8,128)(2,1)}, bf16[256,2048]{1,0:T(8,128)(2,1)}, u32[]{:S(2)}, u32[]{:S(2)}) collective-permute-start(bf16[256,2048]{1,0:T(8,128)(2,1)} %get-tuple-element.231), channel_id=1, source_target_pairs={{0,4},{4,0},{8,12},{12,8},{16,20},{20,16},{24,28},{28,24},{1,5},{5... | collective-permute-start | bytes 3145736 | tf_op jit(solution)/shard_map/ppermute | solution.py:329
  657.2 42.5 %collective-permute-start.51 = (bf16[1,256,768]{2,1,0:T(8,128)(2,1)}, bf16[1,256,768]{2,1,0:T(8,128)(2,1)}, u32[]{:S(2)}, u32[]{:S(2)}) collective-permute-start(bf16[1,256,768]{2,1,0:T(8,128)(2,1)} %get-tuple-element.237), channel_id=1, source_target_pairs={{0,3},{1,0},{2,1},{3,2},{4,7},{5,4},{6,5},{7,6},{8,11},{9,8},{10,9... | collective-permute-start | bytes 1179656 | tf_op jit(solution)/shard_map/ppermute | solution.py:294
  660.8 37.2 %collective-permute-start.50 = (bf16[1,256,768]{2,1,0:T(8,128)(2,1)}, bf16[1,256,768]{2,1,0:T(8,128)(2,1)}, u32[]{:S(2)}, u32[]{:S(2)}) collective-permute-start(bf16[1,256,768]{2,1,0:T(8,128)(2,1)} %get-tuple-element.240), channel_id=1, source_target_pairs={{0,2},{1,3},{2,0},{3,1},{4,6},{5,7},{6,4},{7,5},{8,10},{9,11},{10,... | collective-permute-start | bytes 1179656 | tf_op jit(solution)/shard_map/ppermute | solution.py:294
  664.3 37.2 %collective-permute-start.58 = (bf16[256,2048]{1,0:T(8,128)(2,1)S(1)}, bf16[256,2048]{1,0:T(8,128)(2,1)}, u32[]{:S(2)}, u32[]{:S(2)}) collective-permute-start(bf16[256,2048]{1,0:T(8,128)(2,1)S(1)} %add_convert_fusion.11), channel_id=1, source_target_pairs={{0,8},{12,4},{8,24},{28,12},{24,16},{20,28},{16,0},{4,20},{1,9},{1... | collective-permute-start | bytes 3145736 | tf_op jit(solution)/shard_map/ppermute | solution.py:326
  666.2 41.4 %all-to-all-start.6 = ((f32[4,1,16512]{2,1,0:T(1,128)}), f32[4,1,16512]{2,1,0:T(1,128)S(1)}, u32[]{:S(2)}, u32[]{:S(2)}) async-start(f32[4,1,16512]{2,1,0:T(1,128)} %all_to_all.72), calls=%async_computation.6 | async-start | bytes 528384 | tf_op jit(solution)/shard_map/all_to_all | solution.py:745
  671.0 73.2 %reduce-scatter.4.cloned.1.call-start = ((), (), s32[]{:S(2)}) async-start(), calls=%async_computation.13 | async-start | bytes 1310720 | tf_op jit(solution)/shard_map/reduce_scatter | solution.py:690
  671.0 47.6 %collective-permute-start.28 = (bf16[512,2048]{1,0:T(8,128)(2,1)}, bf16[512,2048]{1,0:T(8,128)(2,1)}, u32[]{:S(2)}, u32[]{:S(2)}) collective-permute-start(bf16[512,2048]{1,0:T(8,128)(2,1)} %get-tuple-element.150), channel_id=1, source_target_pairs={{0,4},{4,0},{8,12},{12,8},{16,20},{20,16},{24,28},{28,24},{1,5},{5... | collective-permute-start | bytes 6291464 | tf_op jit(solution)/shard_map/ppermute | solution.py:329
  680.2 54.4 %collective-permute-start.48 = (bf16[512,2048]{1,0:T(8,128)(2,1)}, bf16[512,2048]{1,0:T(8,128)(2,1)}, u32[]{:S(2)}, u32[]{:S(2)}) collective-permute-start(bf16[512,2048]{1,0:T(8,128)(2,1)} %add_convert_fusion.1), channel_id=1, source_target_pairs={{0,8},{12,4},{8,24},{28,12},{24,16},{20,28},{16,0},{4,20},{1,9},{1... | collective-permute-start | bytes 6291464 | tf_op jit(solution)/shard_map/ppermute | solution.py:326
  (93 other events, 1275.5 us)
Sparse Core Ops, SparseCore 0:
  10.3 48.6 all-gather.5
  108.8 146.8 all-gather.3
  437.6 84.5 reduce-scatter.5
  547.6 78.2 reduce-scatter.7
  705.4 26.6 reduce-scatter.3
where the time goes:
time: 768 us; the launch traced here: 758 us
  Pallas kernels  245 us (32%)
  waiting for transfers between devices  201 us (26%)
  starting transfers between devices  105 us (14%)
  other arithmetic  87.1 us (11%)
  local copies, waits for them, and re-layouts  66.4 us (9%)
  between operations  25.6 us (3%)
  matrix products  16.8 us (2%)
  blocking collectives  11.7 us (2%)
    pallas_call x4, Pallas kernels, units(): pl.pallas_call(functools.partial(units_kernel, count, piece, tiles), grid...  112 us
    ppermute x24, waiting for transfers between devices, step(): return lax.ppermute(value, 'dp', self.pairs)  109 us
    pallas_call x2, Pallas kernels, grads_product(): pl.pallas_call(functools.partial(grads_product_kernel, count), grid=(widt...  52.3 us
    ppermute x24, starting transfers between devices, step(): return lax.ppermute(value, 'dp', self.pairs)  46.1 us
    convert_element_type x12, other arithmetic, sums(): value = total(shares).astype(bf16)  43.9 us
    all_to_all x3, waiting for transfers between devices, axis_gather(): return lax.all_to_all(copies, axis, 0, 0)  29.7 us
    unnamed x123, local copies, waits for them, and re-layouts  28.4 us
    ppermute x3, waiting for transfers between devices, tensor_swaps(): lax.ppermute(part, 'tensor', [(i, (i + s) % size) for i in range(size)])  25.1 us
  transfers between devices with their start and end apart: 72, of which 22 were waited for; matrix products, arithmetic and copies ran while one was open for 18% of the time, Pallas kernels for 32%

commit v1 on v0

--- a/solution.py
+++ b/solution.py
@@ -742,8 +742,7 @@
     units_flat = flat[:, plain:].reshape(n_dp, n_tensor, hidden_own)
     units_flat = units_flat.transpose(1, 0, 2).reshape(n_tensor, n_dp * hidden_own)
     flat = jnp.broadcast_to(jnp.sum(flat[:, :plain], axis=0), (n_tensor, plain))
-    flat = lax.all_to_all(jnp.concatenate([flat, units_flat], axis=1), "tensor", 0, 0, tiled=True)
-    flat = jnp.sum(flat, axis=0)
+    flat = jnp.concatenate([flat, units_flat], axis=1)
 
     first_sent = first_part.astype(bf16)
     first_sent = jnp.concatenate(
@@ -756,6 +755,8 @@
     first_sent = tensor_swaps(first_sent)
     down_grad = lax.all_to_all(after(down_part, up_grad), "dp", 1, 0, tiled=True).astype(f32)
     out_grad = width_owner(after(out_part, first_sent)).T
+    flat = lax.all_to_all(after(flat, down_grad), "tensor", 0, 0, tiled=True)
+    flat = jnp.sum(flat, axis=0)
     first_grad = jnp.sum(first_sent.astype(f32), axis=0)
     query_grad = first_grad[:, :width]
     keyvalue_grad = first_grad[:, width:]

time: 768 us -> 755 us (0.983)
  waiting for transfers between devices: 201 us -> 192 us
    ppermute x3, waiting for transfers between devices: 25.1 us -> 12.7 us  [tensor_swaps(): lax.ppermute(part, 'tensor', [(i, (i + s) % size) for i in range(size)])]
    all_to_all x1, waiting for transfers between devices: 7.94 us -> 0.01 us  [on_device(): lax.all_to_all(after(up_part, first_part), 'dp', 1, 0, tiled=True)]
    unnamed x123 -> x129, local copies, waits for them, and re-layouts: 28.4 us -> 27.9 us
  transfers between devices with their start and end apart: 72 -> 72, of which waited for: 22 -> 24; matrix products, arithmetic and copies ran while one was open for 18% -> 19% of each run, Pallas kernels for 32% -> 33%
where the time goes in v1:
time: 755 us; the launch traced here: 747 us
  Pallas kernels  245 us (32%)
  waiting for transfers between devices  192 us (25%)
  starting transfers between devices  103 us (14%)
  other arithmetic  88.1 us (12%)
  local copies, waits for them, and re-layouts  64.6 us (9%)
  between operations  25.6 us (3%)
  matrix products  16.8 us (2%)
  blocking collectives  11.7 us (2%)
    ppermute x24, waiting for transfers between devices, step(): return lax.ppermute(value, 'dp', self.pairs)  115 us
    pallas_call x4, Pallas kernels, units(): pl.pallas_call(functools.partial(units_kernel, count, piece, tiles), grid...  112 us
    pallas_call x2, Pallas kernels, grads_product(): pl.pallas_call(functools.partial(grads_product_kernel, count), grid=(widt...  52.2 us
    convert_element_type x12, other arithmetic, sums(): value = total(shares).astype(bf16)  43.9 us
    ppermute x24, starting transfers between devices, step(): return lax.ppermute(value, 'dp', self.pairs)  43.7 us
    all_to_all x3, waiting for transfers between devices, axis_gather(): return lax.all_to_all(copies, axis, 0, 0)  29.7 us
    unnamed x129, local copies, waits for them, and re-layouts  27.9 us
    pallas_call x2, Pallas kernels, cols_product(): pl.pallas_call(functools.partial(cols_product_kernel, depth), grid_spec=p...  22.8 us
  transfers between devices with their start and end apart: 72, of which 24 were waited for; matrix products, arithmetic and copies ran while one was open for 19% of the time, Pallas kernels for 33%

profile of v1, /device:TPU:0, one launch (start us, length us, event | category | flops | bytes accessed | tf_op | source)
XLA Modules:
  0.0 746.7 jit_solution(2062243128008658724)
XLA Ops:
  11.0 11.7 %all_to_all.87 = f32[4,1,768]{2,1,0:T(1,128)S(1)} all-to-all(f32[4,1,768]{2,1,0:T(1,128)S(1)} %broadcast_in_dim.16), channel_id=1, replica_groups=mesh['dp'=8,'tensor'=4] {'tensor'}, dimensions={0} | all-to-all | bytes 24576 | tf_op jit(solution)/shard_map/all_to_all | solution.py:278
  32.9 10.1 %all-to-all-done.1 = bf16[8,256,256]{2,1,0:T(8,128)(2,1)S(1)} async-done(((bf16[8,256,256]{2,1,0:T(8,128)(2,1)}), bf16[8,256,256]{2,1,0:T(8,128)(2,1)S(1)}, u32[]{:S(2)}, u32[]{:S(2)}) %all-to-all-start.1) | async-done | bytes 1048608 | tf_op jit(solution)/shard_map/all_to_all | solution.py:278
  48.1 10.9 %all-gather.6.cloned.1.call-done = bf16[8,256,512]{2,1,0:T(8,128)(2,1)} async-done(((bf16[2,256,512]{2,1,0:T(8,128)(2,1)}), bf16[8,256,512]{2,1,0:T(8,128)(2,1)}) %all-gather.6.cloned.1.call-update) | async-done | bytes 2097168 | tf_op jit(solution)/shard_map/all_gather | solution.py:578
  85.3 19.6 %all-to-all-done.3 = bf16[4,512,256]{2,1,0:T(8,128)(2,1)S(1)} async-done(((bf16[4,512,256]{2,1,0:T(8,128)(2,1)}), bf16[4,512,256]{2,1,0:T(8,128)(2,1)S(1)}, u32[]{:S(2)}, u32[]{:S(2)}) %all-to-all-start.3) | async-done | bytes 1048608 | tf_op jit(solution)/shard_map/all_to_all | solution.py:278
  109.6 11.7 %collective-permute-done.6.refs_6_ = bf16[256,2048]{1,0:T(8,128)(2,1)} collective-permute-done((bf16[256,2048]{1,0:T(8,128)(2,1)}, bf16[256,2048]{1,0:T(8,128)(2,1)}, u32[]{:S(2)}, u32[]{:S(2)}) %collective-permute-start.6) | collective-permute-done | bytes 1048608 | tf_op jit(solution)/shard_map/ppermute | solution.py:326
  143.7 10.1 %rows_product.2.q_ref = bf16[512,2048]{1,0:T(8,128)(2,1)} custom-call(s32[8]{0:T(128)} %stack.52.owner_ref, bf16[512,2048]{1,0:T(8,128)(2,1)} %copy-done.13, f32[1,2048]{1,0:T(1,128)} %bitcast.141, bf16[256,2048]{1,0:T(8,128)(2,1)} %bitcast.70.refs_0_, bf16[256,2048]{1,0:T(8,128)(2,1)} %copy-done.46, bf16[256,2048]{1,0:T(8,128)(2,1)} %collective-permute-done.2.refs_2_, ...), custom_call_target="tpu_custom_call" | custom-call | flops 4294967296 | bytes 8388608 | tf_op jit(solution)/shard_map/rows_product/pallas_call | solution.py:449
  159.3 12.0 %attend_forward.1 = (bf16[512,2048]{1,0:T(8,128)(2,1)}, f32[1,4,1,2048]{3,2,1,0:T(1,128)}) custom-call(s32[3,4]{1,0:T(4,128)} %pad_add_fusion.info_ref, bf16[512,2048]{1,0:T(8,128)(2,1)} %rows_product.2.q_ref, bf16[2048,256]{1,0:T(8,128)(2,1)} %bitcast.105, s32[1,512]{1,0:T(1,128)} %bitcast.138), custom_call_target="tpu_custom_call" | custom-call | tf_op jit(solution)/shard_map/attend_forward/pallas_call | solution.py:220
  173.0 30.7 %collective-permute-done.14.refs_6_ = bf16[256,2048]{1,0:T(8,128)(2,1)S(1)} collective-permute-done((bf16[256,2048]{1,0:T(8,128)(2,1)S(1)}, bf16[256,2048]{1,0:T(8,128)(2,1)S(1)}, u32[]{:S(2)}, u32[]{:S(2)}) %collective-permute-start.14) | collective-permute-done | bytes 1048608 | tf_op jit(solution)/shard_map/ppermute | solution.py:326
  206.5 11.4 %cols_product.2 = f32[512,2048]{1,0:T(8,128)} custom-call(s32[8]{0:T(128)} %stack.52.owner_ref, bf16[512,2048]{1,0:T(8,128)(2,1)} %get-tuple-element.127.left_ref.o_ref, bf16[256,2048]{1,0:T(8,128)(2,1)} %bitcast.73.refs_0_, bf16[256,2048]{1,0:T(8,128)(2,1)} %copy-done.52, bf16[256,2048]{1,0:T(8,128)(2,1)} %collective-permute-done.10.refs_2_, ...), custom_call_target="tpu_custom_call" | custom-call | flops 4294967296 | bytes 8388608 | tf_op jit(solution)/shard_map/cols_product/pallas_call | solution.py:525
  227.4 23.6 %collective-permute-done.16.refs_0_.refs_10_ = bf16[512,2048]{1,0:T(8,128)(2,1)} collective-permute-done((bf16[512,2048]{1,0:T(8,128)(2,1)S(1)}, bf16[512,2048]{1,0:T(8,128)(2,1)}, u32[]{:S(2)}, u32[]{:S(2)}) %collective-permute-start.16) | collective-permute-done | bytes 2097184 | tf_op jit(solution)/shard_map/ppermute | solution.py:326
  259.7 28.0 %units.4 = (bf16[512,1024]{1,0:T(8,128)(2,1)}, bf16[512,1024]{1,0:T(8,128)(2,1)}, bf16[512,1024]{1,0:T(8,128)(2,1)}, bf16[512,1024]{1,0:T(8,128)(2,1)}, bf16[512...) custom-call(bf16[512,2048]{1,0:T(8,128)(2,1)} %collective-permute-done.16., ...), custom_call_target="tpu_custom_call" | custom-call | flops 17179869184 | bytes 37748736 | tf_op jit(solution)/shard_map/units/pallas_call | solution.py:414
  288.3 13.2 %collective-permute-start.20 = (bf16[512,2048]{1,0:T(8,128)(2,1)}, bf16[512,2048]{1,0:T(8,128)(2,1)}, u32[]{:S(2)}, u32[]{:S(2)}) collective-permute-start(bf16[512,2048]{1,0:T(8,128)(2,1)} %collective-permute-done.17.refs_0_.refs_12_), channel_id=1, source_target_pairs={{0,8},{12,4},{8,24},{28,12},{24,16},{20,28},{16,0},{4,20},{1,9},{1... | collective-permute-start | bytes 6291464 | tf_op jit(solution)/shard_map/ppermute | solution.py:326
  301.5 27.9 %units.5 = (bf16[512,1024]{1,0:T(8,128)(2,1)}, bf16[512,1024]{1,0:T(8,128)(2,1)}, bf16[512,1024]{1,0:T(8,128)(2,1)}, bf16[512,1024]{1,0:T(8,128)(2,1)}, bf16[512...) custom-call(bf16[512,2048]{1,0:T(8,128)(2,1)} %collective-permute-done.17., ...), custom_call_target="tpu_custom_call" | custom-call | flops 17179869184 | bytes 37748736 | tf_op jit(solution)/shard_map/units/pallas_call | solution.py:414
  337.1 28.0 %units.6 = (bf16[512,1024]{1,0:T(8,128)(2,1)}, bf16[512,1024]{1,0:T(8,128)(2,1)}, bf16[512,1024]{1,0:T(8,128)(2,1)}, bf16[512,1024]{1,0:T(8,128)(2,1)}, bf16[512...) custom-call(bf16[512,2048]{1,0:T(8,128)(2,1)} %collective-permute-done.20., ...), custom_call_target="tpu_custom_call" | custom-call | flops 17179869184 | bytes 37748736 | tf_op jit(solution)/shard_map/units/pallas_call | solution.py:414
  375.4 28.0 %units.7 = (bf16[512,1024]{1,0:T(8,128)(2,1)}, bf16[512,1024]{1,0:T(8,128)(2,1)}, bf16[512,1024]{1,0:T(8,128)(2,1)}, bf16[512,1024]{1,0:T(8,128)(2,1)}, bf16[512...) custom-call(bf16[512,2048]{1,0:T(8,128)(2,1)} %copy-done.20, ...), custom_call_target="tpu_custom_call" | custom-call | flops 17179869184 | bytes 37748736 | tf_op jit(solution)/shard_map/units/pallas_call | solution.py:414
  403.5 5.7 add_convert_fusion.4
  411.4 26.0 %grads_product.2 = (bf16[1024,2048]{1,0:T(8,128)(2,1)}, f32[1,1024]{1,0:T(1,128)}) custom-call(bf16[512,1024]{1,0:T(8,128)(2,1)} %get-tuple-element.155.refs_0_, bf16[512,1024]{1,0:T(8,128)(2,1)} %get-tuple-element.157.refs_1_, bf16[512,1024]{1,0:T(8,128)(2,1)} %get-tuple-element.159.refs_2_, bf16[512,1024]{1,0:T(8,128)(2,1)} %get-tuple-element.161.refs_3_, ...), custom_call_target="tpu_custom_call" | custom-call | flops 17179869184 | bytes 29360128 | tf_op jit(solution)/shard_map/grads_product/pallas_call | solution.py:491
  438.9 9.7 %norm_backward.1 = (f32[512,2048]{1,0:T(8,128)}, bf16[512,2048]{1,0:T(8,128)(2,1)}, f32[8,2048]{1,0:T(8,128)}) custom-call(bf16[512,2048]{1,0:T(8,128)(2,1)} %get-tuple-element.171.one_ref, bf16[512,2048]{1,0:T(8,128)(2,1)} %collective-permute-done.29.two_ref, bf16[512,2048]{1,0:T(8,128)(2,1)} %copy-done.21, f32[512,2048]{1,0:T(8,128)} %copy-done, ...), custom_call_target="tpu_custom_call" | custom-call | tf_op jit(solution)/shard_map/norm_backward/pallas_call | solution.py:78
  449.2 10.2 %rows_product.3.grad_ref = bf16[512,2048]{1,0:T(8,128)(2,1)} custom-call(s32[8]{0:T(128)} %stack.52.owner_ref, bf16[512,2048]{1,0:T(8,128)(2,1)} %get-tuple-element.217.left_ref, f32[1,2048]{1,0:T(1,128)} %reshape.220.shift_ref, bf16[256,2048]{1,0:T(8,128)(2,1)} %bitcast.73.refs_0_, bf16[256,2048]{1,0:T(8,128)(2,1)} %copy-done.52, ...), custom_call_target="tpu_custom_call" | custom-call | flops 4294967296 | bytes 8388608 | tf_op jit(solution)/shard_map/rows_product/pallas_call | solution.py:449
  464.1 16.3 %attend_backward.1 = (bf16[512,2048]{1,0:T(8,128)(2,1)}, f32[2048,256]{1,0:T(8,128)}) custom-call(s32[3,4]{1,0:T(4,128)} %pad_add_fusion.info_ref, bf16[512,2048]{1,0:T(8,128)(2,1)} %rows_product.2.q_ref, bf16[512,2048]{1,0:T(8,128)(2,1)} %rows_product.3.grad_ref, bf16[512,2048]{1,0:T(8,128)(2,1)} %get-tuple-element.127.left_ref.o_ref, ...), custom_call_target="tpu_custom_call" | custom-call | tf_op jit(solution)/shard_map/attend_backward/pallas_call | solution.py:246
  483.3 12.5 %all-to-all-start.4 = ((bf16[4,512,256]{2,1,0:T(8,128)(2,1)}), bf16[4,512,256]{2,1,0:T(8,128)(2,1)S(1)}, u32[]{:S(2)}, u32[]{:S(2)}) async-start(bf16[4,512,256]{2,1,0:T(8,128)(2,1)} %bitcast.31), calls=%async_computation.4 | async-start | bytes 2097152 | tf_op jit(solution)/shard_map/all_to_all | solution.py:283
  500.8 26.2 %grads_product.3 = (bf16[1024,2048]{1,0:T(8,128)(2,1)}, f32[1,1024]{1,0:T(1,128)}) custom-call(bf16[512,1024]{1,0:T(8,128)(2,1)} %get-tuple-element.189.refs_0_, bf16[512,1024]{1,0:T(8,128)(2,1)} %get-tuple-element.191.refs_1_, bf16[512,1024]{1,0:T(8,128)(2,1)} %get-tuple-element.193.refs_2_, bf16[512,1024]{1,0:T(8,128)(2,1)} %get-tuple-element.195.refs_3_, ...), custom_call_target="tpu_custom_call" | custom-call | flops 17179869184 | bytes 29360128 | tf_op jit(solution)/shard_map/grads_product/pallas_call | solution.py:491
  526.9 6.7 all-to-all-done.4
  533.9 7.0 convolution_convert_fusion
  552.7 6.4 convolution_convert_fusion.1
  567.6 18.6 %collective-permute-done.43 = bf16[256,2304]{1,0:T(8,128)(2,1)S(1)} collective-permute-done((bf16[256,2304]{1,0:T(8,128)(2,1)S(1)}, bf16[256,2304]{1,0:T(8,128)(2,1)S(1)}, u32[]{:S(2)}, u32[]{:S(2)}) %collective-permute-start.43) | collective-permute-done | bytes 1179680 | tf_op jit(solution)/shard_map/ppermute | solution.py:326
  597.5 11.4 %cols_product.3 = f32[512,2048]{1,0:T(8,128)} custom-call(s32[8]{0:T(128)} %stack.52.owner_ref, bf16[512,2048]{1,0:T(8,128)(2,1)} %get-tuple-element.211.left_ref, bf16[256,2048]{1,0:T(8,128)(2,1)} %bitcast.70.refs_0_, bf16[256,2048]{1,0:T(8,128)(2,1)} %copy-done.46, bf16[256,2048]{1,0:T(8,128)(2,1)} %collective-permute-done.2.refs_2_, ...), custom_call_target="tpu_custom_call" | custom-call | flops 4294967296 | bytes 8388608 | tf_op jit(solution)/shard_map/cols_product/pallas_call | solution.py:525
  613.6 5.9 fusion.13
  619.6 17.0 %collective-permute-done.45 = bf16[256,2304]{1,0:T(8,128)(2,1)S(1)} collective-permute-done((bf16[256,2304]{1,0:T(8,128)(2,1)S(1)}, bf16[256,2304]{1,0:T(8,128)(2,1)S(1)}, u32[]{:S(2)}, u32[]{:S(2)}) %collective-permute-start.45) | collective-permute-done | bytes 1179680 | tf_op jit(solution)/shard_map/ppermute | solution.py:326
  680.5 11.7 %collective-permute-done.50 = bf16[1,256,768]{2,1,0:T(8,128)(2,1)} collective-permute-done((bf16[1,256,768]{2,1,0:T(8,128)(2,1)}, bf16[1,256,768]{2,1,0:T(8,128)(2,1)}, u32[]{:S(2)}, u32[]{:S(2)}) %collective-permute-start.50) | collective-permute-done | bytes 393248 | tf_op jit(solution)/shard_map/ppermute | solution.py:294
  707.0 7.4 collective-permute-done.48
  714.3 6.3 add_convert_fusion
  (352 shorter events, 239.5 us)
Async XLA Ops:
  7.2 51.8 %all-gather.6.cloned.1.call-start = ((), (), s32[]{:S(2)}) async-start(), calls=%async_computation.16 | async-start | bytes 2621440 | tf_op jit(solution)/shard_map/all_gather | solution.py:578
  43.0 31.1 %all-to-all-start.2 = ((bf16[8,256,512]{2,1,0:T(8,128)(2,1)}), bf16[8,256,512]{2,1,0:T(8,128)(2,1)}, u32[]{:S(2)}, u32[]{:S(2)}) async-start(bf16[8,256,512]{2,1,0:T(8,128)(2,1)} %bitcast.108), calls=%async_computation.2 | async-start | bytes 4194304 | tf_op jit(solution)/shard_map/all_to_all | solution.py:594
  82.0 176.5 %all-gather.4.cloned.1.call-start = ((), (), s32[]{:S(2)}) async-start(), calls=%async_computation.12 | async-start | bytes 10485760 | tf_op jit(solution)/shard_map/all_gather | solution.py:599
  108.6 540.0 %reduce-scatter.6.cloned.1.call-start = ((), (), s32[]{:S(2)}) async-start(), calls=%async_computation.14 | async-start | bytes 5242880 | tf_op jit(solution)/shard_map/reduce_scatter | solution.py:666
  108.7 35.0 %collective-permute-start = (bf16[512,2048]{1,0:T(8,128)(2,1)}, bf16[512,2048]{1,0:T(8,128)(2,1)}, u32[]{:S(2)}, u32[]{:S(2)}) collective-permute-start(bf16[512,2048]{1,0:T(8,128)(2,1)} %refs_8_.1), channel_id=1, source_target_pairs={{0,8},{12,4},{8,24},{28,12},{24,16},{20,28},{16,0},{4,20},{1,9},{1... | collective-permute-start | bytes 6291464 | tf_op jit(solution)/shard_map/ppermute | solution.py:326
  158.8 44.9 %collective-permute-start.8 = (bf16[512,2048]{1,0:T(8,128)(2,1)}, bf16[512,2048]{1,0:T(8,128)(2,1)}, u32[]{:S(2)}, u32[]{:S(2)}) collective-permute-start(bf16[512,2048]{1,0:T(8,128)(2,1)} %collective-permute-done.refs_2_.refs_10_), channel_id=1, source_target_pairs={{0,8},{12,4},{8,24},{28,12},{24,16},{20,28},{16,0},{4,20},{1,9},{1... | collective-permute-start | bytes 6291464 | tf_op jit(solution)/shard_map/ppermute | solution.py:326
  171.3 32.3 %collective-permute-start.14 = (bf16[256,2048]{1,0:T(8,128)(2,1)S(1)}, bf16[256,2048]{1,0:T(8,128)(2,1)S(1)}, u32[]{:S(2)}, u32[]{:S(2)}) collective-permute-start(bf16[256,2048]{1,0:T(8,128)(2,1)S(1)} %collective-permute-done.12.refs_4_), channel_id=1, source_target_pairs={{0,8},{12,4},{8,24},{28,12},{24,16},{20,28},{16,0},{4,20},{1,9},{1... | collective-permute-start | bytes 3145736 | tf_op jit(solution)/shard_map/ppermute | solution.py:326
  172.5 31.2 %collective-permute-start.9 = (bf16[256,2048]{1,0:T(8,128)(2,1)}, bf16[256,2048]{1,0:T(8,128)(2,1)S(1)}, u32[]{:S(2)}, u32[]{:S(2)}) collective-permute-start(bf16[256,2048]{1,0:T(8,128)(2,1)} %bitcast.73.refs_0_), channel_id=1, source_target_pairs={{0,4},{4,0},{8,12},{12,8},{16,20},{20,16},{24,28},{28,24},{1,5},{5... | collective-permute-start | bytes 3145736 | tf_op jit(solution)/shard_map/ppermute | solution.py:329
  172.5 31.3 %collective-permute-start.11 = (bf16[256,2048]{1,0:T(8,128)(2,1)}, bf16[256,2048]{1,0:T(8,128)(2,1)S(1)}, u32[]{:S(2)}, u32[]{:S(2)}) collective-permute-start(bf16[256,2048]{1,0:T(8,128)(2,1)} %collective-permute-done.10.refs_2_), channel_id=1, source_target_pairs={{0,4},{4,0},{8,12},{12,8},{16,20},{20,16},{24,28},{28,24},{1,5},{5... | collective-permute-start | bytes 3145736 | tf_op jit(solution)/shard_map/ppermute | solution.py:329
  251.6 36.2 %collective-permute-start.17 = (bf16[512,2048]{1,0:T(8,128)(2,1)}, bf16[512,2048]{1,0:T(8,128)(2,1)}, u32[]{:S(2)}, u32[]{:S(2)}) collective-permute-start(bf16[512,2048]{1,0:T(8,128)(2,1)} %collective-permute-done.16.refs_0_.refs_10_), channel_id=1, source_target_pairs={{0,8},{12,4},{8,24},{28,12},{24,16},{20,28},{16,0},{4,20},{1,9},{1... | collective-permute-start | bytes 6291464 | tf_op jit(solution)/shard_map/ppermute | solution.py:326
  254.7 46.9 %collective-permute-start.24 = (bf16[512,2048]{1,0:T(8,128)(2,1)}, bf16[512,2048]{1,0:T(8,128)(2,1)}, u32[]{:S(2)}, u32[]{:S(2)}) collective-permute-start(bf16[512,2048]{1,0:T(8,128)(2,1)} %collective-permute-done.8.refs_2_.refs_12_), channel_id=1, source_target_pairs={{0,8},{12,4},{8,24},{28,12},{24,16},{20,28},{16,0},{4,20},{1,9},{1... | collective-permute-start | bytes 6291464 | tf_op jit(solution)/shard_map/ppermute | solution.py:326
  288.3 41.1 %collective-permute-start.20 = (bf16[512,2048]{1,0:T(8,128)(2,1)}, bf16[512,2048]{1,0:T(8,128)(2,1)}, u32[]{:S(2)}, u32[]{:S(2)}) collective-permute-start(bf16[512,2048]{1,0:T(8,128)(2,1)} %collective-permute-done.17.refs_0_.refs_12_), channel_id=1, source_target_pairs={{0,8},{12,4},{8,24},{28,12},{24,16},{20,28},{16,0},{4,20},{1,9},{1... | collective-permute-start | bytes 6291464 | tf_op jit(solution)/shard_map/ppermute | solution.py:326
  330.0 36.0 %collective-permute-start.31 = (bf16[512,2048]{1,0:T(8,128)(2,1)}, bf16[512,2048]{1,0:T(8,128)(2,1)}, u32[]{:S(2)}, u32[]{:S(2)}) collective-permute-start(bf16[512,2048]{1,0:T(8,128)(2,1)} %get-tuple-element.139), channel_id=1, source_target_pairs={{0,4},{4,0},{8,12},{12,8},{16,20},{20,16},{24,28},{28,24},{1,5},{5... | collective-permute-start | bytes 6291464 | tf_op jit(solution)/shard_map/ppermute | solution.py:329
  334.2 31.8 %collective-permute-start.33 = (bf16[512,2048]{1,0:T(8,128)(2,1)}, bf16[512,2048]{1,0:T(8,128)(2,1)}, u32[]{:S(2)}, u32[]{:S(2)}) collective-permute-start(bf16[512,2048]{1,0:T(8,128)(2,1)} %add_convert_fusion.6), channel_id=1, source_target_pairs={{0,8},{12,4},{8,24},{28,12},{24,16},{20,28},{16,0},{4,20},{1,9},{1... | collective-permute-start | bytes 6291464 | tf_op jit(solution)/shard_map/ppermute | solution.py:326
  365.6 37.8 %collective-permute-start.30 = (bf16[512,2048]{1,0:T(8,128)(2,1)}, bf16[512,2048]{1,0:T(8,128)(2,1)}, u32[]{:S(2)}, u32[]{:S(2)}) collective-permute-start(bf16[512,2048]{1,0:T(8,128)(2,1)} %get-tuple-element.145), channel_id=1, source_target_pairs={{0,4},{4,0},{8,12},{12,8},{16,20},{20,16},{24,28},{28,24},{1,5},{5... | collective-permute-start | bytes 6291464 | tf_op jit(solution)/shard_map/ppermute | solution.py:329
  371.6 31.8 %collective-permute-start.34 = (bf16[512,2048]{1,0:T(8,128)(2,1)}, bf16[512,2048]{1,0:T(8,128)(2,1)}, u32[]{:S(2)}, u32[]{:S(2)}) collective-permute-start(bf16[512,2048]{1,0:T(8,128)(2,1)} %add_convert_fusion.5), channel_id=1, source_target_pairs={{0,8},{12,4},{8,24},{28,12},{24,16},{20,28},{16,0},{4,20},{1,9},{1... | collective-permute-start | bytes 6291464 | tf_op jit(solution)/shard_map/ppermute | solution.py:326
  410.9 48.5 %collective-permute-start.36 = (bf16[512,2048]{1,0:T(8,128)(2,1)}, bf16[512,2048]{1,0:T(8,128)(2,1)}, u32[]{:S(2)}, u32[]{:S(2)}) collective-permute-start(bf16[512,2048]{1,0:T(8,128)(2,1)} %get-tuple-element.184), channel_id=1, source_target_pairs={{0,4},{4,0},{8,12},{12,8},{16,20},{20,16},{24,28},{28,24},{1,5},{5... | collective-permute-start | bytes 6291464 | tf_op jit(solution)/shard_map/ppermute | solution.py:329
  437.5 45.9 %collective-permute-start.37 = (bf16[512,2048]{1,0:T(8,128)(2,1)}, bf16[512,2048]{1,0:T(8,128)(2,1)}, u32[]{:S(2)}, u32[]{:S(2)}) collective-permute-start(bf16[512,2048]{1,0:T(8,128)(2,1)} %get-tuple-element.187), channel_id=1, source_target_pairs={{0,4},{4,0},{8,12},{12,8},{16,20},{20,16},{24,28},{28,24},{1,5},{5... | collective-permute-start | bytes 6291464 | tf_op jit(solution)/shard_map/ppermute | solution.py:329
  463.1 32.8 %collective-permute-start.38 = (bf16[512,2048]{1,0:T(8,128)(2,1)}, bf16[512,2048]{1,0:T(8,128)(2,1)}, u32[]{:S(2)}, u32[]{:S(2)}) collective-permute-start(bf16[512,2048]{1,0:T(8,128)(2,1)} %add_convert_fusion.3), channel_id=1, source_target_pairs={{0,8},{12,4},{8,24},{28,12},{24,16},{20,28},{16,0},{4,20},{1,9},{1... | collective-permute-start | bytes 6291464 | tf_op jit(solution)/shard_map/ppermute | solution.py:326
  463.9 83.7 %collective-permute-start.46 = (bf16[512,2048]{1,0:T(8,128)(2,1)}, bf16[512,2048]{1,0:T(8,128)(2,1)}, u32[]{:S(2)}, u32[]{:S(2)}) collective-permute-start(bf16[512,2048]{1,0:T(8,128)(2,1)} %get-tuple-element.208), channel_id=1, source_target_pairs={{0,4},{4,0},{8,12},{12,8},{16,20},{20,16},{24,28},{28,24},{1,5},{5... | collective-permute-start | bytes 6291464 | tf_op jit(solution)/shard_map/ppermute | solution.py:329
  483.3 50.3 %all-to-all-start.4 = ((bf16[4,512,256]{2,1,0:T(8,128)(2,1)}), bf16[4,512,256]{2,1,0:T(8,128)(2,1)S(1)}, u32[]{:S(2)}, u32[]{:S(2)}) async-start(bf16[4,512,256]{2,1,0:T(8,128)(2,1)} %bitcast.31), calls=%async_computation.4 | async-start | bytes 2097152 | tf_op jit(solution)/shard_map/all_to_all | solution.py:283
  495.8 204.7 %reduce-scatter.4.cloned.1.call-start = ((), (), s32[]{:S(2)}) async-start(), calls=%async_computation.13 | async-start | bytes 5242880 | tf_op jit(solution)/shard_map/reduce_scatter | solution.py:700
  545.9 44.8 %collective-permute-start.47 = (bf16[512,2048]{1,0:T(8,128)(2,1)}, bf16[512,2048]{1,0:T(8,128)(2,1)}, u32[]{:S(2)}, u32[]{:S(2)}) collective-permute-start(bf16[512,2048]{1,0:T(8,128)(2,1)} %add_convert_fusion.2), channel_id=1, source_target_pairs={{0,8},{12,4},{8,24},{28,12},{24,16},{20,28},{16,0},{4,20},{1,9},{1... | collective-permute-start | bytes 6291464 | tf_op jit(solution)/shard_map/ppermute | solution.py:326
  551.6 34.6 %collective-permute-start.43 = (bf16[256,2304]{1,0:T(8,128)(2,1)S(1)}, bf16[256,2304]{1,0:T(8,128)(2,1)S(1)}, u32[]{:S(2)}, u32[]{:S(2)}) collective-permute-start(bf16[256,2304]{1,0:T(8,128)(2,1)S(1)} %add_convert_fusion.10), channel_id=1, source_target_pairs={{0,8},{12,4},{8,24},{28,12},{24,16},{20,28},{16,0},{4,20},{1,9},{1... | collective-permute-start | bytes 3538952 | tf_op jit(solution)/shard_map/ppermute | solution.py:326
  560.8 114.7 %collective-permute-start.52 = (bf16[256,2048]{1,0:T(8,128)(2,1)}, bf16[256,2048]{1,0:T(8,128)(2,1)}, u32[]{:S(2)}, u32[]{:S(2)}) collective-permute-start(bf16[256,2048]{1,0:T(8,128)(2,1)} %get-tuple-element.233), channel_id=1, source_target_pairs={{0,4},{4,0},{8,12},{12,8},{16,20},{20,16},{24,28},{28,24},{1,5},{5... | collective-permute-start | bytes 3145736 | tf_op jit(solution)/shard_map/ppermute | solution.py:329
  566.0 72.7 %collective-permute-start.54 = (bf16[256,2048]{1,0:T(8,128)(2,1)}, bf16[256,2048]{1,0:T(8,128)(2,1)}, u32[]{:S(2)}, u32[]{:S(2)}) collective-permute-start(bf16[256,2048]{1,0:T(8,128)(2,1)} %get-tuple-element.235), channel_id=1, source_target_pairs={{0,4},{4,0},{8,12},{12,8},{16,20},{20,16},{24,28},{28,24},{1,5},{5... | collective-permute-start | bytes 3145736 | tf_op jit(solution)/shard_map/ppermute | solution.py:329
  653.7 40.3 %collective-permute-start.51 = (bf16[1,256,768]{2,1,0:T(8,128)(2,1)}, bf16[1,256,768]{2,1,0:T(8,128)(2,1)S(1)}, u32[]{:S(2)}, u32[]{:S(2)}) collective-permute-start(bf16[1,256,768]{2,1,0:T(8,128)(2,1)} %get-tuple-element.239), channel_id=1, source_target_pairs={{0,3},{1,0},{2,1},{3,2},{4,7},{5,4},{6,5},{7,6},{8,11},{9,8},{10,9... | collective-permute-start | bytes 1179656 | tf_op jit(solution)/shard_map/ppermute | solution.py:294
  657.5 34.7 %collective-permute-start.50 = (bf16[1,256,768]{2,1,0:T(8,128)(2,1)}, bf16[1,256,768]{2,1,0:T(8,128)(2,1)}, u32[]{:S(2)}, u32[]{:S(2)}) collective-permute-start(bf16[1,256,768]{2,1,0:T(8,128)(2,1)} %get-tuple-element.242), channel_id=1, source_target_pairs={{0,2},{1,3},{2,0},{3,1},{4,6},{5,7},{6,4},{7,5},{8,10},{9,11},{10,... | collective-permute-start | bytes 1179656 | tf_op jit(solution)/shard_map/ppermute | solution.py:294
  663.4 33.4 %collective-permute-start.58 = (bf16[256,2048]{1,0:T(8,128)(2,1)}, bf16[256,2048]{1,0:T(8,128)(2,1)}, u32[]{:S(2)}, u32[]{:S(2)}) collective-permute-start(bf16[256,2048]{1,0:T(8,128)(2,1)} %add_convert_fusion.11), channel_id=1, source_target_pairs={{0,8},{12,4},{8,24},{28,12},{24,16},{20,28},{16,0},{4,20},{1,9},{1... | collective-permute-start | bytes 3145736 | tf_op jit(solution)/shard_map/ppermute | solution.py:326
  667.5 66.7 %reduce-scatter.8.cloned.1.call-start = ((), (), s32[]{:S(2)}) async-start(), calls=%async_computation.15 | async-start | bytes 1310720 | tf_op jit(solution)/shard_map/reduce_scatter | solution.py:690
  675.4 31.5 %collective-permute-start.28 = (bf16[512,2048]{1,0:T(8,128)(2,1)}, bf16[512,2048]{1,0:T(8,128)(2,1)}, u32[]{:S(2)}, u32[]{:S(2)}) collective-permute-start(bf16[512,2048]{1,0:T(8,128)(2,1)} %get-tuple-element.151), channel_id=1, source_target_pairs={{0,4},{4,0},{8,12},{12,8},{16,20},{20,16},{24,28},{28,24},{1,5},{5... | collective-permute-start | bytes 6291464 | tf_op jit(solution)/shard_map/ppermute | solution.py:329
  676.8 37.5 %collective-permute-start.48 = (bf16[512,2048]{1,0:T(8,128)(2,1)}, bf16[512,2048]{1,0:T(8,128)(2,1)}, u32[]{:S(2)}, u32[]{:S(2)}) collective-permute-start(bf16[512,2048]{1,0:T(8,128)(2,1)} %add_convert_fusion.1), channel_id=1, source_target_pairs={{0,8},{12,4},{8,24},{28,12},{24,16},{20,28},{16,0},{4,20},{1,9},{1... | collective-permute-start | bytes 6291464 | tf_op jit(solution)/shard_map/ppermute | solution.py:326
  (97 other events, 1267.8 us)
Sparse Core Ops, SparseCore 0:
  10.3 48.6 all-gather.5
  108.8 146.8 all-gather.3
  437.6 84.8 reduce-scatter.5
  547.8 79.0 reduce-scatter.3
  700.6 27.5 reduce-scatter.7

commit v2 on v1

--- a/solution.py
+++ b/solution.py
@@ -717,7 +717,7 @@
         last_sent.append(last_sums.send(first_part))
     layer_out = residual + total(last_sent[-1]) + downbias
     up_grad = lax.all_to_all(after(up_part, first_part), "dp", 1, 0, tiled=True).astype(f32).T
-    grad_first = cols_product(after(grad_queries, first_sent[min(1, chips - 1)]), first_list, owners)
+    grad_first = cols_product(after(grad_queries, first_sent[0]), first_list, owners)
     grad_first = grad_first + dot_nt(grad_pairs, pair_full)
     grad_one, attngain_part, attnshift_part = norm_backward(
         rows, first_mean, first_scale, attngain, grad_first

time: 755 us -> 784 us (1.038)
  starting transfers between devices: 103 us -> 123 us
  waiting for transfers between devices: 192 us -> 211 us
    ppermute x24, starting transfers between devices: 43.7 us -> 57.7 us  [step(): return lax.ppermute(value, 'dp', self.pairs)]
    all_to_all x1, waiting for transfers between devices: 6.68 us -> 19.9 us  [tensor_exchange(): return lax.all_to_all(parts, 'tensor', 0, 0)]
    ppermute x24, waiting for transfers between devices: 115 us -> 104 us  [step(): return lax.ppermute(value, 'dp', self.pairs)]
    ppermute x3, waiting for transfers between devices: 12.7 us -> 21.6 us  [tensor_swaps(): lax.ppermute(part, 'tensor', [(i, (i + s) % size) for i in range(size)])]
    unnamed x129 -> x121, local copies, waits for them, and re-layouts: 27.9 us -> 25.5 us
  transfers between devices with their start and end apart: 72 -> 72, of which waited for: 24 -> 24; matrix products, arithmetic and copies ran while one was open for 19% -> 17% of each run, Pallas kernels for 33% -> 31%
where the time goes in v2:
time: 784 us; the launch traced here: 776 us
  Pallas kernels  242 us (31%)
  waiting for transfers between devices  211 us (27%)
  starting transfers between devices  123 us (16%)
  other arithmetic  87.4 us (11%)
  local copies, waits for them, and re-layouts  60.1 us (8%)
  between operations  25.8 us (3%)
  matrix products  15.3 us (2%)
  blocking collectives  11.7 us (1%)
    pallas_call x4, Pallas kernels, units(): pl.pallas_call(functools.partial(units_kernel, count, piece, tiles), grid...  112 us
    ppermute x24, waiting for transfers between devices, step(): return lax.ppermute(value, 'dp', self.pairs)  104 us
    ppermute x24, starting transfers between devices, step(): return lax.ppermute(value, 'dp', self.pairs)  57.7 us
    pallas_call x2, Pallas kernels, grads_product(): pl.pallas_call(functools.partial(grads_product_kernel, count), grid=(widt...  52.2 us
    convert_element_type x12, other arithmetic, sums(): value = total(shares).astype(bf16)  46.9 us
    all_to_all x3, waiting for transfers between devices, axis_gather(): return lax.all_to_all(copies, axis, 0, 0)  29.7 us
    unnamed x121, local copies, waits for them, and re-layouts  25.5 us
    pallas_call x2, Pallas kernels, cols_product(): pl.pallas_call(functools.partial(cols_product_kernel, depth), grid_spec=p...  22.9 us
  transfers between devices with their start and end apart: 72, of which 24 were waited for; matrix products, arithmetic and copies ran while one was open for 17% of the time, Pallas kernels for 31%

profile of v2, /device:TPU:0, one launch (start us, length us, event | category | flops | bytes accessed | tf_op | source)
XLA Modules:
  0.0 775.8 jit_solution(8633484573406969111)
XLA Ops:
  11.0 11.7 %all_to_all.87 = f32[4,1,768]{2,1,0:T(1,128)S(1)} all-to-all(f32[4,1,768]{2,1,0:T(1,128)S(1)} %broadcast_in_dim.16), channel_id=1, replica_groups=mesh['dp'=8,'tensor'=4] {'tensor'}, dimensions={0} | all-to-all | bytes 24576 | tf_op jit(solution)/shard_map/all_to_all | solution.py:278
  32.9 10.1 %all-to-all-done.1 = bf16[8,256,256]{2,1,0:T(8,128)(2,1)S(1)} async-done(((bf16[8,256,256]{2,1,0:T(8,128)(2,1)}), bf16[8,256,256]{2,1,0:T(8,128)(2,1)S(1)}, u32[]{:S(2)}, u32[]{:S(2)}) %all-to-all-start.1) | async-done | bytes 1048608 | tf_op jit(solution)/shard_map/all_to_all | solution.py:278
  48.1 10.9 %all-gather.6.cloned.1.call-done = bf16[8,256,512]{2,1,0:T(8,128)(2,1)} async-done(((bf16[2,256,512]{2,1,0:T(8,128)(2,1)}), bf16[8,256,512]{2,1,0:T(8,128)(2,1)}) %all-gather.6.cloned.1.call-update) | async-done | bytes 2097168 | tf_op jit(solution)/shard_map/all_gather | solution.py:578
  85.3 19.6 %all-to-all-done.3 = bf16[4,512,256]{2,1,0:T(8,128)(2,1)S(1)} async-done(((bf16[4,512,256]{2,1,0:T(8,128)(2,1)}), bf16[4,512,256]{2,1,0:T(8,128)(2,1)S(1)}, u32[]{:S(2)}, u32[]{:S(2)}) %all-to-all-start.3) | async-done | bytes 1048608 | tf_op jit(solution)/shard_map/all_to_all | solution.py:278
  109.6 11.7 %collective-permute-done.6.refs_6_ = bf16[256,2048]{1,0:T(8,128)(2,1)} collective-permute-done((bf16[256,2048]{1,0:T(8,128)(2,1)}, bf16[256,2048]{1,0:T(8,128)(2,1)}, u32[]{:S(2)}, u32[]{:S(2)}) %collective-permute-start.6) | collective-permute-done | bytes 1048608 | tf_op jit(solution)/shard_map/ppermute | solution.py:326
  143.7 10.1 %rows_product.2.q_ref = bf16[512,2048]{1,0:T(8,128)(2,1)} custom-call(s32[8]{0:T(128)} %stack.52.owner_ref, bf16[512,2048]{1,0:T(8,128)(2,1)} %copy-done.15, f32[1,2048]{1,0:T(1,128)} %bitcast.140, bf16[256,2048]{1,0:T(8,128)(2,1)} %bitcast.70.refs_0_, bf16[256,2048]{1,0:T(8,128)(2,1)} %copy-done.45, bf16[256,2048]{1,0:T(8,128)(2,1)} %collective-permute-done.2.refs_2_, ...), custom_call_target="tpu_custom_call" | custom-call | flops 4294967296 | bytes 8388608 | tf_op jit(solution)/shard_map/rows_product/pallas_call | solution.py:449
  159.3 10.8 %attend_forward.1 = (bf16[512,2048]{1,0:T(8,128)(2,1)}, f32[1,4,1,2048]{3,2,1,0:T(1,128)}) custom-call(s32[3,4]{1,0:T(4,128)} %pad_add_fusion.info_ref, bf16[512,2048]{1,0:T(8,128)(2,1)} %rows_product.2.q_ref, bf16[2048,256]{1,0:T(8,128)(2,1)} %bitcast.105, s32[1,512]{1,0:T(1,128)} %bitcast.137), custom_call_target="tpu_custom_call" | custom-call | tf_op jit(solution)/shard_map/attend_forward/pallas_call | solution.py:220
  173.9 29.8 %collective-permute-done.14.refs_6_ = bf16[256,2048]{1,0:T(8,128)(2,1)S(1)} collective-permute-done((bf16[256,2048]{1,0:T(8,128)(2,1)}, bf16[256,2048]{1,0:T(8,128)(2,1)S(1)}, u32[]{:S(2)}, u32[]{:S(2)}) %collective-permute-start.14) | collective-permute-done | bytes 1048608 | tf_op jit(solution)/shard_map/ppermute | solution.py:326
  206.5 11.4 %cols_product.2 = f32[512,2048]{1,0:T(8,128)} custom-call(s32[8]{0:T(128)} %stack.52.owner_ref, bf16[512,2048]{1,0:T(8,128)(2,1)} %get-tuple-element.127.left_ref.o_ref, bf16[256,2048]{1,0:T(8,128)(2,1)} %bitcast.73.refs_0_, bf16[256,2048]{1,0:T(8,128)(2,1)} %collective-permute-done.9.refs_1_, bf16[256,2048]{1,0:T(8,128)(2,1)} %collective-permute-done.10.refs_2_, ...), custom_call_target="tpu_custom_call" | custom-call | flops 4294967296 | bytes 8388608 | tf_op jit(solution)/shard_map/cols_product/pallas_call | solution.py:525
  227.4 23.7 %collective-permute-done.16.refs_0_.refs_10_ = bf16[512,2048]{1,0:T(8,128)(2,1)} collective-permute-done((bf16[512,2048]{1,0:T(8,128)(2,1)S(1)}, bf16[512,2048]{1,0:T(8,128)(2,1)}, u32[]{:S(2)}, u32[]{:S(2)}) %collective-permute-start.16) | collective-permute-done | bytes 2097184 | tf_op jit(solution)/shard_map/ppermute | solution.py:326
  259.9 28.1 %units.4 = (bf16[512,1024]{1,0:T(8,128)(2,1)}, bf16[512,1024]{1,0:T(8,128)(2,1)}, bf16[512,1024]{1,0:T(8,128)(2,1)}, bf16[512,1024]{1,0:T(8,128)(2,1)}, bf16[512...) custom-call(bf16[512,2048]{1,0:T(8,128)(2,1)} %collective-permute-done.16., ...), custom_call_target="tpu_custom_call" | custom-call | flops 17179869184 | bytes 37748736 | tf_op jit(solution)/shard_map/units/pallas_call | solution.py:414
  288.6 13.0 %collective-permute-start.20 = (bf16[512,2048]{1,0:T(8,128)(2,1)}, bf16[512,2048]{1,0:T(8,128)(2,1)}, u32[]{:S(2)}, u32[]{:S(2)}) collective-permute-start(bf16[512,2048]{1,0:T(8,128)(2,1)} %collective-permute-done.17.refs_0_.refs_12_), channel_id=1, source_target_pairs={{0,8},{12,4},{8,24},{28,12},{24,16},{20,28},{16,0},{4,20},{1,9},{1... | collective-permute-start | bytes 6291464 | tf_op jit(solution)/shard_map/ppermute | solution.py:326
  301.6 28.0 %units.5 = (bf16[512,1024]{1,0:T(8,128)(2,1)}, bf16[512,1024]{1,0:T(8,128)(2,1)}, bf16[512,1024]{1,0:T(8,128)(2,1)}, bf16[512,1024]{1,0:T(8,128)(2,1)}, bf16[512...) custom-call(bf16[512,2048]{1,0:T(8,128)(2,1)} %collective-permute-done.17., ...), custom_call_target="tpu_custom_call" | custom-call | flops 17179869184 | bytes 37748736 | tf_op jit(solution)/shard_map/units/pallas_call | solution.py:414
  337.3 27.9 %units.6 = (bf16[512,1024]{1,0:T(8,128)(2,1)}, bf16[512,1024]{1,0:T(8,128)(2,1)}, bf16[512,1024]{1,0:T(8,128)(2,1)}, bf16[512,1024]{1,0:T(8,128)(2,1)}, bf16[512...) custom-call(bf16[512,2048]{1,0:T(8,128)(2,1)} %collective-permute-done.20., ...), custom_call_target="tpu_custom_call" | custom-call | flops 17179869184 | bytes 37748736 | tf_op jit(solution)/shard_map/units/pallas_call | solution.py:414
  375.6 28.2 %units.7 = (bf16[512,1024]{1,0:T(8,128)(2,1)}, bf16[512,1024]{1,0:T(8,128)(2,1)}, bf16[512,1024]{1,0:T(8,128)(2,1)}, bf16[512,1024]{1,0:T(8,128)(2,1)}, bf16[512...) custom-call(bf16[512,2048]{1,0:T(8,128)(2,1)} %copy-done.21, ...), custom_call_target="tpu_custom_call" | custom-call | flops 17179869184 | bytes 37748736 | tf_op jit(solution)/shard_map/units/pallas_call | solution.py:414
  411.6 26.0 %grads_product.2 = (bf16[1024,2048]{1,0:T(8,128)(2,1)}, f32[1,1024]{1,0:T(1,128)}) custom-call(bf16[512,1024]{1,0:T(8,128)(2,1)} %get-tuple-element.155.refs_0_, bf16[512,1024]{1,0:T(8,128)(2,1)} %get-tuple-element.157.refs_1_, bf16[512,1024]{1,0:T(8,128)(2,1)} %get-tuple-element.159.refs_2_, bf16[512,1024]{1,0:T(8,128)(2,1)} %get-tuple-element.161.refs_3_, ...), custom_call_target="tpu_custom_call" | custom-call | flops 17179869184 | bytes 29360128 | tf_op jit(solution)/shard_map/grads_product/pallas_call | solution.py:491
  437.7 9.4 %norm_backward.1 = (f32[512,2048]{1,0:T(8,128)}, bf16[512,2048]{1,0:T(8,128)(2,1)}, f32[8,2048]{1,0:T(8,128)}) custom-call(bf16[512,2048]{1,0:T(8,128)(2,1)} %get-tuple-element.171.one_ref, bf16[512,2048]{1,0:T(8,128)(2,1)} %collective-permute-done.29.two_ref, bf16[512,2048]{1,0:T(8,128)(2,1)} %collective-permute-done.35.three_ref, f32[512,2048]{1,0:T(8,128)} %copy-done, ...), custom_call_target="tpu_custom_call" | custom-call | tf_op jit(solution)/shard_map/norm_backward/pallas_call | solution.py:78
  447.7 10.0 %rows_product.3.grad_ref = bf16[512,2048]{1,0:T(8,128)(2,1)} custom-call(s32[8]{0:T(128)} %stack.52.owner_ref, bf16[512,2048]{1,0:T(8,128)(2,1)} %get-tuple-element.217.left_ref, f32[1,2048]{1,0:T(1,128)} %reshape.220.shift_ref, bf16[256,2048]{1,0:T(8,128)(2,1)} %bitcast.73.refs_0_, bf16[256,2048]{1,0:T(8,128)(2,1)} %collective-permute-done.9.refs_1_, ...), custom_call_target="tpu_custom_call" | custom-call | flops 4294967296 | bytes 8388608 | tf_op jit(solution)/shard_map/rows_product/pallas_call | solution.py:449
  463.3 14.8 %attend_backward.1 = (bf16[512,2048]{1,0:T(8,128)(2,1)}, f32[2048,256]{1,0:T(8,128)}) custom-call(s32[3,4]{1,0:T(4,128)} %pad_add_fusion.info_ref, bf16[512,2048]{1,0:T(8,128)(2,1)} %rows_product.2.q_ref, bf16[512,2048]{1,0:T(8,128)(2,1)} %rows_product.3.grad_ref, bf16[512,2048]{1,0:T(8,128)(2,1)} %get-tuple-element.127.left_ref.o_ref, ...), custom_call_target="tpu_custom_call" | custom-call | tf_op jit(solution)/shard_map/attend_backward/pallas_call | solution.py:246
  480.8 16.7 %all-to-all-start.4 = ((bf16[4,512,256]{2,1,0:T(8,128)(2,1)}), bf16[4,512,256]{2,1,0:T(8,128)(2,1)S(1)}, u32[]{:S(2)}, u32[]{:S(2)}) async-start(bf16[4,512,256]{2,1,0:T(8,128)(2,1)} %bitcast.31), calls=%async_computation.4 | async-start | bytes 2097152 | tf_op jit(solution)/shard_map/all_to_all | solution.py:283
  503.4 26.1 %grads_product.3 = (bf16[1024,2048]{1,0:T(8,128)(2,1)}, f32[1,1024]{1,0:T(1,128)}) custom-call(bf16[512,1024]{1,0:T(8,128)(2,1)} %get-tuple-element.189.refs_0_, bf16[512,1024]{1,0:T(8,128)(2,1)} %get-tuple-element.191.refs_1_, bf16[512,1024]{1,0:T(8,128)(2,1)} %get-tuple-element.193.refs_2_, bf16[512,1024]{1,0:T(8,128)(2,1)} %get-tuple-element.195.refs_3_, ...), custom_call_target="tpu_custom_call" | custom-call | flops 17179869184 | bytes 29360128 | tf_op jit(solution)/shard_map/grads_product/pallas_call | solution.py:491
  529.5 19.9 %all-to-all-done.4 = bf16[4,512,256]{2,1,0:T(8,128)(2,1)S(1)} async-done(((bf16[4,512,256]{2,1,0:T(8,128)(2,1)}), bf16[4,512,256]{2,1,0:T(8,128)(2,1)S(1)}, u32[]{:S(2)}, u32[]{:S(2)}) %all-to-all-start.4) | async-done | bytes 1048608 | tf_op jit(solution)/shard_map/all_to_all | solution.py:283
  549.7 7.0 convolution_convert_fusion
  599.8 11.4 %cols_product.3 = f32[512,2048]{1,0:T(8,128)} custom-call(s32[8]{0:T(128)} %stack.52.owner_ref, bf16[512,2048]{1,0:T(8,128)(2,1)} %get-tuple-element.211.left_ref, bf16[256,2048]{1,0:T(8,128)(2,1)} %bitcast.70.refs_0_, bf16[256,2048]{1,0:T(8,128)(2,1)} %copy-done.45, bf16[256,2048]{1,0:T(8,128)(2,1)} %collective-permute-done.2.refs_2_, ...), custom_call_target="tpu_custom_call" | custom-call | flops 4294967296 | bytes 8388608 | tf_op jit(solution)/shard_map/cols_product/pallas_call | solution.py:525
  619.5 9.8 %collective-permute-done.44 = bf16[256,2304]{1,0:T(8,128)(2,1)} collective-permute-done((bf16[256,2304]{1,0:T(8,128)(2,1)}, bf16[256,2304]{1,0:T(8,128)(2,1)}, u32[]{:S(2)}, u32[]{:S(2)}) %collective-permute-start.44) | collective-permute-done | bytes 1179680 | tf_op jit(solution)/shard_map/ppermute | solution.py:326
  640.5 15.4 %collective-permute-done.45 = bf16[256,2304]{1,0:T(8,128)(2,1)} collective-permute-done((bf16[256,2304]{1,0:T(8,128)(2,1)}, bf16[256,2304]{1,0:T(8,128)(2,1)}, u32[]{:S(2)}, u32[]{:S(2)}) %collective-permute-start.45) | collective-permute-done | bytes 1179680 | tf_op jit(solution)/shard_map/ppermute | solution.py:326
  682.6 6.5 collective-permute-start.58
  698.6 11.5 %collective-permute-done.49 = bf16[1,256,768]{2,1,0:T(8,128)(2,1)S(1)} collective-permute-done((bf16[1,256,768]{2,1,0:T(8,128)(2,1)S(1)}, bf16[1,256,768]{2,1,0:T(8,128)(2,1)S(1)}, u32[]{:S(2)}, u32[]{:S(2)}) %collective-permute-start.49) | collective-permute-done | bytes 393248 | tf_op jit(solution)/shard_map/ppermute | solution.py:294
  711.2 10.0 %collective-permute-done.50 = bf16[1,256,768]{2,1,0:T(8,128)(2,1)S(1)} collective-permute-done((bf16[1,256,768]{2,1,0:T(8,128)(2,1)S(1)}, bf16[1,256,768]{2,1,0:T(8,128)(2,1)S(1)}, u32[]{:S(2)}, u32[]{:S(2)}) %collective-permute-start.50) | collective-permute-done | bytes 393248 | tf_op jit(solution)/shard_map/ppermute | solution.py:294
  736.5 6.3 add_convert_fusion
  742.8 7.2 all-to-all-done.7
  752.3 7.7 all-to-all-start.8
  (344 shorter events, 259.3 us)
Async XLA Ops:
  7.2 51.8 %all-gather.6.cloned.1.call-start = ((), (), s32[]{:S(2)}) async-start(), calls=%async_computation.16 | async-start | bytes 2621440 | tf_op jit(solution)/shard_map/all_gather | solution.py:578
  43.0 31.1 %all-to-all-start.2 = ((bf16[8,256,512]{2,1,0:T(8,128)(2,1)}), bf16[8,256,512]{2,1,0:T(8,128)(2,1)}, u32[]{:S(2)}, u32[]{:S(2)}) async-start(bf16[8,256,512]{2,1,0:T(8,128)(2,1)} %bitcast.108), calls=%async_computation.2 | async-start | bytes 4194304 | tf_op jit(solution)/shard_map/all_to_all | solution.py:594
  81.9 176.7 %all-gather.4.cloned.1.call-start = ((), (), s32[]{:S(2)}) async-start(), calls=%async_computation.12 | async-start | bytes 10485760 | tf_op jit(solution)/shard_map/all_gather | solution.py:599
  108.6 561.3 %reduce-scatter.6.cloned.1.call-start = ((), (), s32[]{:S(2)}) async-start(), calls=%async_computation.14 | async-start | bytes 5242880 | tf_op jit(solution)/shard_map/reduce_scatter | solution.py:666
  108.7 35.0 %collective-permute-start = (bf16[512,2048]{1,0:T(8,128)(2,1)}, bf16[512,2048]{1,0:T(8,128)(2,1)}, u32[]{:S(2)}, u32[]{:S(2)}) collective-permute-start(bf16[512,2048]{1,0:T(8,128)(2,1)} %refs_8_.1), channel_id=1, source_target_pairs={{0,8},{12,4},{8,24},{28,12},{24,16},{20,28},{16,0},{4,20},{1,9},{1... | collective-permute-start | bytes 6291464 | tf_op jit(solution)/shard_map/ppermute | solution.py:326
  158.7 45.0 %collective-permute-start.8 = (bf16[512,2048]{1,0:T(8,128)(2,1)}, bf16[512,2048]{1,0:T(8,128)(2,1)}, u32[]{:S(2)}, u32[]{:S(2)}) collective-permute-start(bf16[512,2048]{1,0:T(8,128)(2,1)} %collective-permute-done.refs_2_.refs_10_), channel_id=1, source_target_pairs={{0,8},{12,4},{8,24},{28,12},{24,16},{20,28},{16,0},{4,20},{1,9},{1... | collective-permute-start | bytes 6291464 | tf_op jit(solution)/shard_map/ppermute | solution.py:326
  171.1 32.6 %collective-permute-start.14 = (bf16[256,2048]{1,0:T(8,128)(2,1)}, bf16[256,2048]{1,0:T(8,128)(2,1)S(1)}, u32[]{:S(2)}, u32[]{:S(2)}) collective-permute-start(bf16[256,2048]{1,0:T(8,128)(2,1)} %copy-done.49), channel_id=1, source_target_pairs={{0,8},{12,4},{8,24},{28,12},{24,16},{20,28},{16,0},{4,20},{1,9},{1... | collective-permute-start | bytes 3145736 | tf_op jit(solution)/shard_map/ppermute | solution.py:326
  251.6 36.4 %collective-permute-start.17 = (bf16[512,2048]{1,0:T(8,128)(2,1)}, bf16[512,2048]{1,0:T(8,128)(2,1)}, u32[]{:S(2)}, u32[]{:S(2)}) collective-permute-start(bf16[512,2048]{1,0:T(8,128)(2,1)} %collective-permute-done.16.refs_0_.refs_10_), channel_id=1, source_target_pairs={{0,8},{12,4},{8,24},{28,12},{24,16},{20,28},{16,0},{4,20},{1,9},{1... | collective-permute-start | bytes 6291464 | tf_op jit(solution)/shard_map/ppermute | solution.py:326
  254.6 46.9 %collective-permute-start.24 = (bf16[512,2048]{1,0:T(8,128)(2,1)}, bf16[512,2048]{1,0:T(8,128)(2,1)}, u32[]{:S(2)}, u32[]{:S(2)}) collective-permute-start(bf16[512,2048]{1,0:T(8,128)(2,1)} %collective-permute-done.8.refs_2_.refs_12_), channel_id=1, source_target_pairs={{0,8},{12,4},{8,24},{28,12},{24,16},{20,28},{16,0},{4,20},{1,9},{1... | collective-permute-start | bytes 6291464 | tf_op jit(solution)/shard_map/ppermute | solution.py:326
  288.6 41.0 %collective-permute-start.20 = (bf16[512,2048]{1,0:T(8,128)(2,1)}, bf16[512,2048]{1,0:T(8,128)(2,1)}, u32[]{:S(2)}, u32[]{:S(2)}) collective-permute-start(bf16[512,2048]{1,0:T(8,128)(2,1)} %collective-permute-done.17.refs_0_.refs_12_), channel_id=1, source_target_pairs={{0,8},{12,4},{8,24},{28,12},{24,16},{20,28},{16,0},{4,20},{1,9},{1... | collective-permute-start | bytes 6291464 | tf_op jit(solution)/shard_map/ppermute | solution.py:326
  330.2 36.0 %collective-permute-start.31 = (bf16[512,2048]{1,0:T(8,128)(2,1)}, bf16[512,2048]{1,0:T(8,128)(2,1)}, u32[]{:S(2)}, u32[]{:S(2)}) collective-permute-start(bf16[512,2048]{1,0:T(8,128)(2,1)} %get-tuple-element.139), channel_id=1, source_target_pairs={{0,4},{4,0},{8,12},{12,8},{16,20},{20,16},{24,28},{28,24},{1,5},{5... | collective-permute-start | bytes 6291464 | tf_op jit(solution)/shard_map/ppermute | solution.py:329
  334.4 31.8 %collective-permute-start.33 = (bf16[512,2048]{1,0:T(8,128)(2,1)}, bf16[512,2048]{1,0:T(8,128)(2,1)}, u32[]{:S(2)}, u32[]{:S(2)}) collective-permute-start(bf16[512,2048]{1,0:T(8,128)(2,1)} %add_convert_fusion.6), channel_id=1, source_target_pairs={{0,8},{12,4},{8,24},{28,12},{24,16},{20,28},{16,0},{4,20},{1,9},{1... | collective-permute-start | bytes 6291464 | tf_op jit(solution)/shard_map/ppermute | solution.py:326
  365.8 37.9 %collective-permute-start.30 = (bf16[512,2048]{1,0:T(8,128)(2,1)}, bf16[512,2048]{1,0:T(8,128)(2,1)}, u32[]{:S(2)}, u32[]{:S(2)}) collective-permute-start(bf16[512,2048]{1,0:T(8,128)(2,1)} %get-tuple-element.145), channel_id=1, source_target_pairs={{0,4},{4,0},{8,12},{12,8},{16,20},{20,16},{24,28},{28,24},{1,5},{5... | collective-permute-start | bytes 6291464 | tf_op jit(solution)/shard_map/ppermute | solution.py:329
  371.8 32.0 %collective-permute-start.34 = (bf16[512,2048]{1,0:T(8,128)(2,1)}, bf16[512,2048]{1,0:T(8,128)(2,1)}, u32[]{:S(2)}, u32[]{:S(2)}) collective-permute-start(bf16[512,2048]{1,0:T(8,128)(2,1)} %add_convert_fusion.5), channel_id=1, source_target_pairs={{0,8},{12,4},{8,24},{28,12},{24,16},{20,28},{16,0},{4,20},{1,9},{1... | collective-permute-start | bytes 6291464 | tf_op jit(solution)/shard_map/ppermute | solution.py:326
  411.1 46.5 %collective-permute-start.36 = (bf16[512,2048]{1,0:T(8,128)(2,1)}, bf16[512,2048]{1,0:T(8,128)(2,1)S(1)}, u32[]{:S(2)}, u32[]{:S(2)}) collective-permute-start(bf16[512,2048]{1,0:T(8,128)(2,1)} %get-tuple-element.184), channel_id=1, source_target_pairs={{0,4},{4,0},{8,12},{12,8},{16,20},{20,16},{24,28},{28,24},{1,5},{5... | collective-permute-start | bytes 6291464 | tf_op jit(solution)/shard_map/ppermute | solution.py:329
  411.6 69.2 %collective-permute-start.37 = (bf16[512,2048]{1,0:T(8,128)(2,1)}, bf16[512,2048]{1,0:T(8,128)(2,1)}, u32[]{:S(2)}, u32[]{:S(2)}) collective-permute-start(bf16[512,2048]{1,0:T(8,128)(2,1)} %get-tuple-element.187), channel_id=1, source_target_pairs={{0,4},{4,0},{8,12},{12,8},{16,20},{20,16},{24,28},{28,24},{1,5},{5... | collective-permute-start | bytes 6291464 | tf_op jit(solution)/shard_map/ppermute | solution.py:329
  462.0 35.7 %collective-permute-start.38 = (bf16[512,2048]{1,0:T(8,128)(2,1)S(1)}, bf16[512,2048]{1,0:T(8,128)(2,1)}, u32[]{:S(2)}, u32[]{:S(2)}) collective-permute-start(bf16[512,2048]{1,0:T(8,128)(2,1)S(1)} %add_convert_fusion.3), channel_id=1, source_target_pairs={{0,8},{12,4},{8,24},{28,12},{24,16},{20,28},{16,0},{4,20},{1,9},{1... | collective-permute-start | bytes 6291464 | tf_op jit(solution)/shard_map/ppermute | solution.py:326
  462.9 119.6 %collective-permute-start.46 = (bf16[512,2048]{1,0:T(8,128)(2,1)}, bf16[512,2048]{1,0:T(8,128)(2,1)}, u32[]{:S(2)}, u32[]{:S(2)}) collective-permute-start(bf16[512,2048]{1,0:T(8,128)(2,1)} %get-tuple-element.208), channel_id=1, source_target_pairs={{0,4},{4,0},{8,12},{12,8},{16,20},{20,16},{24,28},{28,24},{1,5},{5... | collective-permute-start | bytes 6291464 | tf_op jit(solution)/shard_map/ppermute | solution.py:329
  480.8 68.5 %all-to-all-start.4 = ((bf16[4,512,256]{2,1,0:T(8,128)(2,1)}), bf16[4,512,256]{2,1,0:T(8,128)(2,1)S(1)}, u32[]{:S(2)}, u32[]{:S(2)}) async-start(bf16[4,512,256]{2,1,0:T(8,128)(2,1)} %bitcast.31), calls=%async_computation.4 | async-start | bytes 2097152 | tf_op jit(solution)/shard_map/all_to_all | solution.py:283
  497.6 231.0 %reduce-scatter.4.cloned.1.call-start = ((), (), s32[]{:S(2)}) async-start(), calls=%async_computation.13 | async-start | bytes 5242880 | tf_op jit(solution)/shard_map/reduce_scatter | solution.py:700
  577.8 115.8 %collective-permute-start.47 = (bf16[512,2048]{1,0:T(8,128)(2,1)}, bf16[512,2048]{1,0:T(8,128)(2,1)}, u32[]{:S(2)}, u32[]{:S(2)}) collective-permute-start(bf16[512,2048]{1,0:T(8,128)(2,1)} %add_convert_fusion.2), channel_id=1, source_target_pairs={{0,8},{12,4},{8,24},{28,12},{24,16},{20,28},{16,0},{4,20},{1,9},{1... | collective-permute-start | bytes 6291464 | tf_op jit(solution)/shard_map/ppermute | solution.py:326
  582.5 76.0 %collective-permute-start.54 = (bf16[256,2048]{1,0:T(8,128)(2,1)}, bf16[256,2048]{1,0:T(8,128)(2,1)}, u32[]{:S(2)}, u32[]{:S(2)}) collective-permute-start(bf16[256,2048]{1,0:T(8,128)(2,1)} %get-tuple-element.235), channel_id=1, source_target_pairs={{0,4},{4,0},{8,12},{12,8},{16,20},{20,16},{24,28},{28,24},{1,5},{5... | collective-permute-start | bytes 3145736 | tf_op jit(solution)/shard_map/ppermute | solution.py:329
  586.6 53.4 %collective-permute-start.39 = (bf16[256,2304]{1,0:T(8,128)(2,1)S(1)}, bf16[256,2304]{1,0:T(8,128)(2,1)}, u32[]{:S(2)}, u32[]{:S(2)}) collective-permute-start(bf16[256,2304]{1,0:T(8,128)(2,1)S(1)} %copy-done.22), channel_id=1, source_target_pairs={{0,4},{4,0},{8,12},{12,8},{16,20},{20,16},{24,28},{28,24},{1,5},{5... | collective-permute-start | bytes 3538952 | tf_op jit(solution)/shard_map/ppermute | solution.py:329
  597.7 31.6 %collective-permute-start.44 = (bf16[256,2304]{1,0:T(8,128)(2,1)}, bf16[256,2304]{1,0:T(8,128)(2,1)}, u32[]{:S(2)}, u32[]{:S(2)}) collective-permute-start(bf16[256,2304]{1,0:T(8,128)(2,1)} %add_convert_fusion.9), channel_id=1, source_target_pairs={{0,8},{12,4},{8,24},{28,12},{24,16},{20,28},{16,0},{4,20},{1,9},{1... | collective-permute-start | bytes 3538952 | tf_op jit(solution)/shard_map/ppermute | solution.py:326
  617.1 41.4 %collective-permute-start.56 = (bf16[256,2048]{1,0:T(8,128)(2,1)}, bf16[256,2048]{1,0:T(8,128)(2,1)}, u32[]{:S(2)}, u32[]{:S(2)}) collective-permute-start(bf16[256,2048]{1,0:T(8,128)(2,1)} %add_convert_fusion.13), channel_id=1, source_target_pairs={{0,8},{12,4},{8,24},{28,12},{24,16},{20,28},{16,0},{4,20},{1,9},{1... | collective-permute-start | bytes 3145736 | tf_op jit(solution)/shard_map/ppermute | solution.py:326
  635.9 32.8 %all-to-all-start.5 = ((f32[8,1,15488]{2,1,0:T(1,128)}), f32[8,1,15488]{2,1,0:T(1,128)}, u32[]{:S(2)}, u32[]{:S(2)}) async-start(f32[8,1,15488]{2,1,0:T(1,128)} %broadcast_in_dim.20), calls=%async_computation.5 | async-start | bytes 991232 | tf_op jit(solution)/shard_map/all_to_all | solution.py:278
  640.0 58.6 %collective-permute-start.52 = (bf16[256,2048]{1,0:T(8,128)(2,1)}, bf16[256,2048]{1,0:T(8,128)(2,1)}, u32[]{:S(2)}, u32[]{:S(2)}) collective-permute-start(bf16[256,2048]{1,0:T(8,128)(2,1)} %get-tuple-element.233), channel_id=1, source_target_pairs={{0,4},{4,0},{8,12},{12,8},{16,20},{20,16},{24,28},{28,24},{1,5},{5... | collective-permute-start | bytes 3145736 | tf_op jit(solution)/shard_map/ppermute | solution.py:329
  672.4 50.4 %all-to-all-start.6 = ((bf16[256,8,256]{2,0,1:T(8,128)(2,1)}), bf16[256,8,256]{2,0,1:T(8,128)(2,1)S(1)}, u32[]{:S(2)}, u32[]{:S(2)}) async-start(bf16[256,8,256]{2,0,1:T(8,128)(2,1)} %bitcast.102), calls=%async_computation.8 | async-start | bytes 2097152 | tf_op jit(solution)/shard_map/all_to_all | solution.py:719
  676.2 87.2 %reduce-scatter.8.cloned.1.call-start = ((), (), s32[]{:S(2)}) async-start(), calls=%async_computation.15 | async-start | bytes 1310720 | tf_op jit(solution)/shard_map/reduce_scatter | solution.py:690
  682.6 42.2 %collective-permute-start.58 = (bf16[256,2048]{1,0:T(8,128)(2,1)}, bf16[256,2048]{1,0:T(8,128)(2,1)}, u32[]{:S(2)}, u32[]{:S(2)}) collective-permute-start(bf16[256,2048]{1,0:T(8,128)(2,1)} %add_convert_fusion.11), channel_id=1, source_target_pairs={{0,8},{12,4},{8,24},{28,12},{24,16},{20,28},{16,0},{4,20},{1,9},{1... | collective-permute-start | bytes 3145736 | tf_op jit(solution)/shard_map/ppermute | solution.py:326
  691.3 30.7 %collective-permute-start.51 = (bf16[1,256,768]{2,1,0:T(8,128)(2,1)S(1)}, bf16[1,256,768]{2,1,0:T(8,128)(2,1)S(1)}, u32[]{:S(2)}, u32[]{:S(2)}) collective-permute-start(bf16[1,256,768]{2,1,0:T(8,128)(2,1)S(1)} %get-tuple-element.239), channel_id=1, source_target_pairs={{0,3},{1,0},{2,1},{3,2},{4,7},{5,4},{6,5},{7,6},{8,11},{9,8},{10,9... | collective-permute-start | bytes 1179656 | tf_op jit(solution)/shard_map/ppermute | solution.py:294
  698.6 36.1 %collective-permute-start.28 = (bf16[512,2048]{1,0:T(8,128)(2,1)}, bf16[512,2048]{1,0:T(8,128)(2,1)}, u32[]{:S(2)}, u32[]{:S(2)}) collective-permute-start(bf16[512,2048]{1,0:T(8,128)(2,1)} %get-tuple-element.151), channel_id=1, source_target_pairs={{0,4},{4,0},{8,12},{12,8},{16,20},{20,16},{24,28},{28,24},{1,5},{5... | collective-permute-start | bytes 6291464 | tf_op jit(solution)/shard_map/ppermute | solution.py:329
  (93 other events, 1254.6 us)
Sparse Core Ops, SparseCore 0:
  10.3 48.6 all-gather.5
  108.7 146.8 all-gather.3
  462.8 91.5 reduce-scatter.5
  582.7 74.2 reduce-scatter.3
  728.7 28.6 reduce-scatter.7

commit v3 on v1

--- a/solution.py
+++ b/solution.py
@@ -708,15 +708,7 @@
     grad_qkv = jnp.concatenate([grad_queries, grad_pairs], axis=1)
     first_local = dot_tn(normed_first, grad_qkv).astype(bf16)
     first_sums = depth_sums(first_local)
-    first_sent = [first_sums.send(None) for _ in range(chips)]
-    first_part = total(first_sent[-1])
-    for at in range(1, chips):
-        out_sent.append(out_sums.send(first_part))
-    out_part = total(out_sent[-1])
-    for at in range(len(last_sent), chips):
-        last_sent.append(last_sums.send(first_part))
-    layer_out = residual + total(last_sent[-1]) + downbias
-    up_grad = lax.all_to_all(after(up_part, first_part), "dp", 1, 0, tiled=True).astype(f32).T
+    first_sent = [first_sums.send(None) for _ in range(chips - 1)]
     grad_first = cols_product(after(grad_queries, first_sent[min(1, chips - 1)]), first_list, owners)
     grad_first = grad_first + dot_nt(grad_pairs, pair_full)
     grad_one, attngain_part, attnshift_part = norm_backward(
@@ -739,6 +731,15 @@
     plain = sum(sizes)
     flat = jnp.concatenate(vectors + [upbias_part[0]])
     flat = axis_gather(flat, "dp")
+    first_sent.append(first_sums.send(flat))
+    first_part = total(first_sent[-1])
+    for at in range(1, chips):
+        out_sent.append(out_sums.send(first_part))
+    out_part = total(out_sent[-1])
+    for at in range(len(last_sent), chips):
+        last_sent.append(last_sums.send(first_part))
+    layer_out = residual + total(last_sent[-1]) + downbias
+    up_grad = lax.all_to_all(after(up_part, first_part), "dp", 1, 0, tiled=True).astype(f32).T
     units_flat = flat[:, plain:].reshape(n_dp, n_tensor, hidden_own)
     units_flat = units_flat.transpose(1, 0, 2).reshape(n_tensor, n_dp * hidden_own)
     flat = jnp.broadcast_to(jnp.sum(flat[:, :plain], axis=0), (n_tensor, plain))

time: 755 us -> 761 us (level)
    ppermute x24, waiting for transfers between devices: 115 us -> 94.9 us  [step(): return lax.ppermute(value, 'dp', self.pairs)]
    all_to_all x3, waiting for transfers between devices: 29.7 us -> 40.7 us  [axis_gather(): return lax.all_to_all(copies, axis, 0, 0)]
    ppermute x3, waiting for transfers between devices: 12.7 us -> 20.8 us  [tensor_swaps(): lax.ppermute(part, 'tensor', [(i, (i + s) % size) for i in range(size)])]
  transfers between devices with their start and end apart: 72 -> 72, of which waited for: 24 -> 24; matrix products, arithmetic and copies ran while one was open for 19% -> 18% of each run, Pallas kernels for 33% -> 33%
where the time goes in v3:
time: 761 us; the launch traced here: 751 us
  Pallas kernels  245 us (32%)
  waiting for transfers between devices  197 us (26%)
  starting transfers between devices  103 us (14%)
  other arithmetic  87.7 us (12%)
  local copies, waits for them, and re-layouts  63.8 us (8%)
  between operations  25.6 us (3%)
  matrix products  16.8 us (2%)
  blocking collectives  11.7 us (2%)
    pallas_call x4, Pallas kernels, units(): pl.pallas_call(functools.partial(units_kernel, count, piece, tiles), grid...  112 us
    ppermute x24, waiting for transfers between devices, step(): return lax.ppermute(value, 'dp', self.pairs)  94.9 us
    pallas_call x2, Pallas kernels, grads_product(): pl.pallas_call(functools.partial(grads_product_kernel, count), grid=(widt...  52.2 us
    ppermute x24, starting transfers between devices, step(): return lax.ppermute(value, 'dp', self.pairs)  49.1 us
    convert_element_type x12, other arithmetic, sums(): value = total(shares).astype(bf16)  46.3 us
    all_to_all x3, waiting for transfers between devices, axis_gather(): return lax.all_to_all(copies, axis, 0, 0)  40.7 us
    unnamed x129, local copies, waits for them, and re-layouts  29.4 us
    pallas_call x2, Pallas kernels, cols_product(): pl.pallas_call(functools.partial(cols_product_kernel, depth), grid_spec=p...  22.8 us
  transfers between devices with their start and end apart: 72, of which 24 were waited for; matrix products, arithmetic and copies ran while one was open for 18% of the time, Pallas kernels for 33%

profile of v3, /device:TPU:0, one launch (start us, length us, event | category | flops | bytes accessed | tf_op | source)
XLA Modules:
  0.0 751.3 jit_solution(11646354495740708119)
XLA Ops:
  11.0 11.7 %all_to_all.87 = f32[4,1,768]{2,1,0:T(1,128)S(1)} all-to-all(f32[4,1,768]{2,1,0:T(1,128)S(1)} %broadcast_in_dim.16), channel_id=1, replica_groups=mesh['dp'=8,'tensor'=4] {'tensor'}, dimensions={0} | all-to-all | bytes 24576 | tf_op jit(solution)/shard_map/all_to_all | solution.py:278
  32.9 10.1 %all-to-all-done.1 = bf16[8,256,256]{2,1,0:T(8,128)(2,1)S(1)} async-done(((bf16[8,256,256]{2,1,0:T(8,128)(2,1)}), bf16[8,256,256]{2,1,0:T(8,128)(2,1)S(1)}, u32[]{:S(2)}, u32[]{:S(2)}) %all-to-all-start.1) | async-done | bytes 1048608 | tf_op jit(solution)/shard_map/all_to_all | solution.py:278
  48.1 10.9 %all-gather.6.cloned.1.call-done = bf16[8,256,512]{2,1,0:T(8,128)(2,1)} async-done(((bf16[2,256,512]{2,1,0:T(8,128)(2,1)}), bf16[8,256,512]{2,1,0:T(8,128)(2,1)}) %all-gather.6.cloned.1.call-update) | async-done | bytes 2097168 | tf_op jit(solution)/shard_map/all_gather | solution.py:578
  85.3 19.6 %all-to-all-done.3 = bf16[4,512,256]{2,1,0:T(8,128)(2,1)S(1)} async-done(((bf16[4,512,256]{2,1,0:T(8,128)(2,1)}), bf16[4,512,256]{2,1,0:T(8,128)(2,1)S(1)}, u32[]{:S(2)}, u32[]{:S(2)}) %all-to-all-start.3) | async-done | bytes 1048608 | tf_op jit(solution)/shard_map/all_to_all | solution.py:278
  109.6 11.7 %collective-permute-done.6.refs_6_ = bf16[256,2048]{1,0:T(8,128)(2,1)} collective-permute-done((bf16[256,2048]{1,0:T(8,128)(2,1)}, bf16[256,2048]{1,0:T(8,128)(2,1)}, u32[]{:S(2)}, u32[]{:S(2)}) %collective-permute-start.6) | collective-permute-done | bytes 1048608 | tf_op jit(solution)/shard_map/ppermute | solution.py:326
  143.7 10.1 %rows_product.2.q_ref = bf16[512,2048]{1,0:T(8,128)(2,1)} custom-call(s32[8]{0:T(128)} %stack.52.owner_ref, bf16[512,2048]{1,0:T(8,128)(2,1)} %copy-done.15, f32[1,2048]{1,0:T(1,128)} %bitcast.141, bf16[256,2048]{1,0:T(8,128)(2,1)} %bitcast.70.refs_0_, bf16[256,2048]{1,0:T(8,128)(2,1)} %copy-done.46, bf16[256,2048]{1,0:T(8,128)(2,1)} %collective-permute-done.2.refs_2_, ...), custom_call_target="tpu_custom_call" | custom-call | flops 4294967296 | bytes 8388608 | tf_op jit(solution)/shard_map/rows_product/pallas_call | solution.py:449
  159.3 12.0 %attend_forward.1 = (bf16[512,2048]{1,0:T(8,128)(2,1)}, f32[1,4,1,2048]{3,2,1,0:T(1,128)}) custom-call(s32[3,4]{1,0:T(4,128)} %pad_add_fusion.info_ref, bf16[512,2048]{1,0:T(8,128)(2,1)} %rows_product.2.q_ref, bf16[2048,256]{1,0:T(8,128)(2,1)} %bitcast.105, s32[1,512]{1,0:T(1,128)} %bitcast.138), custom_call_target="tpu_custom_call" | custom-call | tf_op jit(solution)/shard_map/attend_forward/pallas_call | solution.py:220
  173.0 30.7 %collective-permute-done.14.refs_6_ = bf16[256,2048]{1,0:T(8,128)(2,1)S(1)} collective-permute-done((bf16[256,2048]{1,0:T(8,128)(2,1)S(1)}, bf16[256,2048]{1,0:T(8,128)(2,1)S(1)}, u32[]{:S(2)}, u32[]{:S(2)}) %collective-permute-start.14) | collective-permute-done | bytes 1048608 | tf_op jit(solution)/shard_map/ppermute | solution.py:326
  206.5 11.4 %cols_product.2 = f32[512,2048]{1,0:T(8,128)} custom-call(s32[8]{0:T(128)} %stack.52.owner_ref, bf16[512,2048]{1,0:T(8,128)(2,1)} %get-tuple-element.128.left_ref.o_ref, bf16[256,2048]{1,0:T(8,128)(2,1)} %bitcast.73.refs_0_, bf16[256,2048]{1,0:T(8,128)(2,1)} %copy-done.52, bf16[256,2048]{1,0:T(8,128)(2,1)} %collective-permute-done.10.refs_2_, ...), custom_call_target="tpu_custom_call" | custom-call | flops 4294967296 | bytes 8388608 | tf_op jit(solution)/shard_map/cols_product/pallas_call | solution.py:525
  227.4 23.6 %collective-permute-done.16.refs_0_.refs_10_ = bf16[512,2048]{1,0:T(8,128)(2,1)} collective-permute-done((bf16[512,2048]{1,0:T(8,128)(2,1)S(1)}, bf16[512,2048]{1,0:T(8,128)(2,1)}, u32[]{:S(2)}, u32[]{:S(2)}) %collective-permute-start.16) | collective-permute-done | bytes 2097184 | tf_op jit(solution)/shard_map/ppermute | solution.py:326
  259.7 28.1 %units.4 = (bf16[512,1024]{1,0:T(8,128)(2,1)}, bf16[512,1024]{1,0:T(8,128)(2,1)}, bf16[512,1024]{1,0:T(8,128)(2,1)}, bf16[512,1024]{1,0:T(8,128)(2,1)}, bf16[512...) custom-call(bf16[512,2048]{1,0:T(8,128)(2,1)} %collective-permute-done.16., ...), custom_call_target="tpu_custom_call" | custom-call | flops 17179869184 | bytes 37748736 | tf_op jit(solution)/shard_map/units/pallas_call | solution.py:414
  288.4 13.2 %collective-permute-start.20 = (bf16[512,2048]{1,0:T(8,128)(2,1)}, bf16[512,2048]{1,0:T(8,128)(2,1)}, u32[]{:S(2)}, u32[]{:S(2)}) collective-permute-start(bf16[512,2048]{1,0:T(8,128)(2,1)} %collective-permute-done.17.refs_0_.refs_12_), channel_id=1, source_target_pairs={{0,8},{12,4},{8,24},{28,12},{24,16},{20,28},{16,0},{4,20},{1,9},{1... | collective-permute-start | bytes 6291464 | tf_op jit(solution)/shard_map/ppermute | solution.py:326
  301.6 27.9 %units.5 = (bf16[512,1024]{1,0:T(8,128)(2,1)}, bf16[512,1024]{1,0:T(8,128)(2,1)}, bf16[512,1024]{1,0:T(8,128)(2,1)}, bf16[512,1024]{1,0:T(8,128)(2,1)}, bf16[512...) custom-call(bf16[512,2048]{1,0:T(8,128)(2,1)} %collective-permute-done.17., ...), custom_call_target="tpu_custom_call" | custom-call | flops 17179869184 | bytes 37748736 | tf_op jit(solution)/shard_map/units/pallas_call | solution.py:414
  337.2 28.0 %units.6 = (bf16[512,1024]{1,0:T(8,128)(2,1)}, bf16[512,1024]{1,0:T(8,128)(2,1)}, bf16[512,1024]{1,0:T(8,128)(2,1)}, bf16[512,1024]{1,0:T(8,128)(2,1)}, bf16[512...) custom-call(bf16[512,2048]{1,0:T(8,128)(2,1)} %collective-permute-done.20., ...), custom_call_target="tpu_custom_call" | custom-call | flops 17179869184 | bytes 37748736 | tf_op jit(solution)/shard_map/units/pallas_call | solution.py:414
  375.6 28.0 %units.7 = (bf16[512,1024]{1,0:T(8,128)(2,1)}, bf16[512,1024]{1,0:T(8,128)(2,1)}, bf16[512,1024]{1,0:T(8,128)(2,1)}, bf16[512,1024]{1,0:T(8,128)(2,1)}, bf16[512...) custom-call(bf16[512,2048]{1,0:T(8,128)(2,1)} %copy-done.22, ...), custom_call_target="tpu_custom_call" | custom-call | flops 17179869184 | bytes 37748736 | tf_op jit(solution)/shard_map/units/pallas_call | solution.py:414
  411.4 26.0 %grads_product.2 = (bf16[1024,2048]{1,0:T(8,128)(2,1)}, f32[1,1024]{1,0:T(1,128)}) custom-call(bf16[512,1024]{1,0:T(8,128)(2,1)} %get-tuple-element.156.refs_0_, bf16[512,1024]{1,0:T(8,128)(2,1)} %get-tuple-element.158.refs_1_, bf16[512,1024]{1,0:T(8,128)(2,1)} %get-tuple-element.160.refs_2_, bf16[512,1024]{1,0:T(8,128)(2,1)} %get-tuple-element.162.refs_3_, ...), custom_call_target="tpu_custom_call" | custom-call | flops 17179869184 | bytes 29360128 | tf_op jit(solution)/shard_map/grads_product/pallas_call | solution.py:491
  439.0 9.7 %norm_backward.1 = (f32[512,2048]{1,0:T(8,128)}, bf16[512,2048]{1,0:T(8,128)(2,1)}, f32[8,2048]{1,0:T(8,128)}) custom-call(bf16[512,2048]{1,0:T(8,128)(2,1)} %get-tuple-element.172.one_ref, bf16[512,2048]{1,0:T(8,128)(2,1)} %collective-permute-done.29.two_ref, bf16[512,2048]{1,0:T(8,128)(2,1)} %copy-done.23, f32[512,2048]{1,0:T(8,128)} %copy-done, ...), custom_call_target="tpu_custom_call" | custom-call | tf_op jit(solution)/shard_map/norm_backward/pallas_call | solution.py:78
  449.2 10.2 %rows_product.3.grad_ref = bf16[512,2048]{1,0:T(8,128)(2,1)} custom-call(s32[8]{0:T(128)} %stack.52.owner_ref, bf16[512,2048]{1,0:T(8,128)(2,1)} %get-tuple-element.219.left_ref, f32[1,2048]{1,0:T(1,128)} %reshape.220.shift_ref, bf16[256,2048]{1,0:T(8,128)(2,1)} %bitcast.73.refs_0_, bf16[256,2048]{1,0:T(8,128)(2,1)} %copy-done.52, ...), custom_call_target="tpu_custom_call" | custom-call | flops 4294967296 | bytes 8388608 | tf_op jit(solution)/shard_map/rows_product/pallas_call | solution.py:449
  464.0 16.4 %attend_backward.1 = (bf16[512,2048]{1,0:T(8,128)(2,1)}, f32[2048,256]{1,0:T(8,128)}) custom-call(s32[3,4]{1,0:T(4,128)} %pad_add_fusion.info_ref, bf16[512,2048]{1,0:T(8,128)(2,1)} %rows_product.2.q_ref, bf16[512,2048]{1,0:T(8,128)(2,1)} %rows_product.3.grad_ref, bf16[512,2048]{1,0:T(8,128)(2,1)} %get-tuple-element.128.left_ref.o_ref, ...), custom_call_target="tpu_custom_call" | custom-call | tf_op jit(solution)/shard_map/attend_backward/pallas_call | solution.py:246
  483.3 13.4 %all-to-all-start.4 = ((bf16[4,512,256]{2,1,0:T(8,128)(2,1)}), bf16[4,512,256]{2,1,0:T(8,128)(2,1)S(1)}, u32[]{:S(2)}, u32[]{:S(2)}) async-start(bf16[4,512,256]{2,1,0:T(8,128)(2,1)} %bitcast.31), calls=%async_computation.4 | async-start | bytes 2097152 | tf_op jit(solution)/shard_map/all_to_all | solution.py:283
  501.7 26.2 %grads_product.3 = (bf16[1024,2048]{1,0:T(8,128)(2,1)}, f32[1,1024]{1,0:T(1,128)}) custom-call(bf16[512,1024]{1,0:T(8,128)(2,1)} %get-tuple-element.190.refs_0_, bf16[512,1024]{1,0:T(8,128)(2,1)} %get-tuple-element.192.refs_1_, bf16[512,1024]{1,0:T(8,128)(2,1)} %get-tuple-element.194.refs_2_, bf16[512,1024]{1,0:T(8,128)(2,1)} %get-tuple-element.196.refs_3_, ...), custom_call_target="tpu_custom_call" | custom-call | flops 17179869184 | bytes 29360128 | tf_op jit(solution)/shard_map/grads_product/pallas_call | solution.py:491
  527.8 6.2 all-to-all-done.4
  534.3 7.0 convolution_convert_fusion
  552.5 6.4 convolution_convert_fusion.1
  568.9 16.7 %collective-permute-done.42 = bf16[256,2304]{1,0:T(8,128)(2,1)S(1)} collective-permute-done((bf16[256,2304]{1,0:T(8,128)(2,1)S(1)}, bf16[256,2304]{1,0:T(8,128)(2,1)S(1)}, u32[]{:S(2)}, u32[]{:S(2)}) %collective-permute-start.42) | collective-permute-done | bytes 1179680 | tf_op jit(solution)/shard_map/ppermute | solution.py:326
  589.3 11.4 %cols_product.3 = f32[512,2048]{1,0:T(8,128)} custom-call(s32[8]{0:T(128)} %stack.52.owner_ref, bf16[512,2048]{1,0:T(8,128)(2,1)} %get-tuple-element.207.left_ref, bf16[256,2048]{1,0:T(8,128)(2,1)} %bitcast.70.refs_0_, bf16[256,2048]{1,0:T(8,128)(2,1)} %copy-done.46, bf16[256,2048]{1,0:T(8,128)(2,1)} %collective-permute-done.2.refs_2_, ...), custom_call_target="tpu_custom_call" | custom-call | flops 4294967296 | bytes 8388608 | tf_op jit(solution)/shard_map/cols_product/pallas_call | solution.py:525
  621.7 11.0 %all-to-all-done.5 = f32[8,1,15488]{2,1,0:T(1,128)S(1)} async-done(((f32[8,1,15488]{2,1,0:T(1,128)}), f32[8,1,15488]{2,1,0:T(1,128)S(1)}, u32[]{:S(2)}, u32[]{:S(2)}) %all-to-all-start.5) | async-done | bytes 495648 | tf_op jit(solution)/shard_map/all_to_all | solution.py:278
  636.5 7.1 collective-permute-done.56
  675.3 8.7 %collective-permute-done.49 = bf16[1,256,768]{2,1,0:T(8,128)(2,1)S(1)} collective-permute-done((bf16[1,256,768]{2,1,0:T(8,128)(2,1)S(1)}, bf16[1,256,768]{2,1,0:T(8,128)(2,1)S(1)}, u32[]{:S(2)}, u32[]{:S(2)}) %collective-permute-start.49) | collective-permute-done | bytes 393248 | tf_op jit(solution)/shard_map/ppermute | solution.py:294
  687.2 12.0 %collective-permute-done.50 = bf16[1,256,768]{2,1,0:T(8,128)(2,1)S(1)} collective-permute-done((bf16[1,256,768]{2,1,0:T(8,128)(2,1)S(1)}, bf16[1,256,768]{2,1,0:T(8,128)(2,1)S(1)}, u32[]{:S(2)}, u32[]{:S(2)}) %collective-permute-start.50) | collective-permute-done | bytes 393248 | tf_op jit(solution)/shard_map/ppermute | solution.py:294
  713.9 6.3 add_convert_fusion
  720.2 9.0 %all-to-all-done.7 = bf16[256,8,256]{2,0,1:T(8,128)(2,1)S(1)} async-done(((bf16[256,8,256]{2,0,1:T(8,128)(2,1)}), bf16[256,8,256]{2,0,1:T(8,128)(2,1)S(1)}, u32[]{:S(2)}, u32[]{:S(2)}) %all-to-all-start.7) | async-done | bytes 1048608 | tf_op jit(solution)/shard_map/all_to_all | solution.py:757
  (352 shorter events, 245.1 us)
Async XLA Ops:
  7.2 51.8 %all-gather.6.cloned.1.call-start = ((), (), s32[]{:S(2)}) async-start(), calls=%async_computation.16 | async-start | bytes 2621440 | tf_op jit(solution)/shard_map/all_gather | solution.py:578
  82.0 176.5 %all-gather.4.cloned.1.call-start = ((), (), s32[]{:S(2)}) async-start(), calls=%async_computation.12 | async-start | bytes 10485760 | tf_op jit(solution)/shard_map/all_gather | solution.py:599
  108.6 545.1 %reduce-scatter.6.cloned.1.call-start = ((), (), s32[]{:S(2)}) async-start(), calls=%async_computation.14 | async-start | bytes 5242880 | tf_op jit(solution)/shard_map/reduce_scatter | solution.py:666
  108.7 35.0 %collective-permute-start = (bf16[512,2048]{1,0:T(8,128)(2,1)}, bf16[512,2048]{1,0:T(8,128)(2,1)}, u32[]{:S(2)}, u32[]{:S(2)}) collective-permute-start(bf16[512,2048]{1,0:T(8,128)(2,1)} %refs_8_.1), channel_id=1, source_target_pairs={{0,8},{12,4},{8,24},{28,12},{24,16},{20,28},{16,0},{4,20},{1,9},{1... | collective-permute-start | bytes 6291464 | tf_op jit(solution)/shard_map/ppermute | solution.py:326
  158.8 44.9 %collective-permute-start.8 = (bf16[512,2048]{1,0:T(8,128)(2,1)}, bf16[512,2048]{1,0:T(8,128)(2,1)}, u32[]{:S(2)}, u32[]{:S(2)}) collective-permute-start(bf16[512,2048]{1,0:T(8,128)(2,1)} %collective-permute-done.refs_2_.refs_10_), channel_id=1, source_target_pairs={{0,8},{12,4},{8,24},{28,12},{24,16},{20,28},{16,0},{4,20},{1,9},{1... | collective-permute-start | bytes 6291464 | tf_op jit(solution)/shard_map/ppermute | solution.py:326
  171.3 32.3 %collective-permute-start.14 = (bf16[256,2048]{1,0:T(8,128)(2,1)S(1)}, bf16[256,2048]{1,0:T(8,128)(2,1)S(1)}, u32[]{:S(2)}, u32[]{:S(2)}) collective-permute-start(bf16[256,2048]{1,0:T(8,128)(2,1)S(1)} %collective-permute-done.12.refs_4_), channel_id=1, source_target_pairs={{0,8},{12,4},{8,24},{28,12},{24,16},{20,28},{16,0},{4,20},{1,9},{1... | collective-permute-start | bytes 3145736 | tf_op jit(solution)/shard_map/ppermute | solution.py:326
  172.5 31.2 %collective-permute-start.9 = (bf16[256,2048]{1,0:T(8,128)(2,1)}, bf16[256,2048]{1,0:T(8,128)(2,1)S(1)}, u32[]{:S(2)}, u32[]{:S(2)}) collective-permute-start(bf16[256,2048]{1,0:T(8,128)(2,1)} %bitcast.73.refs_0_), channel_id=1, source_target_pairs={{0,4},{4,0},{8,12},{12,8},{16,20},{20,16},{24,28},{28,24},{1,5},{5... | collective-permute-start | bytes 3145736 | tf_op jit(solution)/shard_map/ppermute | solution.py:329
  172.5 31.3 %collective-permute-start.11 = (bf16[256,2048]{1,0:T(8,128)(2,1)}, bf16[256,2048]{1,0:T(8,128)(2,1)S(1)}, u32[]{:S(2)}, u32[]{:S(2)}) collective-permute-start(bf16[256,2048]{1,0:T(8,128)(2,1)} %collective-permute-done.10.refs_2_), channel_id=1, source_target_pairs={{0,4},{4,0},{8,12},{12,8},{16,20},{20,16},{24,28},{28,24},{1,5},{5... | collective-permute-start | bytes 3145736 | tf_op jit(solution)/shard_map/ppermute | solution.py:329
  251.6 36.3 %collective-permute-start.17 = (bf16[512,2048]{1,0:T(8,128)(2,1)}, bf16[512,2048]{1,0:T(8,128)(2,1)}, u32[]{:S(2)}, u32[]{:S(2)}) collective-permute-start(bf16[512,2048]{1,0:T(8,128)(2,1)} %collective-permute-done.16.refs_0_.refs_10_), channel_id=1, source_target_pairs={{0,8},{12,4},{8,24},{28,12},{24,16},{20,28},{16,0},{4,20},{1,9},{1... | collective-permute-start | bytes 6291464 | tf_op jit(solution)/shard_map/ppermute | solution.py:326
  254.7 47.0 %collective-permute-start.24 = (bf16[512,2048]{1,0:T(8,128)(2,1)}, bf16[512,2048]{1,0:T(8,128)(2,1)}, u32[]{:S(2)}, u32[]{:S(2)}) collective-permute-start(bf16[512,2048]{1,0:T(8,128)(2,1)} %collective-permute-done.8.refs_2_.refs_12_), channel_id=1, source_target_pairs={{0,8},{12,4},{8,24},{28,12},{24,16},{20,28},{16,0},{4,20},{1,9},{1... | collective-permute-start | bytes 6291464 | tf_op jit(solution)/shard_map/ppermute | solution.py:326
  288.4 41.1 %collective-permute-start.20 = (bf16[512,2048]{1,0:T(8,128)(2,1)}, bf16[512,2048]{1,0:T(8,128)(2,1)}, u32[]{:S(2)}, u32[]{:S(2)}) collective-permute-start(bf16[512,2048]{1,0:T(8,128)(2,1)} %collective-permute-done.17.refs_0_.refs_12_), channel_id=1, source_target_pairs={{0,8},{12,4},{8,24},{28,12},{24,16},{20,28},{16,0},{4,20},{1,9},{1... | collective-permute-start | bytes 6291464 | tf_op jit(solution)/shard_map/ppermute | solution.py:326
  330.2 36.0 %collective-permute-start.31 = (bf16[512,2048]{1,0:T(8,128)(2,1)}, bf16[512,2048]{1,0:T(8,128)(2,1)}, u32[]{:S(2)}, u32[]{:S(2)}) collective-permute-start(bf16[512,2048]{1,0:T(8,128)(2,1)} %get-tuple-element.140), channel_id=1, source_target_pairs={{0,4},{4,0},{8,12},{12,8},{16,20},{20,16},{24,28},{28,24},{1,5},{5... | collective-permute-start | bytes 6291464 | tf_op jit(solution)/shard_map/ppermute | solution.py:329
  334.3 31.8 %collective-permute-start.33 = (bf16[512,2048]{1,0:T(8,128)(2,1)}, bf16[512,2048]{1,0:T(8,128)(2,1)}, u32[]{:S(2)}, u32[]{:S(2)}) collective-permute-start(bf16[512,2048]{1,0:T(8,128)(2,1)} %add_convert_fusion.6), channel_id=1, source_target_pairs={{0,8},{12,4},{8,24},{28,12},{24,16},{20,28},{16,0},{4,20},{1,9},{1... | collective-permute-start | bytes 6291464 | tf_op jit(solution)/shard_map/ppermute | solution.py:326
  365.8 37.8 %collective-permute-start.30 = (bf16[512,2048]{1,0:T(8,128)(2,1)}, bf16[512,2048]{1,0:T(8,128)(2,1)}, u32[]{:S(2)}, u32[]{:S(2)}) collective-permute-start(bf16[512,2048]{1,0:T(8,128)(2,1)} %get-tuple-element.146), channel_id=1, source_target_pairs={{0,4},{4,0},{8,12},{12,8},{16,20},{20,16},{24,28},{28,24},{1,5},{5... | collective-permute-start | bytes 6291464 | tf_op jit(solution)/shard_map/ppermute | solution.py:329
  371.8 31.8 %collective-permute-start.34 = (bf16[512,2048]{1,0:T(8,128)(2,1)}, bf16[512,2048]{1,0:T(8,128)(2,1)}, u32[]{:S(2)}, u32[]{:S(2)}) collective-permute-start(bf16[512,2048]{1,0:T(8,128)(2,1)} %add_convert_fusion.5), channel_id=1, source_target_pairs={{0,8},{12,4},{8,24},{28,12},{24,16},{20,28},{16,0},{4,20},{1,9},{1... | collective-permute-start | bytes 6291464 | tf_op jit(solution)/shard_map/ppermute | solution.py:326
  410.9 48.5 %collective-permute-start.36 = (bf16[512,2048]{1,0:T(8,128)(2,1)}, bf16[512,2048]{1,0:T(8,128)(2,1)}, u32[]{:S(2)}, u32[]{:S(2)}) collective-permute-start(bf16[512,2048]{1,0:T(8,128)(2,1)} %get-tuple-element.185), channel_id=1, source_target_pairs={{0,4},{4,0},{8,12},{12,8},{16,20},{20,16},{24,28},{28,24},{1,5},{5... | collective-permute-start | bytes 6291464 | tf_op jit(solution)/shard_map/ppermute | solution.py:329
  437.5 45.8 %collective-permute-start.37 = (bf16[512,2048]{1,0:T(8,128)(2,1)}, bf16[512,2048]{1,0:T(8,128)(2,1)}, u32[]{:S(2)}, u32[]{:S(2)}) collective-permute-start(bf16[512,2048]{1,0:T(8,128)(2,1)} %get-tuple-element.188), channel_id=1, source_target_pairs={{0,4},{4,0},{8,12},{12,8},{16,20},{20,16},{24,28},{28,24},{1,5},{5... | collective-permute-start | bytes 6291464 | tf_op jit(solution)/shard_map/ppermute | solution.py:329
  463.2 33.7 %collective-permute-start.38 = (bf16[512,2048]{1,0:T(8,128)(2,1)}, bf16[512,2048]{1,0:T(8,128)(2,1)}, u32[]{:S(2)}, u32[]{:S(2)}) collective-permute-start(bf16[512,2048]{1,0:T(8,128)(2,1)} %add_convert_fusion.3), channel_id=1, source_target_pairs={{0,8},{12,4},{8,24},{28,12},{24,16},{20,28},{16,0},{4,20},{1,9},{1... | collective-permute-start | bytes 6291464 | tf_op jit(solution)/shard_map/ppermute | solution.py:326
  483.3 50.7 %all-to-all-start.4 = ((bf16[4,512,256]{2,1,0:T(8,128)(2,1)}), bf16[4,512,256]{2,1,0:T(8,128)(2,1)S(1)}, u32[]{:S(2)}, u32[]{:S(2)}) async-start(bf16[4,512,256]{2,1,0:T(8,128)(2,1)} %bitcast.31), calls=%async_computation.4 | async-start | bytes 2097152 | tf_op jit(solution)/shard_map/all_to_all | solution.py:283
  496.7 210.7 %reduce-scatter.4.cloned.1.call-start = ((), (), s32[]{:S(2)}) async-start(), calls=%async_computation.13 | async-start | bytes 5242880 | tf_op jit(solution)/shard_map/reduce_scatter | solution.py:700
  546.1 73.9 %collective-permute-start.46 = (bf16[512,2048]{1,0:T(8,128)(2,1)}, bf16[512,2048]{1,0:T(8,128)(2,1)}, u32[]{:S(2)}, u32[]{:S(2)}) collective-permute-start(bf16[512,2048]{1,0:T(8,128)(2,1)} %get-tuple-element.213), channel_id=1, source_target_pairs={{0,4},{4,0},{8,12},{12,8},{16,20},{20,16},{24,28},{28,24},{1,5},{5... | collective-permute-start | bytes 6291464 | tf_op jit(solution)/shard_map/ppermute | solution.py:329
  546.6 102.2 %collective-permute-start.47 = (bf16[512,2048]{1,0:T(8,128)(2,1)}, bf16[512,2048]{1,0:T(8,128)(2,1)}, u32[]{:S(2)}, u32[]{:S(2)}) collective-permute-start(bf16[512,2048]{1,0:T(8,128)(2,1)} %add_convert_fusion.2), channel_id=1, source_target_pairs={{0,8},{12,4},{8,24},{28,12},{24,16},{20,28},{16,0},{4,20},{1,9},{1... | collective-permute-start | bytes 6291464 | tf_op jit(solution)/shard_map/ppermute | solution.py:326
  551.2 34.4 %collective-permute-start.42 = (bf16[256,2304]{1,0:T(8,128)(2,1)S(1)}, bf16[256,2304]{1,0:T(8,128)(2,1)S(1)}, u32[]{:S(2)}, u32[]{:S(2)}) collective-permute-start(bf16[256,2304]{1,0:T(8,128)(2,1)S(1)} %add_convert_fusion.10), channel_id=1, source_target_pairs={{0,8},{12,4},{8,24},{28,12},{24,16},{20,28},{16,0},{4,20},{1,9},{1... | collective-permute-start | bytes 3538952 | tf_op jit(solution)/shard_map/ppermute | solution.py:326
  563.7 53.0 %collective-permute-start.55 = (bf16[256,2048]{1,0:T(8,128)(2,1)}, bf16[256,2048]{1,0:T(8,128)(2,1)}, u32[]{:S(2)}, u32[]{:S(2)}) collective-permute-start(bf16[256,2048]{1,0:T(8,128)(2,1)} %get-tuple-element.236), channel_id=1, source_target_pairs={{0,4},{4,0},{8,12},{12,8},{16,20},{20,16},{24,28},{28,24},{1,5},{5... | collective-permute-start | bytes 3145736 | tf_op jit(solution)/shard_map/ppermute | solution.py:329
  568.1 38.5 %collective-permute-start.43 = (bf16[256,2304]{1,0:T(8,128)(2,1)S(1)}, bf16[256,2304]{1,0:T(8,128)(2,1)}, u32[]{:S(2)}, u32[]{:S(2)}) collective-permute-start(bf16[256,2304]{1,0:T(8,128)(2,1)S(1)} %get-tuple-element.232), channel_id=1, source_target_pairs={{0,4},{4,0},{8,12},{12,8},{16,20},{20,16},{24,28},{28,24},{1,5},{5... | collective-permute-start | bytes 3538952 | tf_op jit(solution)/shard_map/ppermute | solution.py:329
  633.5 41.7 %collective-permute-start.52 = (bf16[256,2048]{1,0:T(8,128)(2,1)}, bf16[256,2048]{1,0:T(8,128)(2,1)}, u32[]{:S(2)}, u32[]{:S(2)}) collective-permute-start(bf16[256,2048]{1,0:T(8,128)(2,1)} %get-tuple-element.235), channel_id=1, source_target_pairs={{0,4},{4,0},{8,12},{12,8},{16,20},{20,16},{24,28},{28,24},{1,5},{5... | collective-permute-start | bytes 3145736 | tf_op jit(solution)/shard_map/ppermute | solution.py:329
  656.1 44.7 %all-to-all-start.6 = ((bf16[256,8,256]{2,0,1:T(8,128)(2,1)}), bf16[256,8,256]{2,0,1:T(8,128)(2,1)}, u32[]{:S(2)}, u32[]{:S(2)}) async-start(bf16[256,8,256]{2,0,1:T(8,128)(2,1)} %bitcast.112), calls=%async_computation.8 | async-start | bytes 2097152 | tf_op jit(solution)/shard_map/all_to_all | solution.py:742
  660.5 78.3 %reduce-scatter.8.cloned.1.call-start = ((), (), s32[]{:S(2)}) async-start(), calls=%async_computation.15 | async-start | bytes 1310720 | tf_op jit(solution)/shard_map/reduce_scatter | solution.py:690
  662.8 37.2 %collective-permute-start.51 = (bf16[1,256,768]{2,1,0:T(8,128)(2,1)S(1)}, bf16[1,256,768]{2,1,0:T(8,128)(2,1)S(1)}, u32[]{:S(2)}, u32[]{:S(2)}) collective-permute-start(bf16[1,256,768]{2,1,0:T(8,128)(2,1)S(1)} %get-tuple-element.241), channel_id=1, source_target_pairs={{0,3},{1,0},{2,1},{3,2},{4,7},{5,4},{6,5},{7,6},{8,11},{9,8},{10,9... | collective-permute-start | bytes 1179656 | tf_op jit(solution)/shard_map/ppermute | solution.py:294
  665.0 34.2 %collective-permute-start.50 = (bf16[1,256,768]{2,1,0:T(8,128)(2,1)S(1)}, bf16[1,256,768]{2,1,0:T(8,128)(2,1)S(1)}, u32[]{:S(2)}, u32[]{:S(2)}) collective-permute-start(bf16[1,256,768]{2,1,0:T(8,128)(2,1)S(1)} %get-tuple-element.244), channel_id=1, source_target_pairs={{0,2},{1,3},{2,0},{3,1},{4,6},{5,7},{6,4},{7,5},{8,10},{9,11},{10,... | collective-permute-start | bytes 1179656 | tf_op jit(solution)/shard_map/ppermute | solution.py:294
  669.7 34.3 %collective-permute-start.58 = (bf16[256,2048]{1,0:T(8,128)(2,1)}, bf16[256,2048]{1,0:T(8,128)(2,1)S(1)}, u32[]{:S(2)}, u32[]{:S(2)}) collective-permute-start(bf16[256,2048]{1,0:T(8,128)(2,1)} %add_convert_fusion.11), channel_id=1, source_target_pairs={{0,8},{12,4},{8,24},{28,12},{24,16},{20,28},{16,0},{4,20},{1,9},{1... | collective-permute-start | bytes 3145736 | tf_op jit(solution)/shard_map/ppermute | solution.py:326
  675.2 38.6 %collective-permute-start.28 = (bf16[512,2048]{1,0:T(8,128)(2,1)}, bf16[512,2048]{1,0:T(8,128)(2,1)}, u32[]{:S(2)}, u32[]{:S(2)}) collective-permute-start(bf16[512,2048]{1,0:T(8,128)(2,1)} %get-tuple-element.152), channel_id=1, source_target_pairs={{0,4},{4,0},{8,12},{12,8},{16,20},{20,16},{24,28},{28,24},{1,5},{5... | collective-permute-start | bytes 6291464 | tf_op jit(solution)/shard_map/ppermute | solution.py:329
  (97 other events, 1268.6 us)
Sparse Core Ops, SparseCore 0:
  10.3 48.6 all-gather.5
  108.8 146.8 all-gather.3
  437.6 85.0 reduce-scatter.5
  547.8 77.8 reduce-scatter.3
  707.5 27.5 reduce-scatter.7

commit v4 on v1

--- a/solution.py
+++ b/solution.py
@@ -716,7 +716,7 @@
     for at in range(len(last_sent), chips):
         last_sent.append(last_sums.send(first_part))
     layer_out = residual + total(last_sent[-1]) + downbias
-    up_grad = lax.all_to_all(after(up_part, first_part), "dp", 1, 0, tiled=True).astype(f32).T
+    up_grad = lax.all_to_all(after(up_part, first_sent[-2]), "dp", 1, 0, tiled=True).astype(f32).T
     grad_first = cols_product(after(grad_queries, first_sent[min(1, chips - 1)]), first_list, owners)
     grad_first = grad_first + dot_nt(grad_pairs, pair_full)
     grad_one, attngain_part, attnshift_part = norm_backward(

time: 755 us -> 757 us (level)
  transfers between devices with their start and end apart: 72 -> 72, of which waited for: 24 -> 23; matrix products, arithmetic and copies ran while one was open for 19% -> 19% of each run, Pallas kernels for 33% -> 32%
where the time goes in v4:
time: 757 us; the launch traced here: 747 us
  Pallas kernels  242 us (32%)
  waiting for transfers between devices  189 us (25%)
  starting transfers between devices  107 us (14%)
  other arithmetic  87.9 us (12%)
  local copies, waits for them, and re-layouts  66.6 us (9%)
  between operations  25.6 us (3%)
  matrix products  16.8 us (2%)
  blocking collectives  11.7 us (2%)
    ppermute x24, waiting for transfers between devices, step(): return lax.ppermute(value, 'dp', self.pairs)  112 us
    pallas_call x4, Pallas kernels, units(): pl.pallas_call(functools.partial(units_kernel, count, piece, tiles), grid...  112 us
    pallas_call x2, Pallas kernels, grads_product(): pl.pallas_call(functools.partial(grads_product_kernel, count), grid=(widt...  52.2 us
    ppermute x24, starting transfers between devices, step(): return lax.ppermute(value, 'dp', self.pairs)  50.5 us
    convert_element_type x12, other arithmetic, sums(): value = total(shares).astype(bf16)  43.7 us
    all_to_all x3, waiting for transfers between devices, axis_gather(): return lax.all_to_all(copies, axis, 0, 0)  29.7 us
    unnamed x129, local copies, waits for them, and re-layouts  29 us
    pallas_call x2, Pallas kernels, cols_product(): pl.pallas_call(functools.partial(cols_product_kernel, depth), grid_spec=p...  22.8 us
  transfers between devices with their start and end apart: 72, of which 23 were waited for; matrix products, arithmetic and copies ran while one was open for 19% of the time, Pallas kernels for 32%

profile of v4, /device:TPU:0, one launch (start us, length us, event | category | flops | bytes accessed | tf_op | source)
XLA Modules:
  0.0 747.1 jit_solution(13877335625785792868)
XLA Ops:
  11.0 11.7 %all_to_all.87 = f32[4,1,768]{2,1,0:T(1,128)S(1)} all-to-all(f32[4,1,768]{2,1,0:T(1,128)S(1)} %broadcast_in_dim.16), channel_id=1, replica_groups=mesh['dp'=8,'tensor'=4] {'tensor'}, dimensions={0} | all-to-all | bytes 24576 | tf_op jit(solution)/shard_map/all_to_all | solution.py:278
  32.9 10.1 %all-to-all-done.1 = bf16[8,256,256]{2,1,0:T(8,128)(2,1)S(1)} async-done(((bf16[8,256,256]{2,1,0:T(8,128)(2,1)}), bf16[8,256,256]{2,1,0:T(8,128)(2,1)S(1)}, u32[]{:S(2)}, u32[]{:S(2)}) %all-to-all-start.1) | async-done | bytes 1048608 | tf_op jit(solution)/shard_map/all_to_all | solution.py:278
  48.1 10.9 %all-gather.6.cloned.1.call-done = bf16[8,256,512]{2,1,0:T(8,128)(2,1)} async-done(((bf16[2,256,512]{2,1,0:T(8,128)(2,1)}), bf16[8,256,512]{2,1,0:T(8,128)(2,1)}) %all-gather.6.cloned.1.call-update) | async-done | bytes 2097168 | tf_op jit(solution)/shard_map/all_gather | solution.py:578
  85.3 19.6 %all-to-all-done.3 = bf16[4,512,256]{2,1,0:T(8,128)(2,1)S(1)} async-done(((bf16[4,512,256]{2,1,0:T(8,128)(2,1)}), bf16[4,512,256]{2,1,0:T(8,128)(2,1)S(1)}, u32[]{:S(2)}, u32[]{:S(2)}) %all-to-all-start.3) | async-done | bytes 1048608 | tf_op jit(solution)/shard_map/all_to_all | solution.py:278
  109.6 11.7 %collective-permute-done.6.refs_6_ = bf16[256,2048]{1,0:T(8,128)(2,1)} collective-permute-done((bf16[256,2048]{1,0:T(8,128)(2,1)}, bf16[256,2048]{1,0:T(8,128)(2,1)}, u32[]{:S(2)}, u32[]{:S(2)}) %collective-permute-start.6) | collective-permute-done | bytes 1048608 | tf_op jit(solution)/shard_map/ppermute | solution.py:326
  143.7 10.1 %rows_product.2.q_ref = bf16[512,2048]{1,0:T(8,128)(2,1)} custom-call(s32[8]{0:T(128)} %stack.52.owner_ref, bf16[512,2048]{1,0:T(8,128)(2,1)} %copy-done.13, f32[1,2048]{1,0:T(1,128)} %bitcast.141, bf16[256,2048]{1,0:T(8,128)(2,1)} %bitcast.70.refs_0_, bf16[256,2048]{1,0:T(8,128)(2,1)} %copy-done.46, bf16[256,2048]{1,0:T(8,128)(2,1)} %collective-permute-done.2.refs_2_, ...), custom_call_target="tpu_custom_call" | custom-call | flops 4294967296 | bytes 8388608 | tf_op jit(solution)/shard_map/rows_product/pallas_call | solution.py:449
  159.3 10.8 %attend_forward.1 = (bf16[512,2048]{1,0:T(8,128)(2,1)}, f32[1,4,1,2048]{3,2,1,0:T(1,128)}) custom-call(s32[3,4]{1,0:T(4,128)} %pad_add_fusion.info_ref, bf16[512,2048]{1,0:T(8,128)(2,1)} %rows_product.2.q_ref, bf16[2048,256]{1,0:T(8,128)(2,1)} %bitcast.105, s32[1,512]{1,0:T(1,128)} %bitcast.138), custom_call_target="tpu_custom_call" | custom-call | tf_op jit(solution)/shard_map/attend_forward/pallas_call | solution.py:220
  173.0 30.7 %collective-permute-done.14.refs_6_ = bf16[256,2048]{1,0:T(8,128)(2,1)S(1)} collective-permute-done((bf16[256,2048]{1,0:T(8,128)(2,1)S(1)}, bf16[256,2048]{1,0:T(8,128)(2,1)S(1)}, u32[]{:S(2)}, u32[]{:S(2)}) %collective-permute-start.14) | collective-permute-done | bytes 1048608 | tf_op jit(solution)/shard_map/ppermute | solution.py:326
  206.5 11.5 %cols_product.2 = f32[512,2048]{1,0:T(8,128)} custom-call(s32[8]{0:T(128)} %stack.52.owner_ref, bf16[512,2048]{1,0:T(8,128)(2,1)} %get-tuple-element.127.left_ref.o_ref, bf16[256,2048]{1,0:T(8,128)(2,1)} %bitcast.73.refs_0_, bf16[256,2048]{1,0:T(8,128)(2,1)} %copy-done.52, bf16[256,2048]{1,0:T(8,128)(2,1)} %collective-permute-done.10.refs_2_, ...), custom_call_target="tpu_custom_call" | custom-call | flops 4294967296 | bytes 8388608 | tf_op jit(solution)/shard_map/cols_product/pallas_call | solution.py:525
  227.4 23.7 %collective-permute-done.16.refs_0_.refs_10_ = bf16[512,2048]{1,0:T(8,128)(2,1)} collective-permute-done((bf16[512,2048]{1,0:T(8,128)(2,1)S(1)}, bf16[512,2048]{1,0:T(8,128)(2,1)}, u32[]{:S(2)}, u32[]{:S(2)}) %collective-permute-start.16) | collective-permute-done | bytes 2097184 | tf_op jit(solution)/shard_map/ppermute | solution.py:326
  259.8 28.0 %units.4 = (bf16[512,1024]{1,0:T(8,128)(2,1)}, bf16[512,1024]{1,0:T(8,128)(2,1)}, bf16[512,1024]{1,0:T(8,128)(2,1)}, bf16[512,1024]{1,0:T(8,128)(2,1)}, bf16[512...) custom-call(bf16[512,2048]{1,0:T(8,128)(2,1)} %collective-permute-done.16., ...), custom_call_target="tpu_custom_call" | custom-call | flops 17179869184 | bytes 37748736 | tf_op jit(solution)/shard_map/units/pallas_call | solution.py:414
  288.4 13.1 %collective-permute-start.20 = (bf16[512,2048]{1,0:T(8,128)(2,1)}, bf16[512,2048]{1,0:T(8,128)(2,1)}, u32[]{:S(2)}, u32[]{:S(2)}) collective-permute-start(bf16[512,2048]{1,0:T(8,128)(2,1)} %collective-permute-done.17.refs_0_.refs_12_), channel_id=1, source_target_pairs={{0,8},{12,4},{8,24},{28,12},{24,16},{20,28},{16,0},{4,20},{1,9},{1... | collective-permute-start | bytes 6291464 | tf_op jit(solution)/shard_map/ppermute | solution.py:326
  301.5 27.9 %units.5 = (bf16[512,1024]{1,0:T(8,128)(2,1)}, bf16[512,1024]{1,0:T(8,128)(2,1)}, bf16[512,1024]{1,0:T(8,128)(2,1)}, bf16[512,1024]{1,0:T(8,128)(2,1)}, bf16[512...) custom-call(bf16[512,2048]{1,0:T(8,128)(2,1)} %collective-permute-done.17., ...), custom_call_target="tpu_custom_call" | custom-call | flops 17179869184 | bytes 37748736 | tf_op jit(solution)/shard_map/units/pallas_call | solution.py:414
  337.1 27.9 %units.6 = (bf16[512,1024]{1,0:T(8,128)(2,1)}, bf16[512,1024]{1,0:T(8,128)(2,1)}, bf16[512,1024]{1,0:T(8,128)(2,1)}, bf16[512,1024]{1,0:T(8,128)(2,1)}, bf16[512...) custom-call(bf16[512,2048]{1,0:T(8,128)(2,1)} %collective-permute-done.20., ...), custom_call_target="tpu_custom_call" | custom-call | flops 17179869184 | bytes 37748736 | tf_op jit(solution)/shard_map/units/pallas_call | solution.py:414
  366.0 5.6 add_convert_fusion.5
  375.4 28.0 %units.7 = (bf16[512,1024]{1,0:T(8,128)(2,1)}, bf16[512,1024]{1,0:T(8,128)(2,1)}, bf16[512,1024]{1,0:T(8,128)(2,1)}, bf16[512,1024]{1,0:T(8,128)(2,1)}, bf16[512...) custom-call(bf16[512,2048]{1,0:T(8,128)(2,1)} %copy-done.20, ...), custom_call_target="tpu_custom_call" | custom-call | flops 17179869184 | bytes 37748736 | tf_op jit(solution)/shard_map/units/pallas_call | solution.py:414
  403.5 5.7 add_convert_fusion.4
  411.4 26.0 %grads_product.2 = (bf16[1024,2048]{1,0:T(8,128)(2,1)}, f32[1,1024]{1,0:T(1,128)}) custom-call(bf16[512,1024]{1,0:T(8,128)(2,1)} %get-tuple-element.155.refs_0_, bf16[512,1024]{1,0:T(8,128)(2,1)} %get-tuple-element.157.refs_1_, bf16[512,1024]{1,0:T(8,128)(2,1)} %get-tuple-element.159.refs_2_, bf16[512,1024]{1,0:T(8,128)(2,1)} %get-tuple-element.161.refs_3_, ...), custom_call_target="tpu_custom_call" | custom-call | flops 17179869184 | bytes 29360128 | tf_op jit(solution)/shard_map/grads_product/pallas_call | solution.py:491
  439.0 9.6 %norm_backward.1 = (f32[512,2048]{1,0:T(8,128)}, bf16[512,2048]{1,0:T(8,128)(2,1)}, f32[8,2048]{1,0:T(8,128)}) custom-call(bf16[512,2048]{1,0:T(8,128)(2,1)} %get-tuple-element.171.one_ref, bf16[512,2048]{1,0:T(8,128)(2,1)} %collective-permute-done.29.two_ref, bf16[512,2048]{1,0:T(8,128)(2,1)} %copy-done.21, f32[512,2048]{1,0:T(8,128)} %copy-done, ...), custom_call_target="tpu_custom_call" | custom-call | tf_op jit(solution)/shard_map/norm_backward/pallas_call | solution.py:78
  449.2 10.2 %rows_product.3.grad_ref = bf16[512,2048]{1,0:T(8,128)(2,1)} custom-call(s32[8]{0:T(128)} %stack.52.owner_ref, bf16[512,2048]{1,0:T(8,128)(2,1)} %get-tuple-element.217.left_ref, f32[1,2048]{1,0:T(1,128)} %reshape.220.shift_ref, bf16[256,2048]{1,0:T(8,128)(2,1)} %bitcast.73.refs_0_, bf16[256,2048]{1,0:T(8,128)(2,1)} %copy-done.52, ...), custom_call_target="tpu_custom_call" | custom-call | flops 4294967296 | bytes 8388608 | tf_op jit(solution)/shard_map/rows_product/pallas_call | solution.py:449
  464.2 14.8 %attend_backward.1 = (bf16[512,2048]{1,0:T(8,128)(2,1)}, f32[2048,256]{1,0:T(8,128)}) custom-call(s32[3,4]{1,0:T(4,128)} %pad_add_fusion.info_ref, bf16[512,2048]{1,0:T(8,128)(2,1)} %rows_product.2.q_ref, bf16[512,2048]{1,0:T(8,128)(2,1)} %rows_product.3.grad_ref, bf16[512,2048]{1,0:T(8,128)(2,1)} %get-tuple-element.127.left_ref.o_ref, ...), custom_call_target="tpu_custom_call" | custom-call | tf_op jit(solution)/shard_map/attend_backward/pallas_call | solution.py:246
  481.8 17.0 %all-to-all-start.4 = ((bf16[4,512,256]{2,1,0:T(8,128)(2,1)}), bf16[4,512,256]{2,1,0:T(8,128)(2,1)S(1)}, u32[]{:S(2)}, u32[]{:S(2)}) async-start(bf16[4,512,256]{2,1,0:T(8,128)(2,1)} %bitcast.31), calls=%async_computation.4 | async-start | bytes 2097152 | tf_op jit(solution)/shard_map/all_to_all | solution.py:283
  503.8 26.1 %grads_product.3 = (bf16[1024,2048]{1,0:T(8,128)(2,1)}, f32[1,1024]{1,0:T(1,128)}) custom-call(bf16[512,1024]{1,0:T(8,128)(2,1)} %get-tuple-element.189.refs_0_, bf16[512,1024]{1,0:T(8,128)(2,1)} %get-tuple-element.191.refs_1_, bf16[512,1024]{1,0:T(8,128)(2,1)} %get-tuple-element.193.refs_2_, bf16[512,1024]{1,0:T(8,128)(2,1)} %get-tuple-element.195.refs_3_, ...), custom_call_target="tpu_custom_call" | custom-call | flops 17179869184 | bytes 29360128 | tf_op jit(solution)/shard_map/grads_product/pallas_call | solution.py:491
  534.3 7.0 convolution_convert_fusion
  552.9 6.4 convolution_convert_fusion.1
  566.2 18.9 %collective-permute-done.43 = bf16[256,2304]{1,0:T(8,128)(2,1)S(1)} collective-permute-done((bf16[256,2304]{1,0:T(8,128)(2,1)S(1)}, bf16[256,2304]{1,0:T(8,128)(2,1)S(1)}, u32[]{:S(2)}, u32[]{:S(2)}) %collective-permute-start.43) | collective-permute-done | bytes 1179680 | tf_op jit(solution)/shard_map/ppermute | solution.py:326
  596.2 11.4 %cols_product.3 = f32[512,2048]{1,0:T(8,128)} custom-call(s32[8]{0:T(128)} %stack.52.owner_ref, bf16[512,2048]{1,0:T(8,128)(2,1)} %get-tuple-element.211.left_ref, bf16[256,2048]{1,0:T(8,128)(2,1)} %bitcast.70.refs_0_, bf16[256,2048]{1,0:T(8,128)(2,1)} %copy-done.46, bf16[256,2048]{1,0:T(8,128)(2,1)} %collective-permute-done.2.refs_2_, ...), custom_call_target="tpu_custom_call" | custom-call | flops 4294967296 | bytes 8388608 | tf_op jit(solution)/shard_map/cols_product/pallas_call | solution.py:525
  612.9 5.9 fusion.13
  618.9 16.4 %collective-permute-done.45 = bf16[256,2304]{1,0:T(8,128)(2,1)S(1)} collective-permute-done((bf16[256,2304]{1,0:T(8,128)(2,1)S(1)}, bf16[256,2304]{1,0:T(8,128)(2,1)S(1)}, u32[]{:S(2)}, u32[]{:S(2)}) %collective-permute-start.45) | collective-permute-done | bytes 1179680 | tf_op jit(solution)/shard_map/ppermute | solution.py:326
  681.6 11.6 %collective-permute-done.50 = bf16[1,256,768]{2,1,0:T(8,128)(2,1)} collective-permute-done((bf16[1,256,768]{2,1,0:T(8,128)(2,1)}, bf16[1,256,768]{2,1,0:T(8,128)(2,1)}, u32[]{:S(2)}, u32[]{:S(2)}) %collective-permute-start.50) | collective-permute-done | bytes 393248 | tf_op jit(solution)/shard_map/ppermute | solution.py:294
  708.0 5.7 collective-permute-done.48
  713.7 6.3 add_convert_fusion
  (351 shorter events, 241.4 us)
Async XLA Ops:
  7.2 51.8 %all-gather.6.cloned.1.call-start = ((), (), s32[]{:S(2)}) async-start(), calls=%async_computation.16 | async-start | bytes 2621440 | tf_op jit(solution)/shard_map/all_gather | solution.py:578
  82.0 176.5 %all-gather.4.cloned.1.call-start = ((), (), s32[]{:S(2)}) async-start(), calls=%async_computation.12 | async-start | bytes 10485760 | tf_op jit(solution)/shard_map/all_gather | solution.py:599
  108.6 540.5 %reduce-scatter.6.cloned.1.call-start = ((), (), s32[]{:S(2)}) async-start(), calls=%async_computation.14 | async-start | bytes 5242880 | tf_op jit(solution)/shard_map/reduce_scatter | solution.py:666
  108.7 35.0 %collective-permute-start = (bf16[512,2048]{1,0:T(8,128)(2,1)}, bf16[512,2048]{1,0:T(8,128)(2,1)}, u32[]{:S(2)}, u32[]{:S(2)}) collective-permute-start(bf16[512,2048]{1,0:T(8,128)(2,1)} %refs_8_.1), channel_id=1, source_target_pairs={{0,8},{12,4},{8,24},{28,12},{24,16},{20,28},{16,0},{4,20},{1,9},{1... | collective-permute-start | bytes 6291464 | tf_op jit(solution)/shard_map/ppermute | solution.py:326
  158.8 44.9 %collective-permute-start.8 = (bf16[512,2048]{1,0:T(8,128)(2,1)}, bf16[512,2048]{1,0:T(8,128)(2,1)}, u32[]{:S(2)}, u32[]{:S(2)}) collective-permute-start(bf16[512,2048]{1,0:T(8,128)(2,1)} %collective-permute-done.refs_2_.refs_10_), channel_id=1, source_target_pairs={{0,8},{12,4},{8,24},{28,12},{24,16},{20,28},{16,0},{4,20},{1,9},{1... | collective-permute-start | bytes 6291464 | tf_op jit(solution)/shard_map/ppermute | solution.py:326
  170.2 33.5 %collective-permute-start.14 = (bf16[256,2048]{1,0:T(8,128)(2,1)S(1)}, bf16[256,2048]{1,0:T(8,128)(2,1)S(1)}, u32[]{:S(2)}, u32[]{:S(2)}) collective-permute-start(bf16[256,2048]{1,0:T(8,128)(2,1)S(1)} %collective-permute-done.12.refs_4_), channel_id=1, source_target_pairs={{0,8},{12,4},{8,24},{28,12},{24,16},{20,28},{16,0},{4,20},{1,9},{1... | collective-permute-start | bytes 3145736 | tf_op jit(solution)/shard_map/ppermute | solution.py:326
  172.5 31.2 %collective-permute-start.9 = (bf16[256,2048]{1,0:T(8,128)(2,1)}, bf16[256,2048]{1,0:T(8,128)(2,1)S(1)}, u32[]{:S(2)}, u32[]{:S(2)}) collective-permute-start(bf16[256,2048]{1,0:T(8,128)(2,1)} %bitcast.73.refs_0_), channel_id=1, source_target_pairs={{0,4},{4,0},{8,12},{12,8},{16,20},{20,16},{24,28},{28,24},{1,5},{5... | collective-permute-start | bytes 3145736 | tf_op jit(solution)/shard_map/ppermute | solution.py:329
  172.5 31.3 %collective-permute-start.11 = (bf16[256,2048]{1,0:T(8,128)(2,1)}, bf16[256,2048]{1,0:T(8,128)(2,1)S(1)}, u32[]{:S(2)}, u32[]{:S(2)}) collective-permute-start(bf16[256,2048]{1,0:T(8,128)(2,1)} %collective-permute-done.10.refs_2_), channel_id=1, source_target_pairs={{0,4},{4,0},{8,12},{12,8},{16,20},{20,16},{24,28},{28,24},{1,5},{5... | collective-permute-start | bytes 3145736 | tf_op jit(solution)/shard_map/ppermute | solution.py:329
  251.6 36.2 %collective-permute-start.17 = (bf16[512,2048]{1,0:T(8,128)(2,1)}, bf16[512,2048]{1,0:T(8,128)(2,1)}, u32[]{:S(2)}, u32[]{:S(2)}) collective-permute-start(bf16[512,2048]{1,0:T(8,128)(2,1)} %collective-permute-done.16.refs_0_.refs_10_), channel_id=1, source_target_pairs={{0,8},{12,4},{8,24},{28,12},{24,16},{20,28},{16,0},{4,20},{1,9},{1... | collective-permute-start | bytes 6291464 | tf_op jit(solution)/shard_map/ppermute | solution.py:326
  254.7 46.9 %collective-permute-start.24 = (bf16[512,2048]{1,0:T(8,128)(2,1)}, bf16[512,2048]{1,0:T(8,128)(2,1)}, u32[]{:S(2)}, u32[]{:S(2)}) collective-permute-start(bf16[512,2048]{1,0:T(8,128)(2,1)} %collective-permute-done.8.refs_2_.refs_12_), channel_id=1, source_target_pairs={{0,8},{12,4},{8,24},{28,12},{24,16},{20,28},{16,0},{4,20},{1,9},{1... | collective-permute-start | bytes 6291464 | tf_op jit(solution)/shard_map/ppermute | solution.py:326
  288.4 41.0 %collective-permute-start.20 = (bf16[512,2048]{1,0:T(8,128)(2,1)}, bf16[512,2048]{1,0:T(8,128)(2,1)}, u32[]{:S(2)}, u32[]{:S(2)}) collective-permute-start(bf16[512,2048]{1,0:T(8,128)(2,1)} %collective-permute-done.17.refs_0_.refs_12_), channel_id=1, source_target_pairs={{0,8},{12,4},{8,24},{28,12},{24,16},{20,28},{16,0},{4,20},{1,9},{1... | collective-permute-start | bytes 6291464 | tf_op jit(solution)/shard_map/ppermute | solution.py:326
  330.0 36.0 %collective-permute-start.31 = (bf16[512,2048]{1,0:T(8,128)(2,1)}, bf16[512,2048]{1,0:T(8,128)(2,1)}, u32[]{:S(2)}, u32[]{:S(2)}) collective-permute-start(bf16[512,2048]{1,0:T(8,128)(2,1)} %get-tuple-element.139), channel_id=1, source_target_pairs={{0,4},{4,0},{8,12},{12,8},{16,20},{20,16},{24,28},{28,24},{1,5},{5... | collective-permute-start | bytes 6291464 | tf_op jit(solution)/shard_map/ppermute | solution.py:329
  334.2 31.8 %collective-permute-start.33 = (bf16[512,2048]{1,0:T(8,128)(2,1)}, bf16[512,2048]{1,0:T(8,128)(2,1)}, u32[]{:S(2)}, u32[]{:S(2)}) collective-permute-start(bf16[512,2048]{1,0:T(8,128)(2,1)} %add_convert_fusion.6), channel_id=1, source_target_pairs={{0,8},{12,4},{8,24},{28,12},{24,16},{20,28},{16,0},{4,20},{1,9},{1... | collective-permute-start | bytes 6291464 | tf_op jit(solution)/shard_map/ppermute | solution.py:326
  365.6 37.8 %collective-permute-start.30 = (bf16[512,2048]{1,0:T(8,128)(2,1)}, bf16[512,2048]{1,0:T(8,128)(2,1)}, u32[]{:S(2)}, u32[]{:S(2)}) collective-permute-start(bf16[512,2048]{1,0:T(8,128)(2,1)} %get-tuple-element.145), channel_id=1, source_target_pairs={{0,4},{4,0},{8,12},{12,8},{16,20},{20,16},{24,28},{28,24},{1,5},{5... | collective-permute-start | bytes 6291464 | tf_op jit(solution)/shard_map/ppermute | solution.py:329
  371.6 31.8 %collective-permute-start.34 = (bf16[512,2048]{1,0:T(8,128)(2,1)}, bf16[512,2048]{1,0:T(8,128)(2,1)}, u32[]{:S(2)}, u32[]{:S(2)}) collective-permute-start(bf16[512,2048]{1,0:T(8,128)(2,1)} %add_convert_fusion.5), channel_id=1, source_target_pairs={{0,8},{12,4},{8,24},{28,12},{24,16},{20,28},{16,0},{4,20},{1,9},{1... | collective-permute-start | bytes 6291464 | tf_op jit(solution)/shard_map/ppermute | solution.py:326
  410.9 48.5 %collective-permute-start.36 = (bf16[512,2048]{1,0:T(8,128)(2,1)}, bf16[512,2048]{1,0:T(8,128)(2,1)}, u32[]{:S(2)}, u32[]{:S(2)}) collective-permute-start(bf16[512,2048]{1,0:T(8,128)(2,1)} %get-tuple-element.184), channel_id=1, source_target_pairs={{0,4},{4,0},{8,12},{12,8},{16,20},{20,16},{24,28},{28,24},{1,5},{5... | collective-permute-start | bytes 6291464 | tf_op jit(solution)/shard_map/ppermute | solution.py:329
  437.5 44.3 %collective-permute-start.37 = (bf16[512,2048]{1,0:T(8,128)(2,1)}, bf16[512,2048]{1,0:T(8,128)(2,1)}, u32[]{:S(2)}, u32[]{:S(2)}) collective-permute-start(bf16[512,2048]{1,0:T(8,128)(2,1)} %get-tuple-element.187), channel_id=1, source_target_pairs={{0,4},{4,0},{8,12},{12,8},{16,20},{20,16},{24,28},{28,24},{1,5},{5... | collective-permute-start | bytes 6291464 | tf_op jit(solution)/shard_map/ppermute | solution.py:329
  463.1 35.8 %collective-permute-start.38 = (bf16[512,2048]{1,0:T(8,128)(2,1)}, bf16[512,2048]{1,0:T(8,128)(2,1)}, u32[]{:S(2)}, u32[]{:S(2)}) collective-permute-start(bf16[512,2048]{1,0:T(8,128)(2,1)} %add_convert_fusion.3), channel_id=1, source_target_pairs={{0,8},{12,4},{8,24},{28,12},{24,16},{20,28},{16,0},{4,20},{1,9},{1... | collective-permute-start | bytes 6291464 | tf_op jit(solution)/shard_map/ppermute | solution.py:326
  464.0 83.7 %collective-permute-start.46 = (bf16[512,2048]{1,0:T(8,128)(2,1)}, bf16[512,2048]{1,0:T(8,128)(2,1)}, u32[]{:S(2)}, u32[]{:S(2)}) collective-permute-start(bf16[512,2048]{1,0:T(8,128)(2,1)} %get-tuple-element.208), channel_id=1, source_target_pairs={{0,4},{4,0},{8,12},{12,8},{16,20},{20,16},{24,28},{28,24},{1,5},{5... | collective-permute-start | bytes 6291464 | tf_op jit(solution)/shard_map/ppermute | solution.py:329
  481.8 52.3 %all-to-all-start.4 = ((bf16[4,512,256]{2,1,0:T(8,128)(2,1)}), bf16[4,512,256]{2,1,0:T(8,128)(2,1)S(1)}, u32[]{:S(2)}, u32[]{:S(2)}) async-start(bf16[4,512,256]{2,1,0:T(8,128)(2,1)} %bitcast.31), calls=%async_computation.4 | async-start | bytes 2097152 | tf_op jit(solution)/shard_map/all_to_all | solution.py:283
  498.8 202.7 %reduce-scatter.4.cloned.1.call-start = ((), (), s32[]{:S(2)}) async-start(), calls=%async_computation.13 | async-start | bytes 5242880 | tf_op jit(solution)/shard_map/reduce_scatter | solution.py:700
  546.1 44.6 %collective-permute-start.47 = (bf16[512,2048]{1,0:T(8,128)(2,1)}, bf16[512,2048]{1,0:T(8,128)(2,1)}, u32[]{:S(2)}, u32[]{:S(2)}) collective-permute-start(bf16[512,2048]{1,0:T(8,128)(2,1)} %add_convert_fusion.2), channel_id=1, source_target_pairs={{0,8},{12,4},{8,24},{28,12},{24,16},{20,28},{16,0},{4,20},{1,9},{1... | collective-permute-start | bytes 6291464 | tf_op jit(solution)/shard_map/ppermute | solution.py:326
  551.0 34.1 %collective-permute-start.43 = (bf16[256,2304]{1,0:T(8,128)(2,1)S(1)}, bf16[256,2304]{1,0:T(8,128)(2,1)S(1)}, u32[]{:S(2)}, u32[]{:S(2)}) collective-permute-start(bf16[256,2304]{1,0:T(8,128)(2,1)S(1)} %add_convert_fusion.10), channel_id=1, source_target_pairs={{0,8},{12,4},{8,24},{28,12},{24,16},{20,28},{16,0},{4,20},{1,9},{1... | collective-permute-start | bytes 3538952 | tf_op jit(solution)/shard_map/ppermute | solution.py:326
  561.0 115.5 %collective-permute-start.52 = (bf16[256,2048]{1,0:T(8,128)(2,1)}, bf16[256,2048]{1,0:T(8,128)(2,1)}, u32[]{:S(2)}, u32[]{:S(2)}) collective-permute-start(bf16[256,2048]{1,0:T(8,128)(2,1)} %get-tuple-element.233), channel_id=1, source_target_pairs={{0,4},{4,0},{8,12},{12,8},{16,20},{20,16},{24,28},{28,24},{1,5},{5... | collective-permute-start | bytes 3145736 | tf_op jit(solution)/shard_map/ppermute | solution.py:329
  566.2 71.3 %collective-permute-start.54 = (bf16[256,2048]{1,0:T(8,128)(2,1)}, bf16[256,2048]{1,0:T(8,128)(2,1)}, u32[]{:S(2)}, u32[]{:S(2)}) collective-permute-start(bf16[256,2048]{1,0:T(8,128)(2,1)} %get-tuple-element.235), channel_id=1, source_target_pairs={{0,4},{4,0},{8,12},{12,8},{16,20},{20,16},{24,28},{28,24},{1,5},{5... | collective-permute-start | bytes 3145736 | tf_op jit(solution)/shard_map/ppermute | solution.py:329
  618.9 32.7 %collective-permute-start.53 = (bf16[256,2048]{1,0:T(8,128)(2,1)}, bf16[256,2048]{1,0:T(8,128)(2,1)}, u32[]{:S(2)}, u32[]{:S(2)}) collective-permute-start(bf16[256,2048]{1,0:T(8,128)(2,1)} %get-tuple-element.236), channel_id=1, source_target_pairs={{0,4},{4,0},{8,12},{12,8},{16,20},{20,16},{24,28},{28,24},{1,5},{5... | collective-permute-start | bytes 3145736 | tf_op jit(solution)/shard_map/ppermute | solution.py:329
  655.0 40.0 %collective-permute-start.51 = (bf16[1,256,768]{2,1,0:T(8,128)(2,1)}, bf16[1,256,768]{2,1,0:T(8,128)(2,1)S(1)}, u32[]{:S(2)}, u32[]{:S(2)}) collective-permute-start(bf16[1,256,768]{2,1,0:T(8,128)(2,1)} %get-tuple-element.239), channel_id=1, source_target_pairs={{0,3},{1,0},{2,1},{3,2},{4,7},{5,4},{6,5},{7,6},{8,11},{9,8},{10,9... | collective-permute-start | bytes 1179656 | tf_op jit(solution)/shard_map/ppermute | solution.py:294
  658.5 34.7 %collective-permute-start.50 = (bf16[1,256,768]{2,1,0:T(8,128)(2,1)}, bf16[1,256,768]{2,1,0:T(8,128)(2,1)}, u32[]{:S(2)}, u32[]{:S(2)}) collective-permute-start(bf16[1,256,768]{2,1,0:T(8,128)(2,1)} %get-tuple-element.242), channel_id=1, source_target_pairs={{0,2},{1,3},{2,0},{3,1},{4,6},{5,7},{6,4},{7,5},{8,10},{9,11},{10,... | collective-permute-start | bytes 1179656 | tf_op jit(solution)/shard_map/ppermute | solution.py:294
  663.1 34.7 %collective-permute-start.58 = (bf16[256,2048]{1,0:T(8,128)(2,1)}, bf16[256,2048]{1,0:T(8,128)(2,1)}, u32[]{:S(2)}, u32[]{:S(2)}) collective-permute-start(bf16[256,2048]{1,0:T(8,128)(2,1)} %add_convert_fusion.11), channel_id=1, source_target_pairs={{0,8},{12,4},{8,24},{28,12},{24,16},{20,28},{16,0},{4,20},{1,9},{1... | collective-permute-start | bytes 3145736 | tf_op jit(solution)/shard_map/ppermute | solution.py:326
  668.5 66.1 %reduce-scatter.8.cloned.1.call-start = ((), (), s32[]{:S(2)}) async-start(), calls=%async_computation.15 | async-start | bytes 1310720 | tf_op jit(solution)/shard_map/reduce_scatter | solution.py:690
  676.5 31.5 %collective-permute-start.28 = (bf16[512,2048]{1,0:T(8,128)(2,1)}, bf16[512,2048]{1,0:T(8,128)(2,1)}, u32[]{:S(2)}, u32[]{:S(2)}) collective-permute-start(bf16[512,2048]{1,0:T(8,128)(2,1)} %get-tuple-element.151), channel_id=1, source_target_pairs={{0,4},{4,0},{8,12},{12,8},{16,20},{20,16},{24,28},{28,24},{1,5},{5... | collective-permute-start | bytes 6291464 | tf_op jit(solution)/shard_map/ppermute | solution.py:329
  677.9 35.8 %collective-permute-start.48 = (bf16[512,2048]{1,0:T(8,128)(2,1)}, bf16[512,2048]{1,0:T(8,128)(2,1)}, u32[]{:S(2)}, u32[]{:S(2)}) collective-permute-start(bf16[512,2048]{1,0:T(8,128)(2,1)} %add_convert_fusion.1), channel_id=1, source_target_pairs={{0,8},{12,4},{8,24},{28,12},{24,16},{20,28},{16,0},{4,20},{1,9},{1... | collective-permute-start | bytes 6291464 | tf_op jit(solution)/shard_map/ppermute | solution.py:326
  (96 other events, 1274.1 us)
Sparse Core Ops, SparseCore 0:
  10.3 48.6 all-gather.5
  108.8 146.8 all-gather.3
  437.6 84.9 reduce-scatter.5
  547.8 77.9 reduce-scatter.3
  701.6 27.5 reduce-scatter.7
